TPU v7x, 32 devices: a whole 2x2x4 slice. The times are simulated.
32 devices in a mesh: seq: 8 (over z, y), head: 4 (over x, core).
Axes of the slice: x: 2, y: 2, z: 4, core: 2. Of those that a mesh axis runs over, the one named last changes fastest.
Arguments:
- block_input: bfloat16 [8192, 1024], P(('seq', 'head')), may hold values from -6 to 6
- out_grad: bfloat16 [8192, 1024], P(('seq', 'head')), may hold values from -6 to 6
- lengths: int32 [16], replicated, may hold values from 1 to 4096, 8192 in all
- doc_sets: int32 [16], replicated, may hold values from 0 to 7
- norm1_gain: float32 [1024], replicated, may hold values from 0.5 to 1.5
- w_query: bfloat16 [1024, 1024], P(None, 'head'), may hold values from -0.1875 to 0.1875
- w_key: bfloat16 [1024, 1024], P(None, 'head'), may hold values from -0.1875 to 0.1875
- w_value: bfloat16 [1024, 2048], P(None, 'head'), may hold values from -0.1875 to 0.1875
- conv_query: bfloat16 [4, 1024], P(None, 'head'), may hold values from -0.59765625 to 0.59765625
- conv_key: bfloat16 [4, 1024], P(None, 'head'), may hold values from -0.59765625 to 0.59765625
- conv_value: bfloat16 [4, 2048], P(None, 'head'), may hold values from -0.59765625 to 0.59765625
- w_decay_beta: bfloat16 [1024, 2, 8], P(None, None, 'head'), may hold values from -0.1875 to 0.1875
- decay_rate: float32 [8], P('head'), may hold values from 0.0003 to 0.1
- decay_bias: float32 [8], P('head'), may hold values from -1 to 1
- w_gate_out: bfloat16 [1024, 2048], P(None, 'head'), may hold values from -0.1875 to 0.1875
- out_gain: float32 [256], replicated, may hold values from 0.5 to 1.5
- w_out: bfloat16 [2048, 1024], P('head'), may hold values from -0.1875 to 0.1875
- norm2_gain: float32 [1024], replicated, may hold values from 0.5 to 1.5
- w_gate: bfloat16 [1024, 2816], P(None, 'head'), may hold values from -0.1875 to 0.1875
- w_up: bfloat16 [1024, 2816], P(None, 'head'), may hold values from -0.1875 to 0.1875
- w_down: bfloat16 [2816, 1024], P('head'), may hold values from -0.15625 to 0.15625
- adapt_down: bfloat16 [6, 8, 1024, 16], replicated, may hold values from -0.1875 to 0.1875
- adapt_up_qk: bfloat16 [2, 8, 16, 1024], P(None, None, None, 'head'), may hold values from -0.75 to 0.75
- adapt_up_vg: bfloat16 [2, 8, 16, 2048], P(None, None, None, 'head'), may hold values from -0.75 to 0.75
- adapt_up_ff: bfloat16 [2, 8, 16, 2816], P(None, None, None, 'head'), may hold values from -0.75 to 0.75
- adapt_down_out: bfloat16 [8, 2048, 16], P(None, 'head'), may hold values from -0.125 to 0.125
- adapt_down_ffd: bfloat16 [8, 2816, 16], P(None, 'head'), may hold values from -0.109375 to 0.109375
- adapt_up_res: bfloat16 [2, 8, 16, 1024], replicated, may hold values from -0.75 to 0.75
Outputs:
- block_output: bfloat16 [8192, 1024], P(('seq', 'head'))
- input_grad: float32 [8192, 1024], P(('seq', 'head'))
- adapt_down_grad: float32 [6, 8, 1024, 16], replicated
- adapt_up_qk_grad: float32 [2, 8, 16, 1024], P(None, None, None, 'head')
- adapt_up_vg_grad: float32 [2, 8, 16, 2048], P(None, None, None, 'head')
- adapt_up_ff_grad: float32 [2, 8, 16, 2816], P(None, None, None, 'head')
- adapt_down_out_grad: float32 [8, 2048, 16], P(None, 'head')
- adapt_down_ffd_grad: float32 [8, 2816, 16], P(None, 'head')
- adapt_up_res_grad: float32 [2, 8, 16, 1024], replicated
Inputs may be any that keep to these rules, and one draw needn't show every extreme that they name: Documents in stream order; the lengths sum to 8192 and one document has exactly 4096 tokens.
All inputs are finite; a program needn't handle non-finite values.
Results may differ from a plain program's by a relative error of at most 0.014.
Values may be sent and summed in bfloat16 or wider, within the bound.
No kernel may reach another device: no remote copies, remote signals or barrier semaphores. Data moves between devices by JAX's collectives and lax.ppermute only.
A program may use at most 256 MiB of HBM per device.

v0:
```python
import functools

import jax
import jax.numpy as jnp
from jax import lax
from jax.experimental import pallas as pl
from jax.experimental.pallas import tpu as pltpu
from jax.sharding import PartitionSpec as P

CHUNK = 128
STEP = 256
HALO = 16
DOC_MAX = 4096
EPS = 1e-06
VMEM_LIMIT = 56 * 1024 * 1024
bfloat = jnp.bfloat16
single = jnp.float32


def contract(left, right, left_dim, right_dim):
    return lax.dot_general(
        left,
        right,
        (((left_dim,), (right_dim,)), ((), ())),
        preferred_element_type=single,
    )


def nn(left, right):
    return contract(left, right, 1, 0)


def nt(left, right):
    return contract(left, right, 1, 1)


def tn(left, right):
    return contract(left, right, 0, 0)


def low(array):
    return array.astype(bfloat)


def iotas():
    rows = lax.broadcasted_iota(jnp.int32, (CHUNK, CHUNK), 0)
    columns = lax.broadcasted_iota(jnp.int32, (CHUNK, CHUNK), 1)
    return rows, columns


def split_two(array):
    high = low(array)
    return high, low(array - high.astype(single))


def near_exact(left, right):
    left_high, left_low = split_two(left)
    right_high, right_low = split_two(right)
    return nn(
        jnp.concatenate([left_high, left_high, left_low], axis=1),
        jnp.concatenate([right_high, right_low, right_high], axis=0),
    )


def ones_product(ones, array):
    high = low(array)
    rest = array - high.astype(single)
    middle = low(rest)
    lowest = low(rest - middle.astype(single))
    return nn(
        jnp.concatenate([ones, ones, ones], axis=1),
        jnp.concatenate([high, middle, lowest], axis=0),
    )


def unit_lower_inverses(stricts, rows, columns):
    eye = (rows == columns).astype(single)
    differ = rows ^ columns
    block = 8
    inner = [jnp.where(differ < block, strict, 0.0) for strict in stricts]
    second = [near_exact(a, a) for a in inner]
    inverse = [near_exact(eye - a, eye + b) for a, b in zip(inner, second)]
    fourth = [near_exact(b, b) for b in second]
    inverse = [near_exact(a, eye + b) for a, b in zip(inverse, fourth)]
    while block < CHUNK:
        between = (differ >= block) & (differ < 2 * block)
        off = [jnp.where(between, strict, 0.0) for strict in stricts]
        part = [near_exact(a, b) for a, b in zip(off, inverse)]
        inverse = [a - near_exact(a, b) for a, b in zip(inverse, part)]
        block = 2 * block
    return inverse


def softplus(value):
    return jnp.maximum(value, 0.0) + jnp.log(1.0 + jnp.exp(-jnp.abs(value)))


def sigmoid(value):
    return 1.0 / (1.0 + jnp.exp(-value))


def gates(decay, start, rows, columns):
    lower_ones = low((rows >= columns).astype(single))
    total = ones_product(lower_ones, jnp.broadcast_to(decay, (CHUNK, CHUNK)))
    linked = (rows >= columns) & (columns >= start)
    within = jnp.where(linked, jnp.exp(jnp.where(linked, total - total.T, 0.0)), 0.0)
    running = total[:, :1]
    carried = jnp.where(start < 0, jnp.exp(running), 0.0)
    last = running[CHUNK - 1 : CHUNK]
    ending = jnp.where(
        rows[:, :1] >= start[CHUNK - 1 : CHUNK], jnp.exp(jnp.minimum(last - running, 0.0)), 0.0
    )
    return within, carried, ending


def convolved(window, starts, weights, base):
    positions = base + lax.broadcasted_iota(jnp.int32, (STEP, 1), 0)
    taps = weights.shape[0]
    total = None
    for tap in range(taps):
        back = taps - 1 - tap
        term = window[HALO - back : HALO - back + STEP, :] * weights[tap : tap + 1, :]
        if back:
            term = jnp.where(positions - back >= starts, term, 0.0)
        total = term if total is None else total + term
    return total


def head_scales(rows, width):
    return lax.rsqrt(jnp.sum(rows * rows, axis=-1, keepdims=True) + EPS)


def forward_kernel(
    place,
    rows_ref,
    halo_ref,
    column_ref,
    weight_ref,
    scalar_ref,
    out_ref,
    map_ref,
    written_ref,
    state_ref,
    inverse_ref,
    end_ref,
    window,
    state,
    *,
    heads,
    key_width,
    value_width,
):
    step = pl.program_id(0)
    wide = value_width + key_width
    base = step * STEP
    rows, columns = iotas()

    @pl.when(step == 0)
    def _():
        window[0:HALO, :] = halo_ref[...].astype(single)
        for h in range(heads):
            state[h, :, :value_width] = jnp.zeros((key_width, value_width), single)
            state[h, :, value_width:] = (rows == columns).astype(single)

    @pl.when(step > 0)
    def _():
        window[0:HALO, :] = window[STEP : STEP + HALO, :]

    window[HALO:, :] = rows_ref[...].astype(single)
    info = column_ref[...]
    starts = info[:, 2 * heads : 2 * heads + 1].astype(jnp.int32)
    before = convolved(window, starts, weight_ref[...], base)
    active = before * sigmoid(before)
    qk_lanes = heads * key_width
    chunks = STEP // CHUNK
    local, stricts = [], []
    for c in range(chunks):
        span = slice(c * CHUNK, (c + 1) * CHUNK)
        for h in range(heads):
            query = active[span, h * key_width : (h + 1) * key_width]
            key = active[span, qk_lanes + h * key_width : qk_lanes + (h + 1) * key_width]
            value = active[
                span, 2 * qk_lanes + h * value_width : 2 * qk_lanes + (h + 1) * value_width
            ]
            query = query * (head_scales(query, key_width) * key_width ** (-0.5))
            key = key * head_scales(key, key_width)
            beta = sigmoid(info[span, h : h + 1])
            decay = -scalar_ref[0, h] * softplus(
                info[span, heads + h : heads + h + 1] + scalar_ref[1, h]
            )
            within, carried, ending = gates(
                decay, starts[span] - (base + c * CHUNK), rows, columns
            )
            query, key = low(query), low(key)
            strict = jnp.where(rows > columns, within * nt(key, key), 0.0) * beta
            mixed = low(within * nt(query, key))
            stricts.append(strict)
            local.append((query, key, value, beta, carried, ending, mixed))
    inverses = [low(a) for a in unit_lower_inverses(stricts, rows, columns)]
    each = range(heads)
    now = [state[h] for h in each]
    for c in range(chunks):
        span = slice(c * CHUNK, (c + 1) * CHUNK)
        here = [local[c * heads + h] for h in each]
        inverse = [inverses[c * heads + h] for h in each]
        now_low = [low(a) for a in now]
        read = [nn(here[h][1], now_low[h]) for h in each]
        asked = [nn(here[h][0], now_low[h]) for h in each]
        target = []
        for h in each:
            query, key, value, beta, carried, ending, mixed = here[h]
            gap = -(carried * beta) * read[h]
            target.append(
                jnp.concatenate(
                    [beta * value + gap[:, :value_width], gap[:, value_width:]], axis=1
                )
            )
        written = [nn(inverse[h], low(target[h])) for h in each]
        added = [tn(here[h][1], low(here[h][5] * written[h])) for h in each]
        inner = [nn(here[h][6], low(written[h])) for h in each]
        for h in each:
            carried = here[h][4]
            inverse_ref[span, h * CHUNK : (h + 1) * CHUNK] = inverse[h]
            state_ref[c, h] = now_low[h]
            written_ref[span, h * wide : (h + 1) * wide] = low(written[h])
            output = carried * asked[h] + inner[h]
            out_ref[span, h * value_width : (h + 1) * value_width] = output[:, :value_width]
            map_ref[span, h * key_width : (h + 1) * key_width] = low(output[:, value_width:])
        now = [here[h][4][CHUNK - 1 : CHUNK] * now[h] + added[h] for h in each]
    for h in each:
        state[h] = now[h]

    @pl.when(step == pl.num_programs(0) - 1)
    def _():
        end_ref[...] = state[...]


def backward_kernel(
    place,
    rows_ref,
    before_ref,
    halo_ref,
    column_ref,
    weight_ref,
    scalar_ref,
    grad_ref,
    written_ref,
    state_ref,
    inverse_ref,
    end_ref,
    entering_ref,
    later_ref,
    out_ref,
    mix_ref,
    tail_ref,
    edge_ref,
    window,
    shifted,
    shifted_start,
    cotangent,
    ahead,
    *,
    heads,
    key_width,
    value_width,
):
    step = pl.program_id(0)
    steps = pl.num_programs(0)
    wide = value_width + key_width
    base = (steps - 1 - step) * STEP
    rows, columns = iotas()
    qk_lanes = heads * key_width
    lanes = window.shape[1]
    taps = weight_ref.shape[0]

    @pl.when(step == 0)
    def _():
        shifted[STEP : STEP + 8, :] = jnp.zeros((8, lanes), single)
        shifted_start[STEP : STEP + 8, :] = jnp.zeros((8, 1), jnp.int32)
        for h in range(heads):
            cotangent[h] = later_ref[h].astype(single)
            ahead[h] = end_ref[h, :, :value_width] + nn(
                low(end_ref[h, :, value_width:]), low(entering_ref[h])
            )

    @pl.when(step > 0)
    def _():
        shifted[STEP : STEP + 8, :] = shifted[0:8, :]
        shifted_start[STEP : STEP + 8, :] = shifted_start[0:8, :]

    window[0:HALO, :] = jnp.where(
        step == steps - 1, halo_ref[...].astype(single), before_ref[...].astype(single)
    )
    window[HALO:, :] = rows_ref[...].astype(single)
    info = column_ref[...]
    starts = info[:, 2 * heads : 2 * heads + 1].astype(jnp.int32)
    positions = base + lax.broadcasted_iota(jnp.int32, (STEP, 1), 0)
    before = convolved(window, starts, weight_ref[...], base)
    gate = sigmoid(before)
    active = before * gate
    slope = gate * (1.0 + before * (1.0 - gate))
    upper_ones = low((rows <= columns).astype(single))
    last_row = rows[:, :1] == CHUNK - 1
    chunks = STEP // CHUNK
    each = range(heads)
    items = [(c, h) for c in range(chunks) for h in each]
    spans = {item: slice(item[0] * CHUNK, (item[0] + 1) * CHUNK) for item in items}
    entering = [low(entering_ref[h]) for h in each]
    root = key_width ** (-0.5)

    def per(function):
        return {item: function(*item) for item in items}

    def q_lanes(h):
        return slice(h * key_width, (h + 1) * key_width)

    def k_lanes(h):
        return slice(qk_lanes + h * key_width, qk_lanes + (h + 1) * key_width)

    def v_lanes(h):
        return slice(2 * qk_lanes + h * value_width, 2 * qk_lanes + (h + 1) * value_width)

    def kept(c, h, part):
        return written_ref[spans[c, h], h * wide : (h + 1) * wide][:, part]

    values, maps = slice(0, value_width), slice(value_width, wide)
    query_raw = per(lambda c, h: active[spans[c, h], q_lanes(h)])
    key_raw = per(lambda c, h: active[spans[c, h], k_lanes(h)])
    query_scale = per(lambda c, h: head_scales(query_raw[c, h], key_width))
    key_scale = per(lambda c, h: head_scales(key_raw[c, h], key_width))
    query = per(lambda c, h: query_raw[c, h] * (query_scale[c, h] * root))
    key = per(lambda c, h: key_raw[c, h] * key_scale[c, h])
    query_low = per(lambda c, h: low(query[c, h]))
    key_low = per(lambda c, h: low(key[c, h]))
    beta = per(lambda c, h: sigmoid(info[spans[c, h], h : h + 1]))
    raw = per(lambda c, h: info[spans[c, h], heads + h : heads + h + 1] + scalar_ref[1, h])
    gated = per(
        lambda c, h: gates(
            -scalar_ref[0, h] * softplus(raw[c, h]),
            starts[spans[c, h]] - (base + c * CHUNK),
            rows,
            columns,
        )
    )
    within = per(lambda c, h: gated[c, h][0])
    carried = per(lambda c, h: gated[c, h][1])
    ending = per(lambda c, h: gated[c, h][2])
    mixed = per(lambda c, h: low(within[c, h] * nt(query_low[c, h], key_low[c, h])))
    written = per(
        lambda c, h: kept(c, h, values).astype(single) + nn(kept(c, h, maps), entering[h])
    )
    start_state = per(
        lambda c, h: state_ref[c, h][:, values].astype(single)
        + nn(state_ref[c, h][:, maps], entering[h])
    )
    written_low = per(lambda c, h: low(written[c, h]))
    start_low = per(lambda c, h: low(start_state[c, h]))
    grad = per(lambda c, h: grad_ref[spans[c, h], h * value_width : (h + 1) * value_width])
    grad_low = grad
    carried_grad = per(lambda c, h: low(carried[c, h] * grad[c, h].astype(single)))
    from_output = per(lambda c, h: tn(mixed[c, h], grad_low[c, h]))
    state_part = per(lambda c, h: tn(query_low[c, h], carried_grad[c, h]))
    mixed_grad = per(lambda c, h: low(within[c, h] * nt(grad_low[c, h], written_low[c, h])))
    query_grad = per(
        lambda c, h: nt(carried_grad[c, h], start_low[c, h]) + nn(mixed_grad[c, h], key_low[c, h])
    )
    key_write = per(lambda c, h: tn(mixed_grad[c, h], query_low[c, h]))
    later, later_low, solved, value_grad, read_grad = {}, {}, {}, {}, {}
    now = [cotangent[h] for h in each]
    for c in reversed(range(chunks)):
        for h in each:
            later[c, h], later_low[c, h] = now[h], low(now[h])
        from_state = [nn(key_low[c, h], later_low[c, h]) for h in each]
        written_grad = [low(from_output[c, h] + ending[c, h] * from_state[h]) for h in each]
        for h in each:
            inverse = inverse_ref[spans[c, h], h * CHUNK : (h + 1) * CHUNK]
            solved[c, h] = tn(inverse, written_grad[h])
        for h in each:
            value_grad[c, h] = beta[c, h] * solved[c, h]
            read_grad[c, h] = low(-carried[c, h] * value_grad[c, h])
        now = [
            carried[c, h][CHUNK - 1 : CHUNK] * now[h]
            + state_part[c, h]
            + tn(key_low[c, h], read_grad[c, h])
            for h in each
        ]
    following = {
        (c, h): start_state[c + 1, h] if c + 1 < chunks else ahead[h] for c, h in items
    }
    at_end = per(lambda c, h: jnp.sum(later[c, h] * following[c, h], keepdims=True))
    for h in each:
        cotangent[h] = now[h]
        ahead[h] = start_state[0, h]
    strict_grad = per(
        lambda c, h: low(
            jnp.where(
                rows > columns, -within[c, h] * nt(low(value_grad[c, h]), written_low[c, h]), 0.0
            )
        )
    )
    key_read = per(
        lambda c, h: nt(read_grad[c, h], start_low[c, h]) + nn(strict_grad[c, h], key_low[c, h])
    )
    key_write = per(
        lambda c, h: key_write[c, h]
        + tn(strict_grad[c, h], key_low[c, h])
        + nt(low(ending[c, h] * written[c, h]), later_low[c, h])
    )
    query_dot = per(
        lambda c, h: jnp.sum(query[c, h] * query_grad[c, h], axis=-1, keepdims=True)
    )
    running_grad = per(
        lambda c, h: query_dot[c, h]
        + jnp.sum(key[c, h] * (key_read[c, h] - key_write[c, h]), axis=-1, keepdims=True)
        + jnp.where(last_row, at_end[c, h], 0.0)
    )
    decay_sum = per(
        lambda c, h: ones_product(
            upper_ones, jnp.broadcast_to(running_grad[c, h], (CHUNK, CHUNK))
        )[:, :1]
    )
    decay_grad = per(
        lambda c, h: jnp.where(
            positions[spans[c, h]] == starts[spans[c, h]],
            0.0,
            -scalar_ref[0, h] * sigmoid(raw[c, h]) * decay_sum[c, h],
        )
    )
    beta_grad = per(
        lambda c, h: jnp.sum(solved[c, h] * written[c, h], axis=-1, keepdims=True)
        * sigmoid(-info[spans[c, h], h : h + 1])
    )
    for c, h in items:
        span = spans[c, h]
        key_grad = key_read[c, h] + key_write[c, h]
        key_dot = jnp.sum(key[c, h] * key_grad, axis=-1, keepdims=True)
        query_active = (query_scale[c, h] * root) * query_grad[c, h] - query_raw[c, h] * (
            query_scale[c, h] * query_scale[c, h] * query_dot[c, h]
        )
        key_active = key_scale[c, h] * (key_grad - key[c, h] * key_dot)
        shifted[span, q_lanes(h)] = query_active * slope[span, q_lanes(h)]
        shifted[span, k_lanes(h)] = key_active * slope[span, k_lanes(h)]
        shifted[span, v_lanes(h)] = value_grad[c, h] * slope[span, v_lanes(h)]
    for c in range(chunks):
        mix_ref[c * CHUNK : (c + 1) * CHUNK, :] = jnp.concatenate(
            [beta_grad[c, h] for h in each]
            + [decay_grad[c, h] for h in each]
            + [jnp.zeros((CHUNK, mix_ref.shape[1] - 2 * heads), single)],
            axis=1,
        )
    shifted_start[0:STEP, :] = starts
    total = None
    for tap in range(taps):
        back = taps - 1 - tap
        term = shifted[back : back + STEP, :] * weight_ref[tap : tap + 1, :]
        if back:
            term = jnp.where(positions >= shifted_start[back : back + STEP, :], term, 0.0)
        total = term if total is None else total + term
    out_ref[...] = low(total)

    @pl.when(step == 0)
    def _():
        tail_ref[...] = total[STEP - HALO :, :]

    @pl.when(step == steps - 1)
    def _():
        window[0:8, :] = jnp.zeros((8, lanes), single)
        window[8:16, :] = shifted[0:8, :]
        early = lax.broadcasted_iota(jnp.int32, (8, 1), 0) - 8
        collected = jnp.zeros((8, lanes), single)
        for tap in range(taps - 1):
            back = taps - 1 - tap
            reader = early + back
            reader_start = jnp.zeros((8, 1), jnp.int32)
            for t in range(back):
                reader_start = jnp.where(reader == t, shifted_start[t : t + 1, :], reader_start)
            term = window[back : back + 8, :] * weight_ref[tap : tap + 1, :]
            collected = collected + jnp.where(
                (reader >= 0) & (early >= reader_start), term, 0.0
            )
        edge_ref[0:8, :] = jnp.zeros((8, lanes), single)
        edge_ref[8:16, :] = collected


def block_place(step, place, per_quarter):
    return ((step // per_quarter) ^ place[0]) * per_quarter + step % per_quarter


def run_forward(place, rows, halo, columns, weights, scalars, heads, key_width, value_width, quarter):
    count, lanes = columns.shape[0], rows.shape[1]
    steps, per_quarter = count // STEP, quarter // STEP
    wide = value_width + key_width
    chunks = STEP // CHUNK
    at = lambda i, place: (block_place(i, place, per_quarter), 0)
    fixed = lambda i, place: (0, 0)
    body = functools.partial(
        forward_kernel, heads=heads, key_width=key_width, value_width=value_width
    )
    shapes = (
        jax.ShapeDtypeStruct((count, heads * value_width), single),
        jax.ShapeDtypeStruct((count, heads * key_width), bfloat),
        jax.ShapeDtypeStruct((count, heads * wide), bfloat),
        jax.ShapeDtypeStruct((count // CHUNK, heads, key_width, wide), bfloat),
        jax.ShapeDtypeStruct((count, heads * CHUNK), bfloat),
        jax.ShapeDtypeStruct((heads, key_width, wide), single),
    )
    return pl.pallas_call(
        body,
        out_shape=shapes,
        grid_spec=pltpu.PrefetchScalarGridSpec(
            num_scalar_prefetch=1,
            grid=(steps,),
            in_specs=[
                pl.BlockSpec((STEP, lanes), at),
                pl.BlockSpec((HALO, lanes), lambda i, place: (0, 0)),
                pl.BlockSpec((STEP, columns.shape[1]), at),
                pl.BlockSpec(weights.shape, fixed),
                pl.BlockSpec(memory_space=pltpu.SMEM),
            ],
            out_specs=[
                pl.BlockSpec((STEP, heads * value_width), at),
                pl.BlockSpec((STEP, heads * key_width), at),
                pl.BlockSpec((STEP, heads * wide), at),
                pl.BlockSpec((chunks, heads, key_width, wide), lambda i, place: (i, 0, 0, 0)),
                pl.BlockSpec((STEP, heads * CHUNK), at),
                pl.BlockSpec((heads, key_width, wide), lambda i, place: (0, 0, 0)),
            ],
            scratch_shapes=[
                pltpu.VMEM((STEP + HALO, lanes), single),
                pltpu.VMEM((heads, key_width, wide), single),
            ],
        ),
        compiler_params=pltpu.CompilerParams(
            dimension_semantics=("arbitrary",), vmem_limit_bytes=VMEM_LIMIT
        ),
        cost_estimate=pl.CostEstimate(
            flops=count * 2_000_000, bytes_accessed=count * 10_000, transcendentals=count * 2000
        ),
        name="delta_forward",
    )(place, rows, halo, columns, weights, scalars)


def run_backward(
    place, rows, halo, columns, weights, scalars, grad, saved, entering, later, heads, key_width,
    value_width, quarter,
):
    written, states, inverses, end = saved
    count, lanes = columns.shape[0], rows.shape[1]
    steps, per_quarter = count // STEP, quarter // STEP
    wide = value_width + key_width
    chunks = STEP // CHUNK

    def at(i, place):
        return (block_place(steps - 1 - i, place, per_quarter), 0)

    def halo_at(i, place):
        here = steps - 1 - i
        inner = block_place(jnp.maximum(here - 1, 0), place, per_quarter)
        ratio = STEP // HALO
        return (inner * ratio + ratio - 1, 0)

    fixed = lambda i, place: (0, 0)
    whole = lambda i, place: (0, 0, 0)
    body = functools.partial(
        backward_kernel, heads=heads, key_width=key_width, value_width=value_width
    )
    shapes = (
        jax.ShapeDtypeStruct((count, lanes), bfloat),
        jax.ShapeDtypeStruct((count, columns.shape[1]), single),
        jax.ShapeDtypeStruct((HALO, lanes), single),
        jax.ShapeDtypeStruct((HALO, lanes), single),
    )
    return pl.pallas_call(
        body,
        out_shape=shapes,
        grid_spec=pltpu.PrefetchScalarGridSpec(
            num_scalar_prefetch=1,
            grid=(steps,),
            in_specs=[
                pl.BlockSpec((STEP, lanes), at),
                pl.BlockSpec((HALO, lanes), halo_at),
                pl.BlockSpec((HALO, lanes), fixed),
                pl.BlockSpec((STEP, columns.shape[1]), at),
                pl.BlockSpec(weights.shape, fixed),
                pl.BlockSpec(memory_space=pltpu.SMEM),
                pl.BlockSpec((STEP, heads * value_width), at),
                pl.BlockSpec((STEP, heads * wide), at),
                pl.BlockSpec(
                    (chunks, heads, key_width, wide), lambda i, place: (steps - 1 - i, 0, 0, 0)
                ),
                pl.BlockSpec((STEP, heads * CHUNK), at),
                pl.BlockSpec(end.shape, whole),
                pl.BlockSpec(entering.shape, whole),
                pl.BlockSpec(later.shape, whole),
            ],
            out_specs=[
                pl.BlockSpec((STEP, lanes), at),
                pl.BlockSpec((STEP, columns.shape[1]), at),
                pl.BlockSpec((HALO, lanes), fixed),
                pl.BlockSpec((HALO, lanes), fixed),
            ],
            scratch_shapes=[
                pltpu.VMEM((STEP + HALO, lanes), single),
                pltpu.VMEM((STEP + 8, lanes), single),
                pltpu.VMEM((STEP + 8, 1), jnp.int32),
                pltpu.VMEM((heads, key_width, value_width), single),
                pltpu.VMEM((heads, key_width, value_width), single),
            ],
        ),
        compiler_params=pltpu.CompilerParams(
            dimension_semantics=("arbitrary",), vmem_limit_bytes=VMEM_LIMIT
        ),
        cost_estimate=pl.CostEstimate(
            flops=count * 3_000_000, bytes_accessed=count * 12_000, transcendentals=count * 3000
        ),
        name="delta_backward",
    )(
        place, rows, rows, halo, columns, weights, scalars, grad, written, states, inverses, end,
        entering, later,
    )


def chosen_columns(table, column_sets):
    return column_sets[0:1, :] == table[:, 1:2]


def masked(product, chosen):
    return low(jnp.where(chosen, product, 0.0))


def silu_parts(value):
    logistic = sigmoid(value)
    return logistic, value * logistic


def accumulate(ref, value, first):
    @pl.when(first)
    def _():
        ref[...] = value

    @pl.when(jnp.logical_not(first))
    def _():
        ref[...] += value


def project_kernel(
    rows_ref, table_ref, halo_ref, halo_table_ref, sets_ref, down_ref, wq_ref, wk_ref, wv_ref,
    wg_ref, wm_ref, up_qk_ref, up_vg_ref,
    pre_ref, gate_ref, inner_ref, column_ref, pre_halo_ref,
):
    low_rank = sets_ref.shape[1]
    q_width, v_width = wq_ref.shape[1], wv_ref.shape[1]

    def projections(rows, chosen, store):
        inner = masked(
            nt(rows, down_ref[: 3 * low_rank, :]), jnp.concatenate([chosen] * 3, axis=1)
        )
        store[:, :q_width] = low(
            nn(rows, wq_ref[...]) + nn(inner[:, :low_rank], up_qk_ref[0])
        )
        store[:, q_width : 2 * q_width] = low(
            nn(rows, wk_ref[...]) + nn(inner[:, low_rank : 2 * low_rank], up_qk_ref[1])
        )
        store[:, 2 * q_width :] = low(
            nn(rows, wv_ref[...]) + nn(inner[:, 2 * low_rank :], up_vg_ref[0])
        )
        return inner

    @pl.when(pl.program_id(0) == 0)
    def _():
        projections(
            halo_ref[...], chosen_columns(halo_table_ref[...], sets_ref[...]), pre_halo_ref
        )

    rows = rows_ref[...]
    table = table_ref[...]
    chosen = chosen_columns(table, sets_ref[...])
    inner_ref[:, : 3 * low_rank] = projections(rows, chosen, pre_ref)
    last = masked(nt(rows, down_ref[3 * low_rank :, :]), chosen)
    inner_ref[:, 3 * low_rank :] = last
    gate_ref[...] = nn(rows, wg_ref[...]) + nn(last, up_vg_ref[1])
    mixing = nt(rows, wm_ref[...])
    spare = column_ref.shape[1] - mixing.shape[1]
    column_ref[...] = jnp.concatenate([mixing, table[:, :spare]], axis=1)


def head_outputs(raw_ref, map_ref, entering_ref, heads, key_width, value_width):
    outputs = []
    for h in range(heads):
        outputs.append(
            raw_ref[:, h * value_width : (h + 1) * value_width]
            + nn(map_ref[:, h * key_width : (h + 1) * key_width], entering_ref[h])
        )
    return outputs


def attend_kernel(
    raw_ref, map_ref, gate_ref, table_ref, entering_ref, gain_ref, sets_ref, wo_ref, down_ref,
    up_ref,
    part_ref, z_ref, inner_ref,
    *, heads, key_width, value_width,
):
    chosen = chosen_columns(table_ref[...], sets_ref[...])
    outputs = head_outputs(raw_ref, map_ref, entering_ref, heads, key_width, value_width)
    for h, output in enumerate(outputs):
        lanes = slice(h * value_width, (h + 1) * value_width)
        scale = lax.rsqrt(jnp.mean(output * output, axis=-1, keepdims=True) + EPS)
        _, gate = silu_parts(gate_ref[:, lanes])
        z_ref[:, lanes] = low(output * scale * gain_ref[0:1, :] * gate)
    z = z_ref[...]
    inner = masked(nt(z, down_ref[...]), chosen)
    inner_ref[...] = inner
    part_ref[...] = low(nn(z, wo_ref[...]) + nn(inner, up_ref[...]))


def feed_kernel(
    rows_ref, grad_ref, table_ref, sets_ref, down_ref, wg_ref, wu_ref, wd_ref, up_ff_ref,
    down_ffd_ref, up_ref,
    out_ref, back_ref, down_grad_ref, res_grad_ref, up_grad_ref, ffd_grad_ref,
):
    first = pl.program_id(0) == 0
    low_rank = sets_ref.shape[1]
    chosen = chosen_columns(table_ref[...], sets_ref[...])
    rows, grad = rows_ref[...], grad_ref[...]
    u_gate = masked(nt(rows, down_ref[:low_rank, :]), chosen)
    u_up = masked(nt(rows, down_ref[low_rank:, :]), chosen)
    gate = nt(rows, wg_ref[...]) + nn(u_gate, up_ff_ref[0])
    up = nt(rows, wu_ref[...]) + nn(u_up, up_ff_ref[1])
    logistic, active = silu_parts(gate)
    hidden = low(active * up)
    u_down = masked(nt(hidden, down_ffd_ref[...]), chosen)
    out_ref[...] = low(nn(hidden, wd_ref[...]) + nn(u_down, up_ref[...]))
    du_down = masked(nt(grad, up_ref[...]), chosen)
    hidden_grad = nt(grad, wd_ref[...]) + nn(du_down, down_ffd_ref[...])
    gate_grad = low(hidden_grad * up * logistic * (1.0 + gate * (1.0 - logistic)))
    up_grad = low(hidden_grad * active)
    du_gate = masked(nt(gate_grad, up_ff_ref[0]), chosen)
    du_up = masked(nt(up_grad, up_ff_ref[1]), chosen)
    back_ref[...] = low(
        nn(gate_grad, wg_ref[...])
        + nn(up_grad, wu_ref[...])
        + nn(du_gate, down_ref[:low_rank, :])
        + nn(du_up, down_ref[low_rank:, :])
    )
    accumulate(down_grad_ref.at[0], tn(du_gate, rows), first)
    accumulate(down_grad_ref.at[1], tn(du_up, rows), first)
    accumulate(res_grad_ref, tn(u_down, grad), first)
    accumulate(up_grad_ref.at[0], tn(u_gate, gate_grad), first)
    accumulate(up_grad_ref.at[1], tn(u_up, up_grad), first)
    accumulate(ffd_grad_ref, tn(du_down, hidden), first)


def branch_kernel(
    branch_ref, raw_ref, map_ref, gate_ref, z_ref, u_out_ref, rows_ref, inner_ref, table_ref,
    entering_ref, gain_ref, sets_ref, wo_ref, down_out_ref, up_ref, up_vg_ref,
    raw_grad_ref, gate_grad_ref, du_ref, state_grad_ref, res_grad_ref, out_grad_ref,
    up_grad_ref, down_grad_ref,
    *, heads, key_width, value_width,
):
    first = pl.program_id(0) == 0
    low_rank = sets_ref.shape[1]
    chosen = chosen_columns(table_ref[...], sets_ref[...])
    branch = branch_ref[...]
    outputs = head_outputs(raw_ref, map_ref, entering_ref, heads, key_width, value_width)
    du_out = masked(nt(branch, up_ref[...]), chosen)
    mixed_grad = nt(branch, wo_ref[...]) + nn(du_out, down_out_ref[...])
    gain = gain_ref[0:1, :]
    for h, output in enumerate(outputs):
        lanes = slice(h * value_width, (h + 1) * value_width)
        scale = lax.rsqrt(jnp.mean(output * output, axis=-1, keepdims=True) + EPS)
        value = gate_ref[:, lanes]
        logistic, active = silu_parts(value)
        incoming = mixed_grad[:, lanes]
        gate_grad_ref[:, lanes] = low(
            incoming
            * (output * scale * gain)
            * (logistic * (1.0 + value * (1.0 - logistic)))
        )
        scaled = gain * (incoming * active)
        dot = jnp.mean(output * scaled, axis=-1, keepdims=True)
        raw_grad = low(scale * scaled - output * (scale * scale * scale * dot))
        raw_grad_ref[:, lanes] = raw_grad
        accumulate(
            state_grad_ref.at[h],
            tn(map_ref[:, h * key_width : (h + 1) * key_width], raw_grad),
            first,
        )
    gate_grad = gate_grad_ref[...]
    du_gate = masked(nt(gate_grad, up_vg_ref[1]), chosen)
    du_ref[...] = du_gate
    accumulate(res_grad_ref, tn(u_out_ref[...], branch), first)
    accumulate(out_grad_ref, tn(du_out, z_ref[...]), first)
    accumulate(up_grad_ref, tn(inner_ref[...], gate_grad), first)
    accumulate(down_grad_ref, tn(du_gate, rows_ref[...]), first)


def settle_kernel(
    pre_ref, gate_grad_ref, du_gate_ref, mix_ref, rows_ref, inner_ref, table_ref, sets_ref,
    down_ref, wq_ref, wk_ref, wv_ref, wg_ref, wm_ref, up_qk_ref, up_vg_ref,
    part_ref, down_grad_ref, up_qk_grad_ref, up_v_grad_ref,
):
    first = pl.program_id(0) == 0
    low_rank = sets_ref.shape[1]
    q_width = wq_ref.shape[1]
    chosen = chosen_columns(table_ref[...], sets_ref[...])
    query, key = pre_ref[:, :q_width], pre_ref[:, q_width : 2 * q_width]
    value = pre_ref[:, 2 * q_width :]
    rows = rows_ref[...]
    du = jnp.concatenate(
        [
            masked(nt(query, up_qk_ref[0]), chosen),
            masked(nt(key, up_qk_ref[1]), chosen),
            masked(nt(value, up_vg_ref[0]), chosen),
            du_gate_ref[...],
        ],
        axis=1,
    )
    part_ref[...] = low(
        nt(query, wq_ref[...])
        + nt(key, wk_ref[...])
        + nt(value, wv_ref[...])
        + nt(gate_grad_ref[...], wg_ref[...])
        + nn(du, down_ref[...])
        + nn(low(mix_ref[...]), wm_ref[...])
    )
    accumulate(down_grad_ref, tn(du[:, : 3 * low_rank], rows), first)
    accumulate(up_qk_grad_ref.at[0], tn(inner_ref[:, :low_rank], query), first)
    accumulate(up_qk_grad_ref.at[1], tn(inner_ref[:, low_rank : 2 * low_rank], key), first)
    accumulate(up_v_grad_ref, tn(inner_ref[:, 2 * low_rank : 3 * low_rank], value), first)


def by_rows(width, lane_block=0):
    return ("rows", width, lane_block)


def blocked_call(body, name, count, inputs, outputs, flops):
    block = min(STEP, count)
    in_specs, arrays, moved = [], [], 0
    for array, kind in inputs:
        arrays.append(array)
        moved += array.size * array.dtype.itemsize
        if kind is None:
            zeros = (0,) * array.ndim
            in_specs.append(
                pl.BlockSpec(
                    array.shape, lambda i, zeros=zeros: zeros, pipeline_mode=pl.Buffered(1)
                )
            )
        else:
            in_specs.append(
                pl.BlockSpec((block, kind[1]), lambda i, lane=kind[2]: (i, lane))
            )
    out_specs, shapes = [], []
    for shape, dtype, rowwise in outputs:
        shapes.append(jax.ShapeDtypeStruct(shape, dtype))
        if rowwise:
            out_specs.append(pl.BlockSpec((block, shape[1]), lambda i: (i, 0)))
        else:
            zeros = (0,) * len(shape)
            out_specs.append(pl.BlockSpec(shape, lambda i, zeros=zeros: zeros))
    return pl.pallas_call(
        body,
        out_shape=tuple(shapes),
        grid=(count // block,),
        in_specs=in_specs,
        out_specs=out_specs,
        compiler_params=pltpu.CompilerParams(
            dimension_semantics=("arbitrary",), vmem_limit_bytes=VMEM_LIMIT
        ),
        cost_estimate=pl.CostEstimate(flops=flops, bytes_accessed=moved, transcendentals=0),
        name=name,
    )(*arrays)


def flip(array, bit):
    groups = lax.axis_size("head")
    return lax.ppermute(array, "head", [(i, i ^ bit) for i in range(groups)])


def gather_rows(array):
    far = flip(array, 2)
    near = flip(array, 1)
    return jnp.concatenate([array, near, far, flip(far, 1)], axis=0)


def scatter_sum(blocks):
    near, corner = flip(low(blocks[1]), 1), flip(low(blocks[3]), 1)
    far = blocks[2].astype(single) + corner.astype(single)
    return blocks[0].astype(single) + near.astype(single) + flip(low(far), 2).astype(single)


def scatter_rows(partial):
    size = partial.shape[0] // 4
    return scatter_sum([partial[b * size : (b + 1) * size] for b in range(4)])


def shifted_along(array, axis, by):
    length = lax.axis_size(axis)
    pairs = [(i, i + by) for i in range(length) if 0 <= i + by < length]
    return lax.ppermute(array, axis, pairs)


def reduce_maps(shared, owned):
    members = lax.axis_size("seq")
    place = lax.axis_index("head")
    widths = [part.shape[1] // 4 for part in shared]

    def block(part, relative):
        size = part.shape[1] // 4
        return lax.dynamic_slice_in_dim(part, (place ^ relative) * size, size, 1)

    mine = scatter_sum(
        [jnp.concatenate([block(part, b) for part in shared], axis=1) for b in range(4)]
    )
    flat = jnp.concatenate([low(mine)] + [low(part) for part in owned], axis=1)
    rows, lanes = flat.shape
    parts = lax.all_to_all(flat.reshape(members, rows // members, lanes), "seq", 0, 0)
    summed = low(jnp.sum(parts.astype(single), axis=0))
    spread = jnp.broadcast_to(summed[None], (members,) + summed.shape)
    total = lax.all_to_all(spread, "seq", 0, 0).reshape(rows, lanes)
    shared_lanes = sum(widths)
    piece = total[:, :shared_lanes]
    far = flip(piece, 2)
    pieces = jnp.stack([piece, flip(piece, 1), far, flip(far, 1)])
    ordered = [lax.dynamic_index_in_dim(pieces, place ^ b, 0, False) for b in range(4)]
    full, at = [], 0
    for width in widths:
        full.append(
            jnp.concatenate(
                [ordered[b][:, at : at + width].astype(single) for b in range(4)], axis=1
            )
        )
        at += width
    local, at = [], shared_lanes
    for part in owned:
        local.append(total[:, at : at + part.shape[1]].astype(single))
        at += part.shape[1]
    return full, local


def rms_scale(rows, gain):
    return rows * lax.rsqrt(jnp.mean(rows * rows, axis=-1, keepdims=True) + EPS) * gain


def rms_back(rows, gain, incoming):
    _, back = jax.vjp(lambda value: rms_scale(value, gain), rows)
    return back(incoming)[0]


def on_device(
    block_input,
    out_grad,
    lengths,
    doc_sets,
    norm1_gain,
    w_query,
    w_key,
    w_value,
    conv_query,
    conv_key,
    conv_value,
    w_decay_beta,
    decay_rate,
    decay_bias,
    w_gate_out,
    out_gain,
    w_out,
    norm2_gain,
    w_gate,
    w_up,
    w_down,
    adapt_down,
    adapt_up_qk,
    adapt_up_vg,
    adapt_up_ff,
    adapt_down_out,
    adapt_down_ffd,
    adapt_up_res,
):
    groups = lax.axis_size("head")
    members = lax.axis_size("seq")
    place = lax.axis_index("head")
    quarter, width = block_input.shape
    count = quarter * groups
    heads = decay_rate.shape[0]
    key_width = w_query.shape[1] // heads
    value_width = w_value.shape[1] // heads
    sets, rank = adapt_down.shape[1], adapt_down.shape[3]
    low_rank = sets * rank
    qk = heads * key_width
    device_start = lax.axis_index("seq") * count
    starts = jnp.sum(
        jnp.where(
            jnp.arange(lengths.shape[0])[None, :] < jnp.arange(lengths.shape[0])[:, None],
            lengths[None, :],
            0,
        ),
        axis=1,
    )
    order = jnp.arange(groups, dtype=jnp.int32) ^ place

    def tables(positions):
        reached = positions[:, None] >= starts[None, :]
        token_start = jnp.max(jnp.where(reached, starts[None, :], -1), axis=1)
        ended = positions[:, None] >= (starts + lengths)[None, :]
        token_set = jnp.sum(jnp.where(reached & ~ended, doc_sets[None, :], 0), axis=1)
        pair = jnp.stack([token_start - device_start, token_set], axis=1).astype(single)
        return jnp.pad(pair, ((0, 0), (0, 8 - pair.shape[1])))

    table = tables(
        (
            device_start + order[:, None] * quarter + jnp.arange(quarter, dtype=jnp.int32)[None, :]
        ).reshape(-1)
    )
    halo_table = tables(device_start + jnp.arange(-HALO, 0, dtype=jnp.int32))
    column_sets = jnp.broadcast_to(
        (jnp.arange(low_rank, dtype=jnp.int32) // rank).astype(single)[None, :], (8, low_rank)
    )

    down = adapt_down.transpose(0, 1, 3, 2).reshape(6 * low_rank, width)
    mixer_down, feed_down = down[: 4 * low_rank], down[4 * low_rank :]
    up_qk = adapt_up_qk.reshape(2, low_rank, -1)
    up_vg = adapt_up_vg.reshape(2, low_rank, -1)
    up_ff = adapt_up_ff.reshape(2, low_rank, -1)
    down_out = adapt_down_out.transpose(0, 2, 1).reshape(low_rank, -1)
    down_ffd = adapt_down_ffd.transpose(0, 2, 1).reshape(low_rank, -1)
    up_res = adapt_up_res.reshape(2, low_rank, width)
    conv = jnp.concatenate([conv_query, conv_key, conv_value], axis=1).astype(single)
    scalars = jnp.stack([decay_rate, decay_bias])
    where = place.reshape(1).astype(jnp.int32)
    weight_mix = w_decay_beta.transpose(1, 2, 0).reshape(2 * heads, width)
    weight_mix_padded = jnp.pad(weight_mix, ((0, 8 - 2 * heads), (0, 0)))
    gain = jnp.broadcast_to(out_gain[None, :], (8, value_width))
    hidden_width = w_down.shape[0]
    value_lanes = heads * value_width

    input_float = block_input.astype(single)
    normed = low(rms_scale(input_float, norm1_gain))
    tail = normed[quarter - HALO :]
    halo = sum(
        lax.ppermute(
            tail,
            ("seq", "head"),
            [((s * groups) + groups - 1, (s + 1) * groups + h) for s in range(members - 1)],
        )
        for h in range(groups)
    )
    normed_all = gather_rows(normed)
    grad_all = gather_rows(out_grad)
    pre, gate_input, inner, columns, pre_halo = blocked_call(
        project_kernel,
        "project",
        count,
        [
            (normed_all, by_rows(width)),
            (table, by_rows(8)),
            (halo, None),
            (halo_table, None),
            (column_sets, None),
            (mixer_down, None),
            (w_query, None),
            (w_key, None),
            (w_value, None),
            (w_gate_out, None),
            (weight_mix, None),
            (up_qk, None),
            (up_vg, None),
        ],
        [
            ((count, 2 * qk + value_lanes), bfloat, True),
            ((count, value_lanes), single, True),
            ((count, 4 * low_rank), bfloat, True),
            ((count, 8), single, True),
            ((HALO, 2 * qk + value_lanes), bfloat, False),
        ],
        count * 5_000_000,
    )
    raw_local, mapped, *saved = run_forward(
        where, pre, pre_halo, columns, conv, scalars, heads, key_width, value_width, quarter
    )
    end = saved[-1]

    hops = min(members - 1, -(-(DOC_MAX - 1) // count))
    end_low = low(end)
    entering = None
    for hop in range(hops, 0, -1):
        if entering is None:
            entering = shifted_along(end_low[:, :, :value_width], "seq", hop).astype(single)
        else:
            got = shifted_along(end_low, "seq", hop)
            entering = got[:, :, :value_width].astype(single) + jnp.einsum(
                "hij,hjk->hik",
                got[:, :, value_width:],
                low(entering),
                preferred_element_type=single,
            )
    maps_after = [
        shifted_along(end_low[:, :, value_width:], "seq", -hop) for hop in range(1, hops)
    ]
    entering_low = low(entering)

    sizes = dict(heads=heads, key_width=key_width, value_width=value_width)
    attention_part, mixed, u_out = blocked_call(
        functools.partial(attend_kernel, **sizes),
        "attend",
        count,
        [
            (raw_local, by_rows(value_lanes)),
            (mapped, by_rows(qk)),
            (gate_input, by_rows(value_lanes)),
            (table, by_rows(8)),
            (entering_low, None),
            (gain, None),
            (column_sets, None),
            (w_out, None),
            (down_out, None),
            (up_res[0], None),
        ],
        [
            ((count, width), bfloat, True),
            ((count, value_lanes), bfloat, True),
            ((count, low_rank), bfloat, True),
        ],
        count * 1_600_000,
    )
    residual = input_float + scatter_rows(attention_part)
    normed_mid = low(rms_scale(residual, norm2_gain))
    mid_all = gather_rows(normed_mid)

    out_part, mid_part, feed_down_grad, feed_res_grad, feed_up_grad, ffd_grad = blocked_call(
        feed_kernel,
        "feed",
        count,
        [
            (mid_all, by_rows(width)),
            (grad_all, by_rows(width)),
            (table, by_rows(8)),
            (column_sets, None),
            (feed_down, None),
            (w_gate.T, None),
            (w_up.T, None),
            (w_down, None),
            (up_ff, None),
            (down_ffd, None),
            (up_res[1], None),
        ],
        [
            ((count, width), bfloat, True),
            ((count, width), bfloat, True),
            ((2, low_rank, width), single, False),
            ((low_rank, width), single, False),
            ((2, low_rank, hidden_width), single, False),
            ((low_rank, hidden_width), single, False),
        ],
        count * 13_000_000,
    )
    mid_grad = scatter_rows(mid_part)
    residual_grad = out_grad.astype(single) + rms_back(residual, norm2_gain, mid_grad)
    branch_grad = gather_rows(low(residual_grad))
    result = residual + scatter_rows(out_part)

    (
        raw_grad,
        gate_grad,
        du_outgate,
        state_grad,
        branch_res_grad,
        out_down_grad,
        outgate_up_grad,
        outgate_down_grad,
    ) = blocked_call(
        functools.partial(branch_kernel, **sizes),
        "branch",
        count,
        [
            (branch_grad, by_rows(width)),
            (raw_local, by_rows(value_lanes)),
            (mapped, by_rows(qk)),
            (gate_input, by_rows(value_lanes)),
            (mixed, by_rows(value_lanes)),
            (u_out, by_rows(low_rank)),
            (normed_all, by_rows(width)),
            (inner, by_rows(low_rank, 3)),
            (table, by_rows(8)),
            (entering_low, None),
            (gain, None),
            (column_sets, None),
            (w_out, None),
            (down_out, None),
            (up_res[0], None),
            (up_vg, None),
        ],
        [
            ((count, value_lanes), bfloat, True),
            ((count, value_lanes), bfloat, True),
            ((count, low_rank), bfloat, True),
            ((heads, key_width, value_width), single, False),
            ((low_rank, width), single, False),
            ((low_rank, value_lanes), single, False),
            ((low_rank, value_lanes), single, False),
            ((low_rank, width), single, False),
        ],
        count * 3_000_000,
    )
    state_low = low(state_grad)
    later = None
    for hop in range(hops, 0, -1):
        got = shifted_along(state_low, "seq", -hop).astype(single)
        if later is None:
            later = got
        else:
            later = got + jnp.einsum(
                "hji,hjk->hik", maps_after[hop - 1], low(later), preferred_element_type=single
            )

    first_shared, first_owned = reduce_maps(
        [outgate_down_grad, feed_down_grad[0], feed_down_grad[1], branch_res_grad, feed_res_grad],
        [outgate_up_grad, feed_up_grad[0], feed_up_grad[1], out_down_grad, ffd_grad],
    )

    pre_grad, mix_grad, tail_grad, edge_grad = run_backward(
        where, pre, pre_halo, columns, conv, scalars, raw_grad, saved, entering_low, low(later),
        heads, key_width, value_width, quarter,
    )
    arrived = shifted_along(edge_grad, "seq", -1)
    tail_at = ((groups - 1) ^ place) * quarter + quarter - HALO
    pre_grad = lax.dynamic_update_slice_in_dim(pre_grad, low(tail_grad + arrived), tail_at, 0)
    normed_part, mixer_down_grad, up_qk_grad, up_v_grad = blocked_call(
        settle_kernel,
        "settle",
        count,
        [
            (pre_grad, by_rows(2 * qk + value_lanes)),
            (gate_grad, by_rows(value_lanes)),
            (du_outgate, by_rows(low_rank)),
            (mix_grad, by_rows(8)),
            (normed_all, by_rows(width)),
            (inner, by_rows(4 * low_rank)),
            (table, by_rows(8)),
            (column_sets, None),
            (mixer_down, None),
            (w_query, None),
            (w_key, None),
            (w_value, None),
            (w_gate_out, None),
            (weight_mix_padded, None),
            (up_qk, None),
            (up_vg, None),
        ],
        [
            ((count, width), bfloat, True),
            ((3 * low_rank, width), single, False),
            ((2, low_rank, qk), single, False),
            ((low_rank, value_lanes), single, False),
        ],
        count * 7_000_000,
    )
    last_shared, last_owned = reduce_maps(
        [mixer_down_grad[p * low_rank : (p + 1) * low_rank] for p in range(3)],
        [up_qk_grad[0], up_qk_grad[1], up_v_grad],
    )
    normed_grad = scatter_rows(normed_part)
    input_grad = residual_grad + rms_back(input_float, norm1_gain, normed_grad)

    def as_down(rows):
        return rows.reshape(sets, rank, -1).transpose(0, 2, 1)

    def as_up(rows):
        return rows.reshape(sets, rank, -1)

    down_total = jnp.stack([as_down(part) for part in last_shared + first_shared[:3]])
    return (
        low(result),
        input_grad,
        down_total,
        jnp.stack([as_up(last_owned[0]), as_up(last_owned[1])]),
        jnp.stack([as_up(last_owned[2]), as_up(first_owned[0])]),
        jnp.stack([as_up(first_owned[1]), as_up(first_owned[2])]),
        as_down(first_owned[3]),
        as_down(first_owned[4]),
        jnp.stack([as_up(first_shared[3]), as_up(first_shared[4])]),
    )


def solution(mesh):
    rows = P(("seq", "head"), None)
    lanes = P(None, "head")
    last = P(None, None, None, "head")
    middle = P(None, "head", None)
    in_specs = (
        rows, rows, P(), P(), P(), lanes, lanes, lanes, lanes, lanes, lanes,
        P(None, None, "head"), P("head"), P("head"), lanes, P(), P("head", None), P(), lanes,
        lanes, P("head", None), P(), last, last, last, middle, middle, P(),
    )
    out_specs = (rows, rows, P(), last, last, last, middle, middle, P())
    return jax.shard_map(
        on_device, mesh=mesh, in_specs=in_specs, out_specs=out_specs, check_vma=False
    )
```

profile of v0, /device:TPU:0, one launch (start us, length us, event | category | flops | bytes accessed | tf_op | source)
XLA Modules:
  0.0 449.9 jit_solution(17225516780117549403)
XLA Ops:
  30.9 13.3 %project.1 = (bf16[1024,1024]{1,0:T(8,128)(2,1)}, f32[1024,512]{1,0:T(8,128)}, bf16[1024,512]{1,0:T(8,128)(2,1)}, f32[1024,8]{1,0:T(8,128)}, bf16[16,1024]{1,0:T(8,128)(2,1)}) custom-call(bf16[1024,1024]{1,0:T(8,128)(2,1)} %pad_maximum_fusion.rows_ref, f32[1024,8]{1,0:T(8,128)} %pad.12.table_ref, bf16[16,1024]{1,0:T(8,128)(2,1)} %add_add_fusion.2.halo_ref, ...), custom_call_target="tpu_custom_call" | custom-call | flops 5120000000 | bytes 6763008 | tf_op jit(solution)/shard_map/project/pallas_call | solution.py:861
  44.2 20.3 %delta_forward.1 = (f32[1024,512]{1,0:T(8,128)}, bf16[1024,256]{1,0:T(8,128)(2,1)}, bf16[1024,768]{1,0:T(8,128)(2,1)}, bf16[8,2,128,384]{3,2,1,0:T(8,128)(2,1)},...) custom-call(s32[1]{0:T(128)} %bitcast.place, bf16[1024,1024]{1,0:T(8,128)(2,1)} %get-tuple-element.45.rows_ref.before_ref, ...), custom_call_target="tpu_custom_call" | custom-call | flops 2048000000 | bytes 10240000 | tf_op jit(solution)/shard_map/delta_forward/pallas_call | solution.py:507
  65.6 5.3 %collective-permute-start.9 = (bf16[2,128,384]{2,1,0:T(8,128)(2,1)S(1)}, bf16[2,128,384]{2,1,0:T(8,128)(2,1)S(1)}, u32[]{:S(2)}, u32[]{:S(2)}) collective-permute-start(bf16[2,128,384]{2,1,0:T(8,128)(2,1)S(1)} %convert_element_type.281), channel_id=1, source_target_pairs={{0,12},{4,16},{8,20},{12,24},{16,28},{1,13},{5,17},{9,21},{13,25},... | collective-permute-start | bytes 589832 | tf_op jit(solution)/shard_map/ppermute | solution.py:900
  70.9 3.9 collective-permute-start.10
  85.3 7.6 %attend.1 = (bf16[1024,1024]{1,0:T(8,128)(2,1)}, bf16[1024,512]{1,0:T(8,128)(2,1)}, bf16[1024,128]{1,0:T(8,128)(2,1)}) custom-call(f32[1024,512]{1,0:T(8,128)} %get-tuple-element.48.raw_ref, bf16[1024,256]{1,0:T(8,128)(2,1)} %get-tuple-element.49.map_ref, f32[1024,512]{1,0:T(8,128)} %get-tuple-element.50.gate_ref, f32[1024,8]{1,0:T(8,128)} %pad.12.table_ref, ...), custom_call_target="tpu_custom_call" | custom-call | flops 1638400000 | bytes 6336512 | tf_op jit(solution)/shard_map/attend/pallas_call | solution.py:861
  100.3 12.6 %collective-permute-done.13 = bf16[256,1024]{1,0:T(8,128)(2,1)S(1)} collective-permute-done((bf16[256,1024]{1,0:T(8,128)(2,1)S(1)}, bf16[256,1024]{1,0:T(8,128)(2,1)S(1)}, u32[]{:S(2)}, u32[]{:S(2)}) %collective-permute-start.13) | collective-permute-done | bytes 524320 | tf_op jit(solution)/shard_map/ppermute | solution.py:877
  116.6 7.5 %collective-permute-done.18 = bf16[256,1024]{1,0:T(8,128)(2,1)S(1)} collective-permute-done((bf16[256,1024]{1,0:T(8,128)(2,1)S(1)}, bf16[256,1024]{1,0:T(8,128)(2,1)S(1)}, u32[]{:S(2)}, u32[]{:S(2)}) %collective-permute-start.18) | collective-permute-done | bytes 524320 | tf_op jit(solution)/shard_map/ppermute | solution.py:877
  124.6 10.2 %collective-permute-done.15 = bf16[256,1024]{1,0:T(8,128)(2,1)S(1)} collective-permute-done((bf16[256,1024]{1,0:T(8,128)(2,1)S(1)}, bf16[256,1024]{1,0:T(8,128)(2,1)S(1)}, u32[]{:S(2)}, u32[]{:S(2)}) %collective-permute-start.15) | collective-permute-done | bytes 524320 | tf_op jit(solution)/shard_map/ppermute | solution.py:877
  138.8 32.4 %feed.1 = (bf16[1024,1024]{1,0:T(8,128)(2,1)}, bf16[1024,1024]{1,0:T(8,128)(2,1)}, f32[2,128,1024]{2,1,0:T(8,128)}, f32[128,1024]{1,0:T(8,128)}, f32[2,128,704]{2,1,0:T(8,128)}, /*index=5*/f32[128,704]{1,0:T(8,128)}) custom-call(bf16[1024,1024]{1,0:T(8,128)(2,1)} %pad_maximum_fusion.1.rows_ref, bf16[1024,1024]{1,0:T(8,128)(2,1)} %pad_maximum_fusion.2.grad_ref, ...), custom_call_target="tpu_custom_call" | custom-call | flops 13312000000 | bytes 9883648 | tf_op jit(solution)/shard_map/feed/pallas_call | solution.py:861
  177.6 12.2 %collective-permute-done.25 = bf16[256,1024]{1,0:T(8,128)(2,1)S(1)} collective-permute-done((bf16[256,1024]{1,0:T(8,128)(2,1)S(1)}, bf16[256,1024]{1,0:T(8,128)(2,1)S(1)}, u32[]{:S(2)}, u32[]{:S(2)}) %collective-permute-start.25) | collective-permute-done | bytes 524320 | tf_op jit(solution)/shard_map/ppermute | solution.py:877
  190.2 10.3 %collective-permute-done.22 = bf16[256,1024]{1,0:T(8,128)(2,1)S(1)} collective-permute-done((bf16[256,1024]{1,0:T(8,128)(2,1)S(1)}, bf16[256,1024]{1,0:T(8,128)(2,1)S(1)}, u32[]{:S(2)}, u32[]{:S(2)}) %collective-permute-start.22) | collective-permute-done | bytes 524320 | tf_op jit(solution)/shard_map/ppermute | solution.py:877
  203.7 11.8 %collective-permute-done.27 = bf16[256,1024]{1,0:T(8,128)(2,1)} collective-permute-done((bf16[256,1024]{1,0:T(8,128)(2,1)S(1)}, bf16[256,1024]{1,0:T(8,128)(2,1)}, u32[]{:S(2)}, u32[]{:S(2)}) %collective-permute-start.27) | collective-permute-done | bytes 524320 | tf_op jit(solution)/shard_map/ppermute | solution.py:877
  224.5 15.7 %branch.1 = (bf16[1024,512]{1,0:T(8,128)(2,1)}, bf16[1024,512]{1,0:T(8,128)(2,1)}, bf16[1024,128]{1,0:T(8,128)(2,1)}, f32[2,128,256]{2,1,0:T(8,128)}, f32[128,10...) custom-call(bf16[1024,1024]{1,0:T(8,128)(2,1)} %pad_maximum_fusion.3.branch_ref, ...), custom_call_target="tpu_custom_call" | custom-call | flops 3072000000 | bytes 13152256 | tf_op jit(solution)/shard_map/branch/pallas_call | solution.py:861
  253.7 11.7 %collective-permute-done.35 = bf16[2,128,256]{2,1,0:T(8,128)(2,1)S(1)} collective-permute-done((bf16[2,128,256]{2,1,0:T(8,128)(2,1)}, bf16[2,128,256]{2,1,0:T(8,128)(2,1)S(1)}, u32[]{:S(2)}, u32[]{:S(2)}) %collective-permute-start.35) | collective-permute-done | bytes 131104 | tf_op jit(solution)/shard_map/ppermute | solution.py:900
  268.4 4.8 %collective-permute-done.33 = bf16[2,128,256]{2,1,0:T(8,128)(2,1)} collective-permute-done((bf16[2,128,256]{2,1,0:T(8,128)(2,1)}, bf16[2,128,256]{2,1,0:T(8,128)(2,1)}, u32[]{:S(2)}, u32[]{:S(2)}) %collective-permute-start.33) | collective-permute-done | bytes 131104 | tf_op jit(solution)/shard_map/ppermute | solution.py:900
  276.8 21.0 %delta_backward.1 = (bf16[1024,1024]{1,0:T(8,128)(2,1)}, f32[1024,8]{1,0:T(8,128)}, f32[16,1024]{1,0:T(8,128)}, f32[16,1024]{1,0:T(8,128)}) custom-call(s32[1]{0:T(128)} %bitcast.place, bf16[1024,1024]{1,0:T(8,128)(2,1)} %get-tuple-element.45.rows_ref.before_ref, bf16[1024,1024]{1,0:T(8,128)(2,1)} %get-tuple-element.45.rows_ref.before_ref, ...), custom_call_target="tpu_custom_call" | custom-call | flops 3072000000 | bytes 12288000 | tf_op jit(solution)/shard_map/delta_backward/pallas_call | solution.py:573
  299.8 7.5 %collective-permute-done.36 = f32[16,1024]{1,0:T(8,128)S(1)} collective-permute-done((f32[16,1024]{1,0:T(8,128)}, f32[16,1024]{1,0:T(8,128)S(1)}, u32[]{:S(2)}, u32[]{:S(2)}) %collective-permute-start.36) | collective-permute-done | bytes 65568 | tf_op jit(solution)/shard_map/ppermute | solution.py:900
  308.8 15.3 %settle.1 = (bf16[1024,1024]{1,0:T(8,128)(2,1)}, f32[384,1024]{1,0:T(8,128)}, f32[2,128,256]{2,1,0:T(8,128)}, f32[128,512]{1,0:T(8,128)}) custom-call(bf16[1024,1024]{1,0:T(8,128)(2,1)} %fusion.36.pre_ref, bf16[1024,512]{1,0:T(8,128)(2,1)} %get-tuple-element.66.gate_grad_ref, bf16[1024,128]{1,0:T(8,128)(2,1)} %get-tuple-element.67.du_gate_ref, ...), custom_call_target="tpu_custom_call" | custom-call | flops 7168000000 | bytes 11227136 | tf_op jit(solution)/shard_map/settle/pallas_call | solution.py:861
  329.4 5.4 %collective-permute-done.42 = bf16[128,768]{1,0:T(8,128)(2,1)S(1)} collective-permute-done((bf16[128,768]{1,0:T(8,128)(2,1)S(1)}, bf16[128,768]{1,0:T(8,128)(2,1)S(1)}, u32[]{:S(2)}, u32[]{:S(2)}) %collective-permute-start.42) | collective-permute-done | bytes 196640 | tf_op jit(solution)/shard_map/ppermute | solution.py:877
  335.6 5.2 %all-to-all-start = ((bf16[8,16,1792]{2,1,0:T(8,128)(2,1)}), bf16[8,16,1792]{2,1,0:T(8,128)(2,1)S(1)}, u32[]{:S(2)}, u32[]{:S(2)}) async-start(bf16[8,16,1792]{2,1,0:T(8,128)(2,1)} %bitcast.25), calls=%async_computation | async-start | bytes 917504 | tf_op jit(solution)/shard_map/all_to_all | solution.py:917
  347.6 6.0 %all-to-all-done = bf16[8,16,1792]{2,1,0:T(8,128)(2,1)S(1)} async-done(((bf16[8,16,1792]{2,1,0:T(8,128)(2,1)}), bf16[8,16,1792]{2,1,0:T(8,128)(2,1)S(1)}, u32[]{:S(2)}, u32[]{:S(2)}) %all-to-all-start) | async-done | bytes 458784 | tf_op jit(solution)/shard_map/all_to_all | solution.py:917
  379.3 11.8 %collective-permute-done.39 = bf16[256,1024]{1,0:T(8,128)(2,1)} collective-permute-done((bf16[256,1024]{1,0:T(8,128)(2,1)}, bf16[256,1024]{1,0:T(8,128)(2,1)}, u32[]{:S(2)}, u32[]{:S(2)}) %collective-permute-start.39) | collective-permute-done | bytes 524320 | tf_op jit(solution)/shard_map/ppermute | solution.py:877
  410.0 26.0 %all-to-all-done.3 = bf16[8,16,4416]{2,1,0:T(8,128)(2,1)S(1)} async-done(((bf16[8,16,4416]{2,1,0:T(8,128)(2,1)}), bf16[8,16,4416]{2,1,0:T(8,128)(2,1)S(1)}, u32[]{:S(2)}, u32[]{:S(2)}) %all-to-all-start.3) | async-done | bytes 1130528 | tf_op jit(solution)/shard_map/all_to_all | solution.py:920
  439.6 5.0 %collective-permute-done.50 = bf16[128,1280]{1,0:T(8,128)(2,1)S(1)} collective-permute-done((bf16[128,1280]{1,0:T(8,128)(2,1)S(1)}, bf16[128,1280]{1,0:T(8,128)(2,1)S(1)}, u32[]{:S(2)}, u32[]{:S(2)}) %collective-permute-start.50) | collective-permute-done | bytes 327712 | tf_op jit(solution)/shard_map/ppermute | solution.py:877
  (278 shorter events, 165.5 us)
Async XLA Ops:
  3.3 19.6 %collective-permute-start.3 = (bf16[16,1024]{1,0:T(8,128)(2,1)S(1)}, bf16[16,1024]{1,0:T(8,128)(2,1)S(1)}, u32[]{:S(2)}, u32[]{:S(2)}) collective-permute-start(bf16[16,1024]{1,0:T(8,128)(2,1)S(1)} %slice.337), channel_id=1, source_target_pairs={{3,4},{7,8},{11,12},{15,16},{19,20},{23,24},{27,28}} | collective-permute-start | bytes 98312 | tf_op jit(solution)/shard_map/ppermute | solution.py:1041
  3.9 23.0 %collective-permute-start.4 = (bf16[16,1024]{1,0:T(8,128)(2,1)S(1)}, bf16[16,1024]{1,0:T(8,128)(2,1)S(1)}, u32[]{:S(2)}, u32[]{:S(2)}) collective-permute-start(bf16[16,1024]{1,0:T(8,128)(2,1)S(1)} %slice.337), channel_id=1, source_target_pairs={{3,5},{7,9},{11,13},{15,17},{19,21},{23,25},{27,29}} | collective-permute-start | bytes 98312 | tf_op jit(solution)/shard_map/ppermute | solution.py:1041
  4.6 22.3 %collective-permute-start.5 = (bf16[16,1024]{1,0:T(8,128)(2,1)S(1)}, bf16[16,1024]{1,0:T(8,128)(2,1)S(1)}, u32[]{:S(2)}, u32[]{:S(2)}) collective-permute-start(bf16[16,1024]{1,0:T(8,128)(2,1)S(1)} %slice.337), channel_id=1, source_target_pairs={{3,6},{7,10},{11,14},{15,18},{19,22},{23,26},{27,30}} | collective-permute-start | bytes 98312 | tf_op jit(solution)/shard_map/ppermute | solution.py:1041
  8.3 19.3 %collective-permute-start = (bf16[256,1024]{1,0:T(8,128)(2,1)S(1)}, bf16[256,1024]{1,0:T(8,128)(2,1)}, u32[]{:S(2)}, u32[]{:S(2)}) collective-permute-start(bf16[256,1024]{1,0:T(8,128)(2,1)S(1)} %fusion.4), channel_id=1, source_target_pairs={{0,1},{1,0},{2,3},{3,2},{4,5},{5,4},{6,7},{7,6},{8,9},{9,8},{10,11... | collective-permute-start | bytes 1572872 | tf_op jit(solution)/shard_map/ppermute | solution.py:877
  97.5 15.4 %collective-permute-start.13 = (bf16[256,1024]{1,0:T(8,128)(2,1)S(1)}, bf16[256,1024]{1,0:T(8,128)(2,1)S(1)}, u32[]{:S(2)}, u32[]{:S(2)}) collective-permute-start(bf16[256,1024]{1,0:T(8,128)(2,1)S(1)} %add_convert_fusion.4), channel_id=1, source_target_pairs={{0,2},{1,3},{2,0},{3,1},{4,6},{5,7},{6,4},{7,5},{8,10},{9,11},{10,... | collective-permute-start | bytes 1572872 | tf_op jit(solution)/shard_map/ppermute | solution.py:877
  100.2 23.9 %collective-permute-start.18 = (bf16[256,1024]{1,0:T(8,128)(2,1)S(1)}, bf16[256,1024]{1,0:T(8,128)(2,1)S(1)}, u32[]{:S(2)}, u32[]{:S(2)}) collective-permute-start(bf16[256,1024]{1,0:T(8,128)(2,1)S(1)} %copy-done.3), channel_id=1, source_target_pairs={{0,2},{1,3},{2,0},{3,1},{4,6},{5,7},{6,4},{7,5},{8,10},{9,11},{10,... | collective-permute-start | bytes 1572872 | tf_op jit(solution)/shard_map/ppermute | solution.py:877
  114.5 20.4 %collective-permute-start.15 = (bf16[256,1024]{1,0:T(8,128)(2,1)S(1)}, bf16[256,1024]{1,0:T(8,128)(2,1)S(1)}, u32[]{:S(2)}, u32[]{:S(2)}) collective-permute-start(bf16[256,1024]{1,0:T(8,128)(2,1)S(1)} %multiply_convert_fusion), channel_id=1, source_target_pairs={{0,2},{1,3},{2,0},{3,1},{4,6},{5,7},{6,4},{7,5},{8,10},{9,11},{10,... | collective-permute-start | bytes 1572872 | tf_op jit(solution)/shard_map/ppermute | solution.py:877
  116.6 19.1 %collective-permute-start.17 = (bf16[256,1024]{1,0:T(8,128)(2,1)S(1)}, bf16[256,1024]{1,0:T(8,128)(2,1)S(1)}, u32[]{:S(2)}, u32[]{:S(2)}) collective-permute-start(bf16[256,1024]{1,0:T(8,128)(2,1)S(1)} %copy-done.3), channel_id=1, source_target_pairs={{0,1},{1,0},{2,3},{3,2},{4,5},{5,4},{6,7},{7,6},{8,9},{9,8},{10,11... | collective-permute-start | bytes 1572872 | tf_op jit(solution)/shard_map/ppermute | solution.py:877
  177.1 23.4 %collective-permute-start.22 = (bf16[256,1024]{1,0:T(8,128)(2,1)S(1)}, bf16[256,1024]{1,0:T(8,128)(2,1)S(1)}, u32[]{:S(2)}, u32[]{:S(2)}) collective-permute-start(bf16[256,1024]{1,0:T(8,128)(2,1)S(1)} %add_convert_fusion.3), channel_id=1, source_target_pairs={{0,2},{1,3},{2,0},{3,1},{4,6},{5,7},{6,4},{7,5},{8,10},{9,11},{10,... | collective-permute-start | bytes 1572872 | tf_op jit(solution)/shard_map/ppermute | solution.py:877
  203.7 17.8 %collective-permute-start.26 = (bf16[256,1024]{1,0:T(8,128)(2,1)S(1)}, bf16[256,1024]{1,0:T(8,128)(2,1)}, u32[]{:S(2)}, u32[]{:S(2)}) collective-permute-start(bf16[256,1024]{1,0:T(8,128)(2,1)S(1)} %get-tuple-element.85), channel_id=1, source_target_pairs={{0,1},{1,0},{2,3},{3,2},{4,5},{5,4},{6,7},{7,6},{8,9},{9,8},{10,11... | collective-permute-start | bytes 1572872 | tf_op jit(solution)/shard_map/ppermute | solution.py:877
  216.1 36.4 %collective-permute-start.34 = (bf16[2,128,128]{2,1,0:T(8,128)(2,1)S(1)}, bf16[2,128,128]{2,1,0:T(8,128)(2,1)S(1)}, u32[]{:S(2)}, u32[]{:S(2)}) collective-permute-start(bf16[2,128,128]{2,1,0:T(8,128)(2,1)S(1)} %slice.347), channel_id=1, source_target_pairs={{12,0},{16,4},{20,8},{24,12},{28,16},{13,1},{17,5},{21,9},{25,13},... | collective-permute-start | bytes 196616 | tf_op jit(solution)/shard_map/ppermute | solution.py:900
  217.4 49.6 %collective-permute-start.30 = (bf16[2,128,128]{2,1,0:T(8,128)(2,1)S(1)}, bf16[2,128,128]{2,1,0:T(8,128)(2,1)S(1)}, u32[]{:S(2)}, u32[]{:S(2)}) collective-permute-start(bf16[2,128,128]{2,1,0:T(8,128)(2,1)S(1)} %slice.347), channel_id=1, source_target_pairs={{4,0},{8,4},{12,8},{16,12},{20,16},{24,20},{28,24},{5,1},{9,5},{13... | collective-permute-start | bytes 196616 | tf_op jit(solution)/shard_map/ppermute | solution.py:900
  218.7 48.4 %collective-permute-start.32 = (bf16[2,128,128]{2,1,0:T(8,128)(2,1)S(1)}, bf16[2,128,128]{2,1,0:T(8,128)(2,1)S(1)}, u32[]{:S(2)}, u32[]{:S(2)}) collective-permute-start(bf16[2,128,128]{2,1,0:T(8,128)(2,1)S(1)} %slice.347), channel_id=1, source_target_pairs={{8,0},{12,4},{16,8},{20,12},{24,16},{28,20},{9,1},{13,5},{17,9},{2... | collective-permute-start | bytes 196616 | tf_op jit(solution)/shard_map/ppermute | solution.py:900
  241.8 23.6 %collective-permute-start.35 = (bf16[2,128,256]{2,1,0:T(8,128)(2,1)}, bf16[2,128,256]{2,1,0:T(8,128)(2,1)S(1)}, u32[]{:S(2)}, u32[]{:S(2)}) collective-permute-start(bf16[2,128,256]{2,1,0:T(8,128)(2,1)} %convert_element_type.310), channel_id=1, source_target_pairs={{16,0},{20,4},{24,8},{28,12},{17,1},{21,5},{25,9},{29,13},{18,2},{... | collective-permute-start | bytes 393224 | tf_op jit(solution)/shard_map/ppermute | solution.py:900
  243.1 24.5 %collective-permute-start.31 = (bf16[2,128,256]{2,1,0:T(8,128)(2,1)}, bf16[2,128,256]{2,1,0:T(8,128)(2,1)S(1)}, u32[]{:S(2)}, u32[]{:S(2)}) collective-permute-start(bf16[2,128,256]{2,1,0:T(8,128)(2,1)} %convert_element_type.310), channel_id=1, source_target_pairs={{8,0},{12,4},{16,8},{20,12},{24,16},{28,20},{9,1},{13,5},{17,9},{2... | collective-permute-start | bytes 393224 | tf_op jit(solution)/shard_map/ppermute | solution.py:900
  252.5 20.7 %collective-permute-start.33 = (bf16[2,128,256]{2,1,0:T(8,128)(2,1)}, bf16[2,128,256]{2,1,0:T(8,128)(2,1)}, u32[]{:S(2)}, u32[]{:S(2)}) collective-permute-start(bf16[2,128,256]{2,1,0:T(8,128)(2,1)} %convert_element_type.310), channel_id=1, source_target_pairs={{12,0},{16,4},{20,8},{24,12},{28,16},{13,1},{17,5},{21,9},{25,13},... | collective-permute-start | bytes 393224 | tf_op jit(solution)/shard_map/ppermute | solution.py:900
  267.0 76.9 %collective-permute-start.47 = (bf16[128,1280]{1,0:T(8,128)(2,1)}, bf16[128,1280]{1,0:T(8,128)(2,1)}, u32[]{:S(2)}, u32[]{:S(2)}) collective-permute-start(bf16[128,1280]{1,0:T(8,128)(2,1)} %get-tuple-element.119), channel_id=1, source_target_pairs={{0,1},{1,0},{2,3},{3,2},{4,5},{5,4},{6,7},{7,6},{8,9},{9,8},{10,11... | collective-permute-start | bytes 983048 | tf_op jit(solution)/shard_map/ppermute | solution.py:877
  267.1 96.4 %collective-permute-start.46 = (bf16[128,1280]{1,0:T(8,128)(2,1)}, bf16[128,1280]{1,0:T(8,128)(2,1)}, u32[]{:S(2)}, u32[]{:S(2)}) collective-permute-start(bf16[128,1280]{1,0:T(8,128)(2,1)} %get-tuple-element.118), channel_id=1, source_target_pairs={{0,1},{1,0},{2,3},{3,2},{4,5},{5,4},{6,7},{7,6},{8,9},{9,8},{10,11... | collective-permute-start | bytes 983048 | tf_op jit(solution)/shard_map/ppermute | solution.py:877
  335.6 18.0 %all-to-all-start = ((bf16[8,16,1792]{2,1,0:T(8,128)(2,1)}), bf16[8,16,1792]{2,1,0:T(8,128)(2,1)S(1)}, u32[]{:S(2)}, u32[]{:S(2)}) async-start(bf16[8,16,1792]{2,1,0:T(8,128)(2,1)} %bitcast.25), calls=%async_computation | async-start | bytes 917504 | tf_op jit(solution)/shard_map/all_to_all | solution.py:917
  345.8 17.6 %collective-permute-start.48 = (bf16[128,1280]{1,0:T(8,128)(2,1)}, bf16[128,1280]{1,0:T(8,128)(2,1)}, u32[]{:S(2)}, u32[]{:S(2)}) collective-permute-start(bf16[128,1280]{1,0:T(8,128)(2,1)} %add_convert_fusion.6), channel_id=1, source_target_pairs={{0,2},{1,3},{2,0},{3,1},{4,6},{5,7},{6,4},{7,5},{8,10},{9,11},{10,... | collective-permute-start | bytes 983048 | tf_op jit(solution)/shard_map/ppermute | solution.py:877
  354.4 16.5 %all-to-all-start.1 = ((bf16[8,16,1792]{2,1,0:T(8,128)(2,1)}), bf16[8,16,1792]{2,1,0:T(8,128)(2,1)S(1)}, u32[]{:S(2)}, u32[]{:S(2)}) async-start(bf16[8,16,1792]{2,1,0:T(8,128)(2,1)} %broadcast_in_dim.114), calls=%async_computation.1 | async-start | bytes 917504 | tf_op jit(solution)/shard_map/all_to_all | solution.py:920
  362.9 16.3 %collective-permute-start.37 = (bf16[256,1024]{1,0:T(8,128)(2,1)}, bf16[256,1024]{1,0:T(8,128)(2,1)S(1)}, u32[]{:S(2)}, u32[]{:S(2)}) collective-permute-start(bf16[256,1024]{1,0:T(8,128)(2,1)} %get-tuple-element.89), channel_id=1, source_target_pairs={{0,1},{1,0},{2,3},{3,2},{4,5},{5,4},{6,7},{7,6},{8,9},{9,8},{10,11... | collective-permute-start | bytes 1572872 | tf_op jit(solution)/shard_map/ppermute | solution.py:877
  371.7 31.3 %all-to-all-start.2 = ((bf16[8,16,4416]{2,1,0:T(8,128)(2,1)}), bf16[8,16,4416]{2,1,0:T(8,128)(2,1)S(1)}, u32[]{:S(2)}, u32[]{:S(2)}) async-start(bf16[8,16,4416]{2,1,0:T(8,128)(2,1)} %bitcast.54), calls=%async_computation.2 | async-start | bytes 2293760 | tf_op jit(solution)/shard_map/all_to_all | solution.py:917
  404.3 31.6 %all-to-all-start.3 = ((bf16[8,16,4416]{2,1,0:T(8,128)(2,1)}), bf16[8,16,4416]{2,1,0:T(8,128)(2,1)S(1)}, u32[]{:S(2)}, u32[]{:S(2)}) async-start(bf16[8,16,4416]{2,1,0:T(8,128)(2,1)} %broadcast_in_dim.115), calls=%async_computation.3 | async-start | bytes 2293760 | tf_op jit(solution)/shard_map/all_to_all | solution.py:920
  (56 other events, 547.5 us)
where the time goes:
time: 452 us; the launch traced here: 450 us
  waiting for transfers between devices  161 us (36%)
  Pallas kernels  126 us (28%)
  starting transfers between devices  73.9 us (16%)
  other arithmetic  50 us (11%)
  local copies, waits for them, and re-layouts  35.2 us (8%)
    ppermute x36, waiting for transfers between devices, flip(): return lax.ppermute(array, 'head', [(i, i ^ bit) for i in range(groups)])  94.1 us
    pallas_call x5, Pallas kernels, blocked_call(): pl.pallas_call(body, out_shape=tuple(shapes), grid=(count // block,), in_...  84.4 us
    ppermute x36, starting transfers between devices, flip(): return lax.ppermute(array, 'head', [(i, i ^ bit) for i in range(groups)])  31 us
    all_to_all x2, waiting for transfers between devices, reduce_maps(): total = lax.all_to_all(spread, 'seq', 0, 0).reshape(rows, lanes)  29.5 us
    ppermute x12, waiting for transfers between devices, shifted_along(): return lax.ppermute(array, axis, pairs)  28 us
    ppermute x12, starting transfers between devices, shifted_along(): return lax.ppermute(array, axis, pairs)  24.1 us
    pallas_call x1, Pallas kernels, run_backward(): pl.pallas_call(body, out_shape=shapes, grid_spec=pltpu.PrefetchScalarGrid...  21 us
    pallas_call x1, Pallas kernels, run_forward(): pl.pallas_call(body, out_shape=shapes, grid_spec=pltpu.PrefetchScalarGrid...  20.3 us
  transfers between devices with their start and end apart: 56, of which 24 were waited for; matrix products, arithmetic and copies ran while one was open for 15% of the time, Pallas kernels for 12%

commit v1 on v0

--- a/solution.py
+++ b/solution.py
@@ -143,6 +143,9 @@
     state_ref,
     inverse_ref,
     end_ref,
+    sent_ref,
+    sent_state_ref,
+    sent_map_ref,
     window,
     state,
     *,
@@ -232,7 +235,11 @@
 
     @pl.when(step == pl.num_programs(0) - 1)
     def _():
-        end_ref[...] = state[...]
+        final = state[...]
+        end_ref[...] = final
+        sent_ref[...] = low(final)
+        sent_state_ref[...] = low(final[:, :, :value_width])
+        sent_map_ref[...] = low(final[:, :, value_width:])
 
 
 def backward_kernel(
@@ -249,21 +256,14 @@
     inverse_ref,
     end_ref,
     entering_ref,
-    later_ref,
-    out_ref,
-    mix_ref,
-    tail_ref,
-    edge_ref,
-    window,
-    shifted,
-    shifted_start,
-    cotangent,
-    ahead,
-    *,
+    *rest,
+    hops,
     heads,
     key_width,
     value_width,
 ):
+    got_refs, after_refs, rest = rest[:hops], rest[hops : 2 * hops - 1], rest[2 * hops - 1 :]
+    out_ref, mix_ref, tail_ref, edge_ref, window, shifted, shifted_start, cotangent, ahead = rest
     step = pl.program_id(0)
     steps = pl.num_programs(0)
     wide = value_width + key_width
@@ -278,7 +278,12 @@
         shifted[STEP : STEP + 8, :] = jnp.zeros((8, lanes), single)
         shifted_start[STEP : STEP + 8, :] = jnp.zeros((8, 1), jnp.int32)
         for h in range(heads):
-            cotangent[h] = later_ref[h].astype(single)
+            passed = got_refs[hops - 1][h].astype(single)
+            for hop in range(hops - 1, 0, -1):
+                passed = got_refs[hop - 1][h].astype(single) + tn(
+                    after_refs[hop - 1][h], low(passed)
+                )
+            cotangent[h] = passed
             ahead[h] = end_ref[h, :, :value_width] + nn(
                 low(end_ref[h, :, value_width:]), low(entering_ref[h])
             )
@@ -503,6 +508,9 @@
         jax.ShapeDtypeStruct((count // CHUNK, heads, key_width, wide), bfloat),
         jax.ShapeDtypeStruct((count, heads * CHUNK), bfloat),
         jax.ShapeDtypeStruct((heads, key_width, wide), single),
+        jax.ShapeDtypeStruct((heads, key_width, wide), bfloat),
+        jax.ShapeDtypeStruct((heads, key_width, value_width), bfloat),
+        jax.ShapeDtypeStruct((heads, key_width, key_width), bfloat),
     )
     return pl.pallas_call(
         body,
@@ -524,6 +532,9 @@
                 pl.BlockSpec((chunks, heads, key_width, wide), lambda i, place: (i, 0, 0, 0)),
                 pl.BlockSpec((STEP, heads * CHUNK), at),
                 pl.BlockSpec((heads, key_width, wide), lambda i, place: (0, 0, 0)),
+                pl.BlockSpec((heads, key_width, wide), lambda i, place: (0, 0, 0)),
+                pl.BlockSpec((heads, key_width, value_width), lambda i, place: (0, 0, 0)),
+                pl.BlockSpec((heads, key_width, key_width), lambda i, place: (0, 0, 0)),
             ],
             scratch_shapes=[
                 pltpu.VMEM((STEP + HALO, lanes), single),
@@ -541,8 +552,8 @@
 
 
 def run_backward(
-    place, rows, halo, columns, weights, scalars, grad, saved, entering, later, heads, key_width,
-    value_width, quarter,
+    place, rows, halo, columns, weights, scalars, grad, saved, entering, got, after, heads,
+    key_width, value_width, quarter,
 ):
     written, states, inverses, end = saved
     count, lanes = columns.shape[0], rows.shape[1]
@@ -562,7 +573,11 @@
     fixed = lambda i, place: (0, 0)
     whole = lambda i, place: (0, 0, 0)
     body = functools.partial(
-        backward_kernel, heads=heads, key_width=key_width, value_width=value_width
+        backward_kernel,
+        hops=len(got),
+        heads=heads,
+        key_width=key_width,
+        value_width=value_width,
     )
     shapes = (
         jax.ShapeDtypeStruct((count, lanes), bfloat),
@@ -591,8 +606,8 @@
                 pl.BlockSpec((STEP, heads * CHUNK), at),
                 pl.BlockSpec(end.shape, whole),
                 pl.BlockSpec(entering.shape, whole),
-                pl.BlockSpec(later.shape, whole),
-            ],
+            ]
+            + [pl.BlockSpec(part.shape, whole) for part in (*got, *after)],
             out_specs=[
                 pl.BlockSpec((STEP, lanes), at),
                 pl.BlockSpec((STEP, columns.shape[1]), at),
@@ -616,7 +631,7 @@
         name="delta_backward",
     )(
         place, rows, rows, halo, columns, weights, scalars, grad, written, states, inverses, end,
-        entering, later,
+        entering, *got, *after,
     )
 
 
@@ -634,54 +649,60 @@
 
 
 def accumulate(ref, value, first):
-    @pl.when(first)
-    def _():
-        ref[...] = value
-
-    @pl.when(jnp.logical_not(first))
-    def _():
-        ref[...] += value
+    ref[...] = jnp.where(first, value, ref[...] + value)
+
+
+def at_start(fill):
+    pl.when(pl.program_id(0) == 0)(fill)
 
 
 def project_kernel(
-    rows_ref, table_ref, halo_ref, halo_table_ref, sets_ref, down_ref, wq_ref, wk_ref, wv_ref,
-    wg_ref, wm_ref, up_qk_ref, up_vg_ref,
+    rows_ref, table_ref, halo_ref, halo_table_ref, sets_ref, down_mix_ref, wq_ref, wk_ref, wv_ref,
+    wg_ref, up_qk_ref, up_vg_ref,
     pre_ref, gate_ref, inner_ref, column_ref, pre_halo_ref,
+    joined,
 ):
     low_rank = sets_ref.shape[1]
-    q_width, v_width = wq_ref.shape[1], wv_ref.shape[1]
-
-    def projections(rows, chosen, store):
-        inner = masked(
-            nt(rows, down_ref[: 3 * low_rank, :]), jnp.concatenate([chosen] * 3, axis=1)
-        )
-        store[:, :q_width] = low(
-            nn(rows, wq_ref[...]) + nn(inner[:, :low_rank], up_qk_ref[0])
-        )
-        store[:, q_width : 2 * q_width] = low(
-            nn(rows, wk_ref[...]) + nn(inner[:, low_rank : 2 * low_rank], up_qk_ref[1])
-        )
-        store[:, 2 * q_width :] = low(
-            nn(rows, wv_ref[...]) + nn(inner[:, 2 * low_rank :], up_vg_ref[0])
-        )
-        return inner
-
-    @pl.when(pl.program_id(0) == 0)
+    width, q_width = wq_ref.shape
+    v_width = wv_ref.shape[1]
+    bounds = [0, q_width, 2 * q_width, 2 * q_width + v_width, 2 * q_width + 2 * v_width]
+
+    @at_start
     def _():
-        projections(
-            halo_ref[...], chosen_columns(halo_table_ref[...], sets_ref[...]), pre_halo_ref
-        )
-
-    rows = rows_ref[...]
+        weights = (wq_ref, wk_ref, wv_ref, wg_ref)
+        ups = (up_qk_ref[0], up_qk_ref[1], up_vg_ref[0], up_vg_ref[1])
+        for p in range(4):
+            joined[:width, bounds[p] : bounds[p + 1]] = weights[p][...]
+            joined[width:, bounds[p] : bounds[p + 1]] = ups[p]
+
+    def projections(rows, table, store, last):
+        chosen = chosen_columns(table, sets_ref[...])
+        product = nt(rows, down_mix_ref[...])
+        inner = [
+            masked(product[:, p * low_rank : (p + 1) * low_rank], chosen) for p in range(last)
+        ]
+        outputs = [
+            nn(
+                jnp.concatenate([rows, inner[p]], axis=1), joined[:, bounds[p] : bounds[p + 1]]
+            )
+            for p in range(last)
+        ]
+        for p in range(3):
+            store[:, bounds[p] : bounds[p + 1]] = low(outputs[p])
+        return product, inner, outputs
+
+    @at_start
+    def _():
+        projections(halo_ref[...], halo_table_ref[...], pre_halo_ref, 3)
+
     table = table_ref[...]
-    chosen = chosen_columns(table, sets_ref[...])
-    inner_ref[:, : 3 * low_rank] = projections(rows, chosen, pre_ref)
-    last = masked(nt(rows, down_ref[3 * low_rank :, :]), chosen)
-    inner_ref[:, 3 * low_rank :] = last
-    gate_ref[...] = nn(rows, wg_ref[...]) + nn(last, up_vg_ref[1])
-    mixing = nt(rows, wm_ref[...])
-    spare = column_ref.shape[1] - mixing.shape[1]
-    column_ref[...] = jnp.concatenate([mixing, table[:, :spare]], axis=1)
+    product, inner, outputs = projections(rows_ref[...], table, pre_ref, 4)
+    for p in range(4):
+        inner_ref[:, p * low_rank : (p + 1) * low_rank] = inner[p]
+    gate_ref[...] = outputs[3]
+    column_ref[...] = jnp.concatenate(
+        [product[:, 4 * low_rank : 4 * low_rank + 4], table[:, :4]], axis=1
+    )
 
 
 def head_outputs(raw_ref, map_ref, entering_ref, heads, key_width, value_width):
@@ -695,181 +716,385 @@
 
 
 def attend_kernel(
-    raw_ref, map_ref, gate_ref, table_ref, entering_ref, gain_ref, sets_ref, wo_ref, down_ref,
-    up_ref,
-    part_ref, z_ref, inner_ref,
-    *, heads, key_width, value_width,
+    raw_ref, map_ref, gate_ref, table_ref, gain_ref, sets_ref, wo_ref, down_ref, up_ref, *rest,
+    heads, key_width, value_width, hops,
 ):
+    got_refs, rest = rest[:hops], rest[hops:]
+    part_ref, z_ref, inner_ref, entering_ref, joined = rest
+    value_lanes = wo_ref.shape[0]
+
+    @at_start
+    def _():
+        joined[:value_lanes, :] = wo_ref[...]
+        joined[value_lanes:, :] = up_ref[...]
+        for h in range(heads):
+            state = got_refs[hops - 1][h].astype(single)
+            for hop in range(hops - 1, 0, -1):
+                got = got_refs[hop - 1][h]
+                state = got[:, :value_width].astype(single) + nn(got[:, value_width:], low(state))
+            entering_ref[h] = low(state)
+
     chosen = chosen_columns(table_ref[...], sets_ref[...])
     outputs = head_outputs(raw_ref, map_ref, entering_ref, heads, key_width, value_width)
+    parts = []
     for h, output in enumerate(outputs):
         lanes = slice(h * value_width, (h + 1) * value_width)
         scale = lax.rsqrt(jnp.mean(output * output, axis=-1, keepdims=True) + EPS)
         _, gate = silu_parts(gate_ref[:, lanes])
-        z_ref[:, lanes] = low(output * scale * gain_ref[0:1, :] * gate)
-    z = z_ref[...]
+        parts.append(low(output * scale * gain_ref[0:1, :] * gate))
+    z = jnp.concatenate(parts, axis=1)
+    z_ref[...] = z
     inner = masked(nt(z, down_ref[...]), chosen)
     inner_ref[...] = inner
-    part_ref[...] = low(nn(z, wo_ref[...]) + nn(inner, up_ref[...]))
+    part_ref[...] = low(nn(jnp.concatenate([z, inner], axis=1), joined[...]))
+
+
+def feed_before_kernel(
+    grad_ref, table_ref, sets_ref, wd_ref, down_ffd_t_ref, up_ref, hidden_grad_ref, du_ref, joined
+):
+    hidden, width = wd_ref.shape
+
+    @at_start
+    def _():
+        joined[:hidden, :width] = wd_ref[...]
+        joined[:hidden, width:] = down_ffd_t_ref[...]
+        joined[hidden:, :] = jnp.zeros((joined.shape[0] - hidden, joined.shape[1]), bfloat)
+
+    grad = grad_ref[...]
+    du_down = masked(nt(grad, up_ref[...]), chosen_columns(table_ref[...], sets_ref[...]))
+    du_ref[...] = du_down
+    hidden_grad_ref[...] = nt(jnp.concatenate([grad, du_down], axis=1), joined[...])
 
 
 def feed_kernel(
-    rows_ref, grad_ref, table_ref, sets_ref, down_ref, wg_ref, wu_ref, wd_ref, up_ff_ref,
-    down_ffd_ref, up_ref,
-    out_ref, back_ref, down_grad_ref, res_grad_ref, up_grad_ref, ffd_grad_ref,
+    rows_ref, hidden_grad_ref, table_ref, sets_ref, down_ref, wg_ref, wu_ref, up_t_ref, up_ref,
+    back_ref, hidden_ref, ff_grad_ref, inner_ref, du_ref,
+    joined_gate, joined_up, joined_back,
+):
+    low_rank = sets_ref.shape[1]
+    hidden, width = wg_ref.shape
+    padded = joined_gate.shape[0]
+
+    @at_start
+    def _():
+        for p, (joined, weight) in enumerate(((joined_gate, wg_ref), (joined_up, wu_ref))):
+            joined[:hidden, :width] = weight[...]
+            joined[:hidden, width:] = up_t_ref[p]
+            joined[hidden:, :] = jnp.zeros((padded - hidden, joined.shape[1]), bfloat)
+            joined_back[p * padded : p * padded + hidden, :] = weight[...]
+            joined_back[p * padded + hidden : (p + 1) * padded, :] = jnp.zeros(
+                (padded - hidden, width), bfloat
+            )
+        joined_back[2 * padded :, :] = down_ref[...]
+
+    chosen = chosen_columns(table_ref[...], sets_ref[...])
+    both = jnp.concatenate([chosen, chosen], axis=1)
+    rows = rows_ref[...]
+    inner = masked(nt(rows, down_ref[...]), both)
+    inner_ref[...] = inner
+    gate = nt(jnp.concatenate([rows, inner[:, :low_rank]], axis=1), joined_gate[...])
+    up = nt(jnp.concatenate([rows, inner[:, low_rank:]], axis=1), joined_up[...])
+    logistic, active = silu_parts(gate)
+    hidden_ref[...] = low(active * up)
+    hidden_grad = hidden_grad_ref[...]
+    gate_grad = low(hidden_grad * up * logistic * (1.0 + gate * (1.0 - logistic)))
+    up_grad = low(hidden_grad * active)
+    du_gate = masked(nt(gate_grad, up_ref[0]), chosen)
+    du_up = masked(nt(up_grad, up_ref[1]), chosen)
+    du_ref[:, :low_rank] = du_gate
+    du_ref[:, low_rank:] = du_up
+    ff_grad_ref[:, :padded] = gate_grad
+    ff_grad_ref[:, padded:] = up_grad
+    back_ref[...] = low(
+        nn(jnp.concatenate([gate_grad, up_grad, du_gate, du_up], axis=1), joined_back[...])
+    )
+
+
+def feed_after_kernel(
+    rows_ref, grad_ref, hidden_ref, ff_grad_ref, inner_ref, du_ref, du_down_ref, table_ref,
+    sets_ref, wd_ref, down_ffd_ref, up_ref,
+    out_ref, down_grad_ref, res_grad_ref, up_grad_ref, ffd_grad_ref,
+    joined,
 ):
     first = pl.program_id(0) == 0
     low_rank = sets_ref.shape[1]
-    chosen = chosen_columns(table_ref[...], sets_ref[...])
-    rows, grad = rows_ref[...], grad_ref[...]
-    u_gate = masked(nt(rows, down_ref[:low_rank, :]), chosen)
-    u_up = masked(nt(rows, down_ref[low_rank:, :]), chosen)
-    gate = nt(rows, wg_ref[...]) + nn(u_gate, up_ff_ref[0])
-    up = nt(rows, wu_ref[...]) + nn(u_up, up_ff_ref[1])
-    logistic, active = silu_parts(gate)
-    hidden = low(active * up)
-    u_down = masked(nt(hidden, down_ffd_ref[...]), chosen)
-    out_ref[...] = low(nn(hidden, wd_ref[...]) + nn(u_down, up_ref[...]))
-    du_down = masked(nt(grad, up_ref[...]), chosen)
-    hidden_grad = nt(grad, wd_ref[...]) + nn(du_down, down_ffd_ref[...])
-    gate_grad = low(hidden_grad * up * logistic * (1.0 + gate * (1.0 - logistic)))
-    up_grad = low(hidden_grad * active)
-    du_gate = masked(nt(gate_grad, up_ff_ref[0]), chosen)
-    du_up = masked(nt(up_grad, up_ff_ref[1]), chosen)
-    back_ref[...] = low(
-        nn(gate_grad, wg_ref[...])
-        + nn(up_grad, wu_ref[...])
-        + nn(du_gate, down_ref[:low_rank, :])
-        + nn(du_up, down_ref[low_rank:, :])
-    )
-    accumulate(down_grad_ref.at[0], tn(du_gate, rows), first)
-    accumulate(down_grad_ref.at[1], tn(du_up, rows), first)
-    accumulate(res_grad_ref, tn(u_down, grad), first)
-    accumulate(up_grad_ref.at[0], tn(u_gate, gate_grad), first)
-    accumulate(up_grad_ref.at[1], tn(u_up, up_grad), first)
-    accumulate(ffd_grad_ref, tn(du_down, hidden), first)
+    width_hidden = wd_ref.shape[0]
+    padded = down_ffd_ref.shape[1]
+
+    @at_start
+    def _():
+        joined[:width_hidden, :] = wd_ref[...]
+        joined[width_hidden:padded, :] = jnp.zeros(
+            (padded - width_hidden, joined.shape[1]), bfloat
+        )
+        joined[padded:, :] = up_ref[...]
+
+    hidden = hidden_ref[...]
+    inner = inner_ref[...]
+    u_down = masked(
+        nt(hidden, down_ffd_ref[...]), chosen_columns(table_ref[...], sets_ref[...])
+    )
+    out_ref[...] = low(nn(jnp.concatenate([hidden, u_down], axis=1), joined[...]))
+    accumulate(down_grad_ref, tn(du_ref[...], rows_ref[...]), first)
+    accumulate(res_grad_ref, tn(u_down, grad_ref[...]), first)
+    accumulate(up_grad_ref.at[0], tn(inner[:, :low_rank], ff_grad_ref[:, :padded]), first)
+    accumulate(up_grad_ref.at[1], tn(inner[:, low_rank:], ff_grad_ref[:, padded:]), first)
+    accumulate(ffd_grad_ref, tn(du_down_ref[...], hidden), first)
 
 
 def branch_kernel(
-    branch_ref, raw_ref, map_ref, gate_ref, z_ref, u_out_ref, rows_ref, inner_ref, table_ref,
-    entering_ref, gain_ref, sets_ref, wo_ref, down_out_ref, up_ref, up_vg_ref,
-    raw_grad_ref, gate_grad_ref, du_ref, state_grad_ref, res_grad_ref, out_grad_ref,
-    up_grad_ref, down_grad_ref,
+    branch_ref, raw_ref, map_ref, gate_ref, table_ref, entering_ref, gain_ref, sets_ref, wo_ref,
+    down_out_t_ref, up_ref, up_gate_ref,
+    raw_grad_ref, gate_grad_ref, du_out_ref, du_gate_ref, state_grad_ref,
+    joined, total,
     *, heads, key_width, value_width,
 ):
     first = pl.program_id(0) == 0
-    low_rank = sets_ref.shape[1]
+    width = wo_ref.shape[1]
+
+    @at_start
+    def _():
+        joined[:, :width] = wo_ref[...]
+        joined[:, width:] = down_out_t_ref[...]
+
     chosen = chosen_columns(table_ref[...], sets_ref[...])
     branch = branch_ref[...]
     outputs = head_outputs(raw_ref, map_ref, entering_ref, heads, key_width, value_width)
     du_out = masked(nt(branch, up_ref[...]), chosen)
-    mixed_grad = nt(branch, wo_ref[...]) + nn(du_out, down_out_ref[...])
+    du_out_ref[...] = du_out
+    mixed_grad = nt(jnp.concatenate([branch, du_out], axis=1), joined[...])
     gain = gain_ref[0:1, :]
+    gate_grads = []
     for h, output in enumerate(outputs):
         lanes = slice(h * value_width, (h + 1) * value_width)
         scale = lax.rsqrt(jnp.mean(output * output, axis=-1, keepdims=True) + EPS)
         value = gate_ref[:, lanes]
         logistic, active = silu_parts(value)
         incoming = mixed_grad[:, lanes]
-        gate_grad_ref[:, lanes] = low(
-            incoming
-            * (output * scale * gain)
-            * (logistic * (1.0 + value * (1.0 - logistic)))
+        gate_grads.append(
+            low(
+                incoming
+                * (output * scale * gain)
+                * (logistic * (1.0 + value * (1.0 - logistic)))
+            )
         )
         scaled = gain * (incoming * active)
         dot = jnp.mean(output * scaled, axis=-1, keepdims=True)
         raw_grad = low(scale * scaled - output * (scale * scale * scale * dot))
         raw_grad_ref[:, lanes] = raw_grad
         accumulate(
-            state_grad_ref.at[h],
-            tn(map_ref[:, h * key_width : (h + 1) * key_width], raw_grad),
-            first,
+            total.at[h], tn(map_ref[:, h * key_width : (h + 1) * key_width], raw_grad), first
         )
-    gate_grad = gate_grad_ref[...]
-    du_gate = masked(nt(gate_grad, up_vg_ref[1]), chosen)
-    du_ref[...] = du_gate
-    accumulate(res_grad_ref, tn(u_out_ref[...], branch), first)
-    accumulate(out_grad_ref, tn(du_out, z_ref[...]), first)
-    accumulate(up_grad_ref, tn(inner_ref[...], gate_grad), first)
-    accumulate(down_grad_ref, tn(du_gate, rows_ref[...]), first)
-
-
-def settle_kernel(
-    pre_ref, gate_grad_ref, du_gate_ref, mix_ref, rows_ref, inner_ref, table_ref, sets_ref,
-    down_ref, wq_ref, wk_ref, wv_ref, wg_ref, wm_ref, up_qk_ref, up_vg_ref,
-    part_ref, down_grad_ref, up_qk_grad_ref, up_v_grad_ref,
+    gate_grad = jnp.concatenate(gate_grads, axis=1)
+    gate_grad_ref[...] = gate_grad
+    du_gate_ref[...] = masked(nt(gate_grad, up_gate_ref[...]), chosen)
+
+    @pl.when(pl.program_id(0) == pl.num_programs(0) - 1)
+    def _():
+        state_grad_ref[...] = low(total[...])
+
+
+def branch_after_kernel(
+    branch_ref, z_ref, u_out_ref, rows_ref, inner_ref, du_out_ref, du_gate_ref, gate_grad_ref,
+    down_grad_ref, res_grad_ref, out_grad_ref, up_grad_ref,
+):
+    first = pl.program_id(0) == 0
+    accumulate(down_grad_ref, tn(du_gate_ref[...], rows_ref[...]), first)
+    accumulate(res_grad_ref, tn(u_out_ref[...], branch_ref[...]), first)
+    accumulate(out_grad_ref, tn(du_out_ref[...], z_ref[...]), first)
+    accumulate(up_grad_ref, tn(inner_ref[...], gate_grad_ref[...]), first)
+
+
+def settled_rows(pre_ref, tail_ref, arrived_ref, place_ref, quarters, window):
+    per_quarter = pl.num_programs(0) // quarters
+    last = ((quarters - 1) ^ place_ref[0]) * per_quarter + per_quarter - 1
+    window[...] = pre_ref[...]
+
+    @pl.when(pl.program_id(0) == last)
+    def _():
+        window[window.shape[0] - HALO :, :] = low(tail_ref[...] + arrived_ref[...])
+
+    return window[...]
+
+
+def settle_grads_kernel(
+    pre_ref, rows_ref, inner_ref, table_ref, tail_ref, arrived_ref, place_ref, sets_ref,
+    up_qk_ref, up_value_ref,
+    du_ref, down_grad_ref, up_qk_grad_ref, up_v_grad_ref,
+    window,
 ):
     first = pl.program_id(0) == 0
     low_rank = sets_ref.shape[1]
-    q_width = wq_ref.shape[1]
+    q_width = up_qk_ref.shape[2]
     chosen = chosen_columns(table_ref[...], sets_ref[...])
-    query, key = pre_ref[:, :q_width], pre_ref[:, q_width : 2 * q_width]
-    value = pre_ref[:, 2 * q_width :]
-    rows = rows_ref[...]
+    pre = settled_rows(pre_ref, tail_ref, arrived_ref, place_ref, 4, window)
+    query, key, value = pre[:, :q_width], pre[:, q_width : 2 * q_width], pre[:, 2 * q_width :]
+    inner = inner_ref[...]
     du = jnp.concatenate(
         [
             masked(nt(query, up_qk_ref[0]), chosen),
             masked(nt(key, up_qk_ref[1]), chosen),
-            masked(nt(value, up_vg_ref[0]), chosen),
-            du_gate_ref[...],
+            masked(nt(value, up_value_ref[...]), chosen),
         ],
         axis=1,
     )
+    du_ref[...] = du
+    accumulate(down_grad_ref, tn(du, rows_ref[...]), first)
+    accumulate(up_qk_grad_ref.at[0], tn(inner[:, :low_rank], query), first)
+    accumulate(up_qk_grad_ref.at[1], tn(inner[:, low_rank : 2 * low_rank], key), first)
+    accumulate(up_v_grad_ref, tn(inner[:, 2 * low_rank : 3 * low_rank], value), first)
+
+
+def settle_kernel(
+    pre_ref, gate_grad_ref, du_ref, du_gate_ref, mix_ref, tail_ref, arrived_ref, place_ref,
+    down_mix_ref, wq_ref, wk_ref, wv_ref, wg_ref,
+    part_ref,
+    window, joined,
+):
+    q_width, v_width = wq_ref.shape[1], wv_ref.shape[1]
+
+    @at_start
+    def _():
+        joined[:, :q_width] = wq_ref[...]
+        joined[:, q_width : 2 * q_width] = wk_ref[...]
+        joined[:, 2 * q_width : 2 * q_width + v_width] = wv_ref[...]
+        joined[:, 2 * q_width + v_width :] = wg_ref[...]
+
+    pre = settled_rows(pre_ref, tail_ref, arrived_ref, place_ref, 4, window)
+    mix = low(mix_ref[...])
+    spare = down_mix_ref.shape[0] - du_ref.shape[1] - du_gate_ref.shape[1] - mix.shape[1]
+    small = jnp.concatenate(
+        [du_ref[...], du_gate_ref[...], mix, jnp.zeros((mix.shape[0], spare), bfloat)], axis=1
+    )
     part_ref[...] = low(
-        nt(query, wq_ref[...])
-        + nt(key, wk_ref[...])
-        + nt(value, wv_ref[...])
-        + nt(gate_grad_ref[...], wg_ref[...])
-        + nn(du, down_ref[...])
-        + nn(low(mix_ref[...]), wm_ref[...])
-    )
-    accumulate(down_grad_ref, tn(du[:, : 3 * low_rank], rows), first)
-    accumulate(up_qk_grad_ref.at[0], tn(inner_ref[:, :low_rank], query), first)
-    accumulate(up_qk_grad_ref.at[1], tn(inner_ref[:, low_rank : 2 * low_rank], key), first)
-    accumulate(up_v_grad_ref, tn(inner_ref[:, 2 * low_rank : 3 * low_rank], value), first)
+        nt(jnp.concatenate([pre, gate_grad_ref[...]], axis=1), joined[...])
+        + nn(small, down_mix_ref[...])
+    )
+
+
+WHOLE, SCALAR = "whole", "scalar"
 
 
 def by_rows(width, lane_block=0):
     return ("rows", width, lane_block)
 
 
-def blocked_call(body, name, count, inputs, outputs, flops):
-    block = min(STEP, count)
-    in_specs, arrays, moved = [], [], 0
+def pieces(width):
+    return ("pieces", width)
+
+
+def blocked_call(body, name, count, inputs, outputs, scratch, flops, block=STEP):
+    steps = count // block
+    per = max(steps // 4, 1)
+    in_specs, arrays, moved, groups_in, extra = [], [], 0, [], []
     for array, kind in inputs:
-        arrays.append(array)
-        moved += array.size * array.dtype.itemsize
-        if kind is None:
+        members = array if isinstance(array, (list, tuple)) else [array]
+        groups_in.append(len(members))
+        arrays += members
+        moved += sum(a.size * a.dtype.itemsize for a in members)
+        if kind == WHOLE:
             zeros = (0,) * array.ndim
             in_specs.append(
                 pl.BlockSpec(
                     array.shape, lambda i, zeros=zeros: zeros, pipeline_mode=pl.Buffered(1)
                 )
             )
-        else:
+        elif kind == SCALAR:
+            in_specs.append(pl.BlockSpec(memory_space=pltpu.SMEM))
+        elif kind[0] == "rows":
             in_specs.append(
                 pl.BlockSpec((block, kind[1]), lambda i, lane=kind[2]: (i, lane))
             )
-    out_specs, shapes = [], []
-    for shape, dtype, rowwise in outputs:
-        shapes.append(jax.ShapeDtypeStruct(shape, dtype))
-        if rowwise:
-            out_specs.append(pl.BlockSpec((block, shape[1]), lambda i: (i, 0)))
         else:
-            zeros = (0,) * len(shape)
-            out_specs.append(pl.BlockSpec(shape, lambda i, zeros=zeros: zeros))
-    return pl.pallas_call(
-        body,
+            for b in range(4):
+                in_specs.append(
+                    pl.BlockSpec(
+                        (block, kind[1]), lambda i, b=b: (jnp.clip(i - b * per, 0, per - 1), 0)
+                    )
+                )
+            extra.append(pltpu.VMEM((block, kind[1]), members[0].dtype))
+    out_specs, shapes, groups_out = [], [], []
+    for shape, dtype, kind in outputs:
+        if kind == "parts":
+            quarter = shape[0] // 4
+            for rows in (quarter, quarter, 2 * quarter):
+                shapes.append(jax.ShapeDtypeStruct((rows, shape[1]), dtype))
+            spec = (block, shape[1])
+            out_specs += [
+                pl.BlockSpec(spec, lambda i: (jnp.clip(i, 0, per - 1), 0)),
+                pl.BlockSpec(spec, lambda i: (jnp.clip(i - 2 * per, 0, per - 1), 0)),
+                pl.BlockSpec(
+                    spec,
+                    lambda i: (
+                        jnp.clip(i - per, 0, per - 1) + jnp.clip(i - 3 * per + 1, 0, per), 0
+                    ),
+                ),
+            ]
+            groups_out.append(3)
+            extra.append(pltpu.VMEM(spec, dtype))
+        else:
+            groups_out.append(1)
+            shapes.append(jax.ShapeDtypeStruct(shape, dtype))
+            if kind == "rows":
+                out_specs.append(pl.BlockSpec((block, shape[1]), lambda i: (i, 0)))
+            else:
+                zeros = (0,) * len(shape)
+                out_specs.append(pl.BlockSpec(shape, lambda i, zeros=zeros: zeros))
+
+    def wrapped(*refs):
+        refs = list(refs)
+        spare = refs[len(in_specs) + len(out_specs) + len(scratch) :]
+        own_scratch = refs[len(in_specs) + len(out_specs) : len(refs) - len(spare)]
+        quarter = pl.program_id(0) // per
+        given, later, at, used = [], [], 0, 0
+        for size in groups_in:
+            if size == 1:
+                given.append(refs[at])
+            else:
+                held = spare[used]
+                used += 1
+                for b in range(size):
+
+                    @pl.when(quarter == b)
+                    def _(held=held, source=refs[at + b]):
+                        held[...] = source[...]
+
+                given.append(held)
+            at += size
+        for size in groups_out:
+            if size == 1:
+                given.append(refs[at])
+            else:
+                given.append(spare[used])
+                later.append((spare[used], refs[at : at + size]))
+                used += 1
+            at += size
+        body(*given, *own_scratch)
+        for held, targets in later:
+            for b, target in ((0, targets[0]), (2, targets[1]), (1, targets[2]), (3, targets[2])):
+
+                @pl.when(quarter == b)
+                def _(held=held, target=target):
+                    target[...] = held[...]
+
+    results = pl.pallas_call(
+        wrapped,
         out_shape=tuple(shapes),
-        grid=(count // block,),
+        grid=(steps,),
         in_specs=in_specs,
         out_specs=out_specs,
+        scratch_shapes=list(scratch) + extra,
         compiler_params=pltpu.CompilerParams(
             dimension_semantics=("arbitrary",), vmem_limit_bytes=VMEM_LIMIT
         ),
         cost_estimate=pl.CostEstimate(flops=flops, bytes_accessed=moved, transcendentals=0),
         name=name,
     )(*arrays)
+    grouped, at = [], 0
+    for size in groups_out:
+        grouped.append(results[at] if size == 1 else results[at : at + size])
+        at += size
+    return grouped
 
 
 def flip(array, bit):
@@ -880,18 +1105,25 @@
 def gather_rows(array):
     far = flip(array, 2)
     near = flip(array, 1)
-    return jnp.concatenate([array, near, far, flip(far, 1)], axis=0)
-
-
-def scatter_sum(blocks):
-    near, corner = flip(low(blocks[1]), 1), flip(low(blocks[3]), 1)
-    far = blocks[2].astype(single) + corner.astype(single)
-    return blocks[0].astype(single) + near.astype(single) + flip(low(far), 2).astype(single)
-
-
-def scatter_rows(partial):
-    size = partial.shape[0] // 4
-    return scatter_sum([partial[b * size : (b + 1) * size] for b in range(4)])
+    return [array, near, far, flip(far, 1)]
+
+
+def tie(*arrays):
+    return lax.optimization_barrier(arrays)
+
+
+def near_sum(parts):
+    own, far, pair = parts
+    size = own.shape[0]
+    arrived = flip(pair, 1)
+    return (
+        own.astype(single) + arrived[:size].astype(single),
+        low(far.astype(single) + arrived[size:].astype(single)),
+    )
+
+
+def far_sum(own, far):
+    return own + flip(far, 2).astype(single)
 
 
 def shifted_along(array, axis, by):
@@ -900,42 +1132,46 @@
     return lax.ppermute(array, axis, pairs)
 
 
-def reduce_maps(shared, owned):
+def head_blocks(parts):
+    place = lax.axis_index("head")
+
+    def block(relative):
+        blocks = []
+        for part in parts:
+            size = part.shape[1] // 4
+            blocks.append(
+                low(lax.dynamic_slice_in_dim(part, (place ^ relative) * size, size, 1))
+            )
+        return jnp.concatenate(blocks, axis=1)
+
+    return block(0), block(2), jnp.concatenate([block(1), block(3)], axis=0)
+
+
+def seq_parts(flat):
     members = lax.axis_size("seq")
+    rows, lanes = flat.shape
+    return lax.all_to_all(flat.reshape(members, rows // members, lanes), "seq", 0, 0)
+
+
+def seq_spread(parts):
+    members, rows, lanes = parts.shape
+    summed = low(jnp.sum(parts.astype(single), axis=0))
+    spread = jnp.broadcast_to(summed[None], parts.shape)
+    return lax.all_to_all(spread, "seq", 0, 0).reshape(members * rows, lanes)
+
+
+def head_spread(piece, count):
     place = lax.axis_index("head")
-    widths = [part.shape[1] // 4 for part in shared]
-
-    def block(part, relative):
-        size = part.shape[1] // 4
-        return lax.dynamic_slice_in_dim(part, (place ^ relative) * size, size, 1)
-
-    mine = scatter_sum(
-        [jnp.concatenate([block(part, b) for part in shared], axis=1) for b in range(4)]
-    )
-    flat = jnp.concatenate([low(mine)] + [low(part) for part in owned], axis=1)
-    rows, lanes = flat.shape
-    parts = lax.all_to_all(flat.reshape(members, rows // members, lanes), "seq", 0, 0)
-    summed = low(jnp.sum(parts.astype(single), axis=0))
-    spread = jnp.broadcast_to(summed[None], (members,) + summed.shape)
-    total = lax.all_to_all(spread, "seq", 0, 0).reshape(rows, lanes)
-    shared_lanes = sum(widths)
-    piece = total[:, :shared_lanes]
     far = flip(piece, 2)
-    pieces = jnp.stack([piece, flip(piece, 1), far, flip(far, 1)])
-    ordered = [lax.dynamic_index_in_dim(pieces, place ^ b, 0, False) for b in range(4)]
-    full, at = [], 0
-    for width in widths:
-        full.append(
-            jnp.concatenate(
-                [ordered[b][:, at : at + width].astype(single) for b in range(4)], axis=1
-            )
+    blocks = jnp.stack([piece, flip(piece, 1), far, flip(far, 1)])
+    ordered = [lax.dynamic_index_in_dim(blocks, place ^ b, 0, False) for b in range(4)]
+    size = piece.shape[1] // count
+    return [
+        jnp.concatenate(
+            [o[:, k * size : (k + 1) * size].astype(single) for o in ordered], axis=1
         )
-        at += width
-    local, at = [], shared_lanes
-    for part in owned:
-        local.append(total[:, at : at + part.shape[1]].astype(single))
-        at += part.shape[1]
-    return full, local
+        for k in range(count)
+    ]
 
 
 def rms_scale(rows, gain):
@@ -1028,11 +1264,20 @@
     conv = jnp.concatenate([conv_query, conv_key, conv_value], axis=1).astype(single)
     scalars = jnp.stack([decay_rate, decay_bias])
     where = place.reshape(1).astype(jnp.int32)
-    weight_mix = w_decay_beta.transpose(1, 2, 0).reshape(2 * heads, width)
-    weight_mix_padded = jnp.pad(weight_mix, ((0, 8 - 2 * heads), (0, 0)))
+    down_mix = jnp.concatenate(
+        [
+            mixer_down,
+            w_decay_beta.transpose(1, 2, 0).reshape(2 * heads, width),
+            jnp.zeros((low_rank - 2 * heads, width), bfloat),
+        ],
+        axis=0,
+    )
     gain = jnp.broadcast_to(out_gain[None, :], (8, value_width))
     hidden_width = w_down.shape[0]
+    padded = -(-hidden_width // 256) * 256
     value_lanes = heads * value_width
+    widen = lambda a: jnp.pad(a, [(0, 0)] * (a.ndim - 1) + [(0, padded - hidden_width)])
+    up_ff_padded, down_ffd_padded = widen(up_ff), widen(down_ffd)
 
     input_float = block_input.astype(single)
     normed = low(rms_scale(input_float, norm1_gain))
@@ -1046,62 +1291,65 @@
         for h in range(groups)
     )
     normed_all = gather_rows(normed)
-    grad_all = gather_rows(out_grad)
     pre, gate_input, inner, columns, pre_halo = blocked_call(
         project_kernel,
         "project",
         count,
         [
-            (normed_all, by_rows(width)),
+            (normed_all, pieces(width)),
             (table, by_rows(8)),
-            (halo, None),
-            (halo_table, None),
-            (column_sets, None),
-            (mixer_down, None),
-            (w_query, None),
-            (w_key, None),
-            (w_value, None),
-            (w_gate_out, None),
-            (weight_mix, None),
-            (up_qk, None),
-            (up_vg, None),
-        ],
-        [
-            ((count, 2 * qk + value_lanes), bfloat, True),
-            ((count, value_lanes), single, True),
-            ((count, 4 * low_rank), bfloat, True),
-            ((count, 8), single, True),
-            ((HALO, 2 * qk + value_lanes), bfloat, False),
-        ],
-        count * 5_000_000,
-    )
-    raw_local, mapped, *saved = run_forward(
+            (halo, WHOLE),
+            (halo_table, WHOLE),
+            (column_sets, WHOLE),
+            (down_mix, WHOLE),
+            (w_query, WHOLE),
+            (w_key, WHOLE),
+            (w_value, WHOLE),
+            (w_gate_out, WHOLE),
+            (up_qk, WHOLE),
+            (up_vg, WHOLE),
+        ],
+        [
+            ((count, 2 * qk + value_lanes), bfloat, "rows"),
+            ((count, value_lanes), single, "rows"),
+            ((count, 4 * low_rank), bfloat, "rows"),
+            ((count, 8), single, "rows"),
+            ((HALO, 2 * qk + value_lanes), bfloat, "whole"),
+        ],
+        [pltpu.VMEM((width + low_rank, 2 * qk + 2 * value_lanes), bfloat)],
+        count * 9_000_000,
+    )
+    out_grad_late, pre = tie(out_grad, pre)
+    grad_all = gather_rows(out_grad_late)
+    raw_local, mapped, *saved, sent, sent_state, sent_map = run_forward(
         where, pre, pre_halo, columns, conv, scalars, heads, key_width, value_width, quarter
     )
-    end = saved[-1]
 
     hops = min(members - 1, -(-(DOC_MAX - 1) // count))
-    end_low = low(end)
-    entering = None
-    for hop in range(hops, 0, -1):
-        if entering is None:
-            entering = shifted_along(end_low[:, :, :value_width], "seq", hop).astype(single)
-        else:
-            got = shifted_along(end_low, "seq", hop)
-            entering = got[:, :, :value_width].astype(single) + jnp.einsum(
-                "hij,hjk->hik",
-                got[:, :, value_width:],
-                low(entering),
-                preferred_element_type=single,
-            )
-    maps_after = [
-        shifted_along(end_low[:, :, value_width:], "seq", -hop) for hop in range(1, hops)
-    ]
-    entering_low = low(entering)
+    got = [shifted_along(sent, "seq", hop) for hop in range(1, hops)]
+    got.append(shifted_along(sent_state, "seq", hops))
+    *grad_all, sent_map = tie(*grad_all, sent_map)
+    hidden_grad, du_down = blocked_call(
+        feed_before_kernel,
+        "feed_before",
+        count,
+        [
+            (grad_all, pieces(width)),
+            (table, by_rows(8)),
+            (column_sets, WHOLE),
+            (w_down, WHOLE),
+            (down_ffd.T, WHOLE),
+            (up_res[1], WHOLE),
+        ],
+        [((count, padded), single, "rows"), ((count, low_rank), bfloat, "rows")],
+        [pltpu.VMEM((padded, width + low_rank), bfloat)],
+        count * 6_000_000,
+    )
+    raw_local, hidden_grad = tie(raw_local, hidden_grad)
 
     sizes = dict(heads=heads, key_width=key_width, value_width=value_width)
-    attention_part, mixed, u_out = blocked_call(
-        functools.partial(attend_kernel, **sizes),
+    attention_part, mixed, u_out, entering = blocked_call(
+        functools.partial(attend_kernel, hops=hops, **sizes),
         "attend",
         count,
         [
@@ -1109,158 +1357,277 @@
             (mapped, by_rows(qk)),
             (gate_input, by_rows(value_lanes)),
             (table, by_rows(8)),
-            (entering_low, None),
-            (gain, None),
-            (column_sets, None),
-            (w_out, None),
-            (down_out, None),
-            (up_res[0], None),
-        ],
-        [
-            ((count, width), bfloat, True),
-            ((count, value_lanes), bfloat, True),
-            ((count, low_rank), bfloat, True),
-        ],
-        count * 1_600_000,
-    )
-    residual = input_float + scatter_rows(attention_part)
+            (gain, WHOLE),
+            (column_sets, WHOLE),
+            (w_out, WHOLE),
+            (down_out, WHOLE),
+            (up_res[0], WHOLE),
+        ]
+        + [(part, WHOLE) for part in got],
+        [
+            ((count, width), bfloat, "parts"),
+            ((count, value_lanes), bfloat, "rows"),
+            ((count, low_rank), bfloat, "rows"),
+            ((heads, key_width, value_width), bfloat, "whole"),
+        ],
+        [pltpu.VMEM((value_lanes + low_rank, width), bfloat)],
+        count * 5_000_000,
+    )
+    residual = input_float + far_sum(*near_sum(attention_part))
     normed_mid = low(rms_scale(residual, norm2_gain))
     mid_all = gather_rows(normed_mid)
-
-    out_part, mid_part, feed_down_grad, feed_res_grad, feed_up_grad, ffd_grad = blocked_call(
+    normed_mid_done, sent_map = tie(mid_all[3], sent_map)
+    mid_all = mid_all[:3] + [normed_mid_done]
+
+    mid_part, hidden, ff_grad, u_ff, du_ff = blocked_call(
         feed_kernel,
         "feed",
         count,
         [
-            (mid_all, by_rows(width)),
-            (grad_all, by_rows(width)),
+            (mid_all, pieces(width)),
+            (hidden_grad, by_rows(padded)),
             (table, by_rows(8)),
-            (column_sets, None),
-            (feed_down, None),
-            (w_gate.T, None),
-            (w_up.T, None),
-            (w_down, None),
-            (up_ff, None),
-            (down_ffd, None),
-            (up_res[1], None),
-        ],
-        [
-            ((count, width), bfloat, True),
-            ((count, width), bfloat, True),
-            ((2, low_rank, width), single, False),
-            ((low_rank, width), single, False),
-            ((2, low_rank, hidden_width), single, False),
-            ((low_rank, hidden_width), single, False),
-        ],
-        count * 13_000_000,
-    )
-    mid_grad = scatter_rows(mid_part)
+            (column_sets, WHOLE),
+            (feed_down, WHOLE),
+            (w_gate.T, WHOLE),
+            (w_up.T, WHOLE),
+            (up_ff.transpose(0, 2, 1), WHOLE),
+            (up_ff_padded, WHOLE),
+        ],
+        [
+            ((count, width), bfloat, "parts"),
+            ((count, padded), bfloat, "rows"),
+            ((count, 2 * padded), bfloat, "rows"),
+            ((count, 2 * low_rank), bfloat, "rows"),
+            ((count, 2 * low_rank), bfloat, "rows"),
+        ],
+        [
+            pltpu.VMEM((padded, width + low_rank), bfloat),
+            pltpu.VMEM((padded, width + low_rank), bfloat),
+            pltpu.VMEM((2 * padded + 2 * low_rank, width), bfloat),
+        ],
+        count * 15_000_000,
+    )
+    mid_own, mid_far = near_sum(mid_part)
+    mid_far, hidden = tie(mid_far, hidden)
+    mid_grad = far_sum(mid_own, mid_far)
+    out_part, feed_down_grad, feed_res_grad, feed_up_grad, ffd_grad = blocked_call(
+        feed_after_kernel,
+        "feed_after",
+        count,
+        [
+            (mid_all, pieces(width)),
+            (grad_all, pieces(width)),
+            (hidden, by_rows(padded)),
+            (ff_grad, by_rows(2 * padded)),
+            (u_ff, by_rows(2 * low_rank)),
+            (du_ff, by_rows(2 * low_rank)),
+            (du_down, by_rows(low_rank)),
+            (table, by_rows(8)),
+            (column_sets, WHOLE),
+            (w_down, WHOLE),
+            (down_ffd_padded, WHOLE),
+            (up_res[1], WHOLE),
+        ],
+        [
+            ((count, width), bfloat, "parts"),
+            ((2 * low_rank, width), single, "whole"),
+            ((low_rank, width), single, "whole"),
+            ((2, low_rank, padded), single, "whole"),
+            ((low_rank, padded), single, "whole"),
+        ],
+        [pltpu.VMEM((padded + low_rank, width), bfloat)],
+        count * 12_000_000,
+    )
     residual_grad = out_grad.astype(single) + rms_back(residual, norm2_gain, mid_grad)
-    branch_grad = gather_rows(low(residual_grad))
-    result = residual + scatter_rows(out_part)
-
-    (
-        raw_grad,
-        gate_grad,
-        du_outgate,
-        state_grad,
-        branch_res_grad,
-        out_down_grad,
-        outgate_up_grad,
-        outgate_down_grad,
-    ) = blocked_call(
+    branch_low = low(residual_grad)
+    branch_all = gather_rows(branch_low)
+    feed_own, feed_far = near_sum(
+        head_blocks([feed_down_grad[:low_rank], feed_down_grad[low_rank:], feed_res_grad])
+    )
+    feed_flat = jnp.concatenate(
+        [
+            low(far_sum(feed_own, feed_far)),
+            low(feed_up_grad[0]),
+            low(feed_up_grad[1]),
+            low(ffd_grad),
+        ],
+        axis=1,
+    )
+    corner, feed_flat = tie(branch_all[3], feed_flat)
+    branch_all = branch_all[:3] + [corner]
+    feed_parts = seq_parts(feed_flat)
+
+    raw_grad, gate_grad, du_out, du_outgate, state_grad = blocked_call(
         functools.partial(branch_kernel, **sizes),
         "branch",
         count,
         [
-            (branch_grad, by_rows(width)),
+            (branch_all, pieces(width)),
             (raw_local, by_rows(value_lanes)),
             (mapped, by_rows(qk)),
             (gate_input, by_rows(value_lanes)),
+            (table, by_rows(8)),
+            (entering, WHOLE),
+            (gain, WHOLE),
+            (column_sets, WHOLE),
+            (w_out, WHOLE),
+            (down_out.T, WHOLE),
+            (up_res[0], WHOLE),
+            (up_vg[1], WHOLE),
+        ],
+        [
+            ((count, value_lanes), bfloat, "rows"),
+            ((count, value_lanes), bfloat, "rows"),
+            ((count, low_rank), bfloat, "rows"),
+            ((count, low_rank), bfloat, "rows"),
+            ((heads, key_width, value_width), bfloat, "whole"),
+        ],
+        [
+            pltpu.VMEM((value_lanes, width + low_rank), bfloat),
+            pltpu.VMEM((heads, key_width, value_width), single),
+        ],
+        count * 7_000_000,
+    )
+    feed_parts, state_grad = tie(feed_parts, state_grad)
+    maps_after = [shifted_along(sent_map, "seq", -hop) for hop in range(1, hops)]
+    state_got = [shifted_along(state_grad, "seq", -hop) for hop in range(1, hops + 1)]
+    mixer_down_late, branch_res_grad, out_down_grad, outgate_up_grad = blocked_call(
+        branch_after_kernel,
+        "branch_after",
+        count,
+        [
+            (branch_all, pieces(width)),
             (mixed, by_rows(value_lanes)),
             (u_out, by_rows(low_rank)),
-            (normed_all, by_rows(width)),
+            (normed_all, pieces(width)),
             (inner, by_rows(low_rank, 3)),
+            (du_out, by_rows(low_rank)),
+            (du_outgate, by_rows(low_rank)),
+            (gate_grad, by_rows(value_lanes)),
+        ],
+        [
+            ((low_rank, width), single, "whole"),
+            ((low_rank, width), single, "whole"),
+            ((low_rank, value_lanes), single, "whole"),
+            ((low_rank, value_lanes), single, "whole"),
+        ],
+        [],
+        count * 3_000_000,
+    )
+    branch_flat = jnp.concatenate(
+        [
+            low(far_sum(*near_sum(head_blocks([mixer_down_late, branch_res_grad])))),
+            low(out_down_grad),
+            low(outgate_up_grad),
+        ],
+        axis=1,
+    )
+    out_own, out_far = near_sum(out_part)
+    raw_grad, branch_flat, feed_parts, out_far = tie(raw_grad, branch_flat, feed_parts, out_far)
+    result = residual + far_sum(out_own, out_far)
+    feed_total = seq_spread(feed_parts)
+    branch_parts = seq_parts(branch_flat)
+
+    pre_grad, mix_grad, tail_grad, edge_grad = run_backward(
+        where, pre, pre_halo, columns, conv, scalars, raw_grad, saved, entering, state_got,
+        maps_after, heads, key_width, value_width, quarter,
+    )
+    arrived = shifted_along(edge_grad, "seq", -1)
+    arrived, feed_total, branch_parts = tie(arrived, feed_total, branch_parts)
+    branch_total = seq_spread(branch_parts)
+    settled = [
+        (pre_grad, by_rows(2 * qk + value_lanes)),
+        (tail_grad, WHOLE),
+        (arrived, WHOLE),
+        (where, SCALAR),
+    ]
+    du_mix, mixer_down_grad, up_qk_grad, up_v_grad = blocked_call(
+        settle_grads_kernel,
+        "settle_grads",
+        count,
+        [
+            settled[0],
+            (normed_all, pieces(width)),
+            (inner, by_rows(4 * low_rank)),
             (table, by_rows(8)),
-            (entering_low, None),
-            (gain, None),
-            (column_sets, None),
-            (w_out, None),
-            (down_out, None),
-            (up_res[0], None),
-            (up_vg, None),
-        ],
-        [
-            ((count, value_lanes), bfloat, True),
-            ((count, value_lanes), bfloat, True),
-            ((count, low_rank), bfloat, True),
-            ((heads, key_width, value_width), single, False),
-            ((low_rank, width), single, False),
-            ((low_rank, value_lanes), single, False),
-            ((low_rank, value_lanes), single, False),
-            ((low_rank, width), single, False),
-        ],
-        count * 3_000_000,
-    )
-    state_low = low(state_grad)
-    later = None
-    for hop in range(hops, 0, -1):
-        got = shifted_along(state_low, "seq", -hop).astype(single)
-        if later is None:
-            later = got
-        else:
-            later = got + jnp.einsum(
-                "hji,hjk->hik", maps_after[hop - 1], low(later), preferred_element_type=single
-            )
-
-    first_shared, first_owned = reduce_maps(
-        [outgate_down_grad, feed_down_grad[0], feed_down_grad[1], branch_res_grad, feed_res_grad],
-        [outgate_up_grad, feed_up_grad[0], feed_up_grad[1], out_down_grad, ffd_grad],
-    )
-
-    pre_grad, mix_grad, tail_grad, edge_grad = run_backward(
-        where, pre, pre_halo, columns, conv, scalars, raw_grad, saved, entering_low, low(later),
-        heads, key_width, value_width, quarter,
-    )
-    arrived = shifted_along(edge_grad, "seq", -1)
-    tail_at = ((groups - 1) ^ place) * quarter + quarter - HALO
-    pre_grad = lax.dynamic_update_slice_in_dim(pre_grad, low(tail_grad + arrived), tail_at, 0)
-    normed_part, mixer_down_grad, up_qk_grad, up_v_grad = blocked_call(
+            *settled[1:],
+            (column_sets, WHOLE),
+            (up_qk, WHOLE),
+            (up_vg[0], WHOLE),
+        ],
+        [
+            ((count, 3 * low_rank), bfloat, "rows"),
+            ((3 * low_rank, width), single, "whole"),
+            ((2, low_rank, qk), single, "whole"),
+            ((low_rank, value_lanes), single, "whole"),
+        ],
+        [pltpu.VMEM((STEP, 2 * qk + value_lanes), bfloat)],
+        count * 4_000_000,
+    )
+    last_own, last_far = near_sum(
+        head_blocks([mixer_down_grad[p * low_rank : (p + 1) * low_rank] for p in range(3)])
+    )
+    last_far, gate_grad = tie(last_far, gate_grad)
+    (normed_part,) = blocked_call(
         settle_kernel,
         "settle",
         count,
         [
-            (pre_grad, by_rows(2 * qk + value_lanes)),
+            settled[0],
             (gate_grad, by_rows(value_lanes)),
+            (du_mix, by_rows(3 * low_rank)),
             (du_outgate, by_rows(low_rank)),
             (mix_grad, by_rows(8)),
-            (normed_all, by_rows(width)),
-            (inner, by_rows(4 * low_rank)),
-            (table, by_rows(8)),
-            (column_sets, None),
-            (mixer_down, None),
-            (w_query, None),
-            (w_key, None),
-            (w_value, None),
-            (w_gate_out, None),
-            (weight_mix_padded, None),
-            (up_qk, None),
-            (up_vg, None),
-        ],
-        [
-            ((count, width), bfloat, True),
-            ((3 * low_rank, width), single, False),
-            ((2, low_rank, qk), single, False),
-            ((low_rank, value_lanes), single, False),
-        ],
-        count * 7_000_000,
-    )
-    last_shared, last_owned = reduce_maps(
-        [mixer_down_grad[p * low_rank : (p + 1) * low_rank] for p in range(3)],
-        [up_qk_grad[0], up_qk_grad[1], up_v_grad],
-    )
-    normed_grad = scatter_rows(normed_part)
+            *settled[1:],
+            (down_mix, WHOLE),
+            (w_query, WHOLE),
+            (w_key, WHOLE),
+            (w_value, WHOLE),
+            (w_gate_out, WHOLE),
+        ],
+        [((count, width), bfloat, "parts")],
+        [
+            pltpu.VMEM((STEP, 2 * qk + value_lanes), bfloat),
+            pltpu.VMEM((width, 2 * qk + 2 * value_lanes), bfloat),
+        ],
+        count * 10_000_000,
+    )
+    last_flat = jnp.concatenate(
+        [
+            low(far_sum(last_own, last_far)),
+            low(up_qk_grad[0]),
+            low(up_qk_grad[1]),
+            low(up_v_grad),
+        ],
+        axis=1,
+    )
+    last_parts = seq_parts(last_flat)
+    normed_grad = far_sum(*near_sum(normed_part))
     input_grad = residual_grad + rms_back(input_float, norm1_gain, normed_grad)
+    last_total = seq_spread(last_parts)
+    block_width = width // groups
+    shared = head_spread(
+        jnp.concatenate(
+            [
+                last_total[:, : 3 * block_width],
+                branch_total[:, : 2 * block_width],
+                feed_total[:, : 3 * block_width],
+            ],
+            axis=1,
+        ),
+        8,
+    )
+
+    def lanes_of(total, start, size):
+        return total[:, start : start + size].astype(single)
+
+    owned_qk = [lanes_of(last_total, 3 * block_width + k * qk, qk) for k in range(2)]
+    owned_value = lanes_of(last_total, 3 * block_width + 2 * qk, value_lanes)
+    owned_out = lanes_of(branch_total, 2 * block_width, value_lanes)
+    owned_outgate = lanes_of(branch_total, 2 * block_width + value_lanes, value_lanes)
+    owned_ff = [lanes_of(feed_total, 3 * block_width + k * padded, hidden_width) for k in range(2)]
+    owned_ffd = lanes_of(feed_total, 3 * block_width + 2 * padded, hidden_width)
 
     def as_down(rows):
         return rows.reshape(sets, rank, -1).transpose(0, 2, 1)
@@ -1268,17 +1635,16 @@
     def as_up(rows):
         return rows.reshape(sets, rank, -1)
 
-    down_total = jnp.stack([as_down(part) for part in last_shared + first_shared[:3]])
     return (
         low(result),
         input_grad,
-        down_total,
-        jnp.stack([as_up(last_owned[0]), as_up(last_owned[1])]),
-        jnp.stack([as_up(last_owned[2]), as_up(first_owned[0])]),
-        jnp.stack([as_up(first_owned[1]), as_up(first_owned[2])]),
-        as_down(first_owned[3]),
-        as_down(first_owned[4]),
-        jnp.stack([as_up(first_shared[3]), as_up(first_shared[4])]),
+        jnp.stack([as_down(shared[k]) for k in (0, 1, 2, 3, 5, 6)]),
+        jnp.stack([as_up(part) for part in owned_qk]),
+        jnp.stack([as_up(owned_value), as_up(owned_outgate)]),
+        jnp.stack([as_up(part) for part in owned_ff]),
+        as_down(owned_out),
+        as_down(owned_ffd),
+        jnp.stack([as_up(shared[4]), as_up(shared[7])]),
     )
 
 

time: 452 us -> 445 us (0.985); the launches traced: 450 us -> 437 us
  waiting for transfers between devices: 161 us -> 143 us
  starting transfers between devices: 73.9 us -> 89.6 us
  other arithmetic: 50 us -> 40.3 us
  Pallas kernels: 126 us -> 131 us
    all_to_all x4 -> x6, starting transfers between devices: 16.1 us -> 36.8 us  [the longest x3 22.7 us: seq_parts(): lax.all_to_all(flat.reshape(members, rows // members, lanes), 'seq', 0, 0)]
    ppermute x36 -> x29, waiting for transfers between devices: 94.1 us -> 76.5 us  [flip(): return lax.ppermute(array, 'head', [(i, i ^ bit) for i in range(groups)])]
    all_to_all x4 -> x6, waiting for transfers between devices: 38.5 us -> 28.7 us  [the longest x3 22.1 us: seq_parts(): lax.all_to_all(flat.reshape(members, rows // members, lanes), 'seq', 0, 0)]
    ppermute x12, waiting for transfers between devices: 28 us -> 37.7 us  [shifted_along(): return lax.ppermute(array, axis, pairs)]
    unnamed x62 -> x120, local copies, waits for them, and re-layouts: 11.3 us -> 3.66 us
    concatenate x3 -> x1, local copies, waits for them, and re-layouts: 5.13 us -> 0.08 us  [on_device(): jnp.concatenate([mixer_down, w_decay_beta.transpose(1, 2, 0).reshape(2 *...]
    ppermute x36 -> x29, starting transfers between devices: 31 us -> 26 us  [flip(): return lax.ppermute(array, 'head', [(i, i ^ bit) for i in range(groups)])]
    concatenate x15, other arithmetic: 9.7 us -> 4.83 us  [the longest x1 1.31 us: on_device(): jnp.concatenate([mixer_down, w_decay_beta.transpose(1, 2, 0).reshape(2 *...]
  transfers between devices with their start and end apart: 56 -> 51, of which waited for: 24 -> 22; matrix products, arithmetic and copies ran while one was open for 15% -> 12% of each run, Pallas kernels for 12% -> 20%
where the time goes in v1:
time: 445 us; the launch traced here: 437 us
  waiting for transfers between devices  143 us (32%)
  Pallas kernels  131 us (29%)
  starting transfers between devices  89.6 us (20%)
  other arithmetic  40.3 us (9%)
  local copies, waits for them, and re-layouts  30.7 us (7%)
    pallas_call x9, Pallas kernels, blocked_call(): pl.pallas_call(wrapped, out_shape=tuple(shapes), grid=(steps,), in_specs=...  88.9 us
    ppermute x29, waiting for transfers between devices, flip(): return lax.ppermute(array, 'head', [(i, i ^ bit) for i in range(groups)])  76.5 us
    ppermute x12, waiting for transfers between devices, shifted_along(): return lax.ppermute(array, axis, pairs)  37.7 us
    ppermute x29, starting transfers between devices, flip(): return lax.ppermute(array, 'head', [(i, i ^ bit) for i in range(groups)])  26 us
    ppermute x12, starting transfers between devices, shifted_along(): return lax.ppermute(array, axis, pairs)  24.1 us
    all_to_all x3, starting transfers between devices, seq_parts(): lax.all_to_all(flat.reshape(members, rows // members, lanes), 'seq', 0, 0)  22.7 us
    all_to_all x3, waiting for transfers between devices, seq_parts(): lax.all_to_all(flat.reshape(members, rows // members, lanes), 'seq', 0, 0)  22.1 us
    pallas_call x1, Pallas kernels, run_backward(): pl.pallas_call(body, out_shape=shapes, grid_spec=pltpu.PrefetchScalarGrid...  21.8 us
  transfers between devices with their start and end apart: 51, of which 22 were waited for; matrix products, arithmetic and copies ran while one was open for 12% of the time, Pallas kernels for 20%

profile of v1, /device:TPU:0, one launch (start us, length us, event | category | flops | bytes accessed | tf_op | source)
XLA Modules:
  0.0 437.1 jit_solution(17602269886964392070)
XLA Ops:
  25.7 11.8 %project.1 = (bf16[1024,1024]{1,0:T(8,128)(2,1)}, f32[1024,512]{1,0:T(8,128)}, bf16[1024,512]{1,0:T(8,128)(2,1)}, f32[1024,8]{1,0:T(8,128)}, bf16[16,1024]{1,0:T(8,128)(2,1)}) custom-call(bf16[256,1024]{1,0:T(8,128)(2,1)} %copy-done.9, bf16[256,1024]{1,0:T(8,128)(2,1)} %collective-permute-done.refs_1_.refs_7_.refs_2_, ...), custom_call_target="tpu_custom_call" | custom-call | flops 9216000000 | bytes 7016960 | tf_op jit(solution)/shard_map/project/pallas_call | solution.py:1080
  43.2 7.4 %collective-permute-done.8.refs_2_.refs_6_ = bf16[256,1024]{1,0:T(8,128)(2,1)S(1)} collective-permute-done((bf16[256,1024]{1,0:T(8,128)(2,1)S(1)}, bf16[256,1024]{1,0:T(8,128)(2,1)S(1)}, u32[]{:S(2)}, u32[]{:S(2)}) %collective-permute-start.8) | collective-permute-done | bytes 524320 | tf_op jit(solution)/shard_map/ppermute | solution.py:1102
  53.7 20.5 %delta_forward.1 = (f32[1024,512]{1,0:T(8,128)}, bf16[1024,256]{1,0:T(8,128)(2,1)}, bf16[1024,768]{1,0:T(8,128)(2,1)}, bf16[8,2,128,384]{3,2,1,0:T(8,128)(2,1)},...) custom-call(s32[1]{0:T(128)} %bitcast.place.refs_9_.refs_7_, ...), custom_call_target="tpu_custom_call" | custom-call | flops 2048000000 | bytes 10240000 | tf_op jit(solution)/shard_map/delta_forward/pallas_call | solution.py:515
  88.9 6.9 %feed_before.1 = (f32[1024,768]{1,0:T(8,128)}, bf16[1024,128]{1,0:T(8,128)(2,1)}) custom-call(bf16[256,1024]{1,0:T(8,128)(2,1)} %refs_4_, bf16[256,1024]{1,0:T(8,128)(2,1)} %copy-done.40, bf16[256,1024]{1,0:T(8,128)(2,1)} %copy-done.39, bf16[256,1024]{1,0:T(8,128)(2,1)} %copy-done.41, f32[1024,8]{1,0:T(8,128)} %pad.16.refs_4_.refs_3_.refs_5_.refs_13_.refs_7_.refs_6_, ...), custom_call_target="tpu_custom_call" | custom-call | flops 6144000000 | bytes 4018176 | tf_op jit(solution)/shard_map/feed_before/pallas_call | solution.py:1080
  96.7 8.6 %attend.1 = (bf16[256,1024]{1,0:T(8,128)(2,1)}, bf16[256,1024]{1,0:T(8,128)(2,1)}, bf16[512,1024]{1,0:T(8,128)(2,1)}, bf16[1024,512]{1,0:T(8,128)(2,1)}, bf16[10...) custom-call(f32[1024,512]{1,0:T(8,128)} %get-tuple-element.103.refs_0_.refs_4_, ...), custom_call_target="tpu_custom_call" | custom-call | flops 5120000000 | bytes 6926336 | tf_op jit(solution)/shard_map/attend/pallas_call | solution.py:1080
  110.5 13.0 %collective-permute-done.15 = bf16[256,1024]{1,0:T(8,128)(2,1)S(1)} collective-permute-done((bf16[256,1024]{1,0:T(8,128)(2,1)S(1)}, bf16[256,1024]{1,0:T(8,128)(2,1)S(1)}, u32[]{:S(2)}, u32[]{:S(2)}) %collective-permute-start.15) | collective-permute-done | bytes 524320 | tf_op jit(solution)/shard_map/ppermute | solution.py:1102
  125.4 12.2 %collective-permute-done.17.refs_2_ = bf16[256,1024]{1,0:T(8,128)(2,1)S(1)} collective-permute-done((bf16[256,1024]{1,0:T(8,128)(2,1)S(1)}, bf16[256,1024]{1,0:T(8,128)(2,1)S(1)}, u32[]{:S(2)}, u32[]{:S(2)}) %collective-permute-start.17) | collective-permute-done | bytes 524320 | tf_op jit(solution)/shard_map/ppermute | solution.py:1102
  141.7 17.3 %feed.1 = (bf16[256,1024]{1,0:T(8,128)(2,1)}, bf16[256,1024]{1,0:T(8,128)(2,1)}, bf16[512,1024]{1,0:T(8,128)(2,1)}, bf16[1024,768]{1,0:T(8,128)(2,1)}, bf16[1024...) custom-call(bf16[256,1024]{1,0:T(8,128)(2,1)} %copy-done.15, ...), custom_call_target="tpu_custom_call" | custom-call | flops 15360000000 | bytes 9441280 | tf_op jit(solution)/shard_map/feed/pallas_call | solution.py:1080
  164.5 11.5 %feed_after.1 = (bf16[256,1024]{1,0:T(8,128)(2,1)}, bf16[256,1024]{1,0:T(8,128)(2,1)}, bf16[512,1024]{1,0:T(8,128)(2,1)}, f32[256,1024]{1,0:T(8,128)}, f32[128,1...) custom-call(bf16[256,1024]{1,0:T(8,128)(2,1)} %copy-done.15, ...), custom_call_target="tpu_custom_call" | custom-call | flops 12288000000 | bytes 12161024 | tf_op jit(solution)/shard_map/feed_after/pallas_call | solution.py:1080
  189.9 8.1 %collective-permute-done.23.refs_2_ = bf16[256,1024]{1,0:T(8,128)(2,1)} collective-permute-done((bf16[256,1024]{1,0:T(8,128)(2,1)}, bf16[256,1024]{1,0:T(8,128)(2,1)}, u32[]{:S(2)}, u32[]{:S(2)}) %collective-permute-start.23) | collective-permute-done | bytes 524320 | tf_op jit(solution)/shard_map/ppermute | solution.py:1102
  203.7 12.5 %all-to-all-start = ((bf16[8,16,3072]{2,1,0:T(8,128)(2,1)}), bf16[8,16,3072]{2,1,0:T(8,128)(2,1)S(1)}, u32[]{:S(2)}, u32[]{:S(2)}) async-start(bf16[8,16,3072]{2,1,0:T(8,128)(2,1)} %bitcast.111), calls=%async_computation | async-start | bytes 1572864 | tf_op jit(solution)/shard_map/all_to_all | solution.py:1153
  216.2 8.9 %branch.1 = (bf16[1024,512]{1,0:T(8,128)(2,1)}, bf16[1024,512]{1,0:T(8,128)(2,1)}, bf16[1024,128]{1,0:T(8,128)(2,1)}, bf16[1024,128]{1,0:T(8,128)(2,1)}, bf16[2,128,256]{2,1,0:T(8,128)(2,1)}) custom-call(bf16[256,1024]{1,0:T(8,128)(2,1)} %get-tuple-element.177.refs_0_, bf16[256,1024]{1,0:T(8,128)(2,1)} %collective-permute-done.22.refs_1_, ...), custom_call_target="tpu_custom_call" | custom-call | flops 7168000000 | bytes 8564736 | tf_op jit(solution)/shard_map/branch/pallas_call | solution.py:1080
  225.1 6.2 %branch_after.1 = (f32[128,1024]{1,0:T(8,128)}, f32[128,1024]{1,0:T(8,128)}, f32[128,512]{1,0:T(8,128)}, f32[128,512]{1,0:T(8,128)}) custom-call(bf16[256,1024]{1,0:T(8,128)(2,1)} %get-tuple-element.177.refs_0_, bf16[256,1024]{1,0:T(8,128)(2,1)} %collective-permute-done.22.refs_1_, bf16[256,1024]{1,0:T(8,128)(2,1)} %collective-permute-done.23.refs_2_, ...), custom_call_target="tpu_custom_call" | custom-call | flops 3072000000 | bytes 8126464 | tf_op jit(solution)/shard_map/branch_after/pallas_call | solution.py:1080
  241.8 6.0 %all-to-all-start.2 = ((bf16[8,16,1536]{2,1,0:T(8,128)(2,1)}), bf16[8,16,1536]{2,1,0:T(8,128)(2,1)}, u32[]{:S(2)}, u32[]{:S(2)}) async-start(bf16[8,16,1536]{2,1,0:T(8,128)(2,1)} %bitcast.113), calls=%async_computation.2 | async-start | bytes 786432 | tf_op jit(solution)/shard_map/all_to_all | solution.py:1153
  247.9 11.2 %all-to-all-done.2 = bf16[8,16,1536]{2,1,0:T(8,128)(2,1)} async-done(((bf16[8,16,1536]{2,1,0:T(8,128)(2,1)}), bf16[8,16,1536]{2,1,0:T(8,128)(2,1)}, u32[]{:S(2)}, u32[]{:S(2)}) %all-to-all-start.2) | async-done | bytes 393248 | tf_op jit(solution)/shard_map/all_to_all | solution.py:1153
  281.1 13.6 %collective-permute-done.36.rest_6_ = bf16[2,128,128]{2,1,0:T(8,128)(2,1)S(1)} collective-permute-done((bf16[2,128,128]{2,1,0:T(8,128)(2,1)}, bf16[2,128,128]{2,1,0:T(8,128)(2,1)S(1)}, u32[]{:S(2)}, u32[]{:S(2)}) %collective-permute-start.36) | collective-permute-done | bytes 65568 | tf_op jit(solution)/shard_map/ppermute | solution.py:1132
  294.7 10.5 %collective-permute-done.33.rest_3_ = bf16[2,128,256]{2,1,0:T(8,128)(2,1)S(1)} collective-permute-done((bf16[2,128,256]{2,1,0:T(8,128)(2,1)S(1)}, bf16[2,128,256]{2,1,0:T(8,128)(2,1)S(1)}, u32[]{:S(2)}, u32[]{:S(2)}) %collective-permute-start.33) | collective-permute-done | bytes 131104 | tf_op jit(solution)/shard_map/ppermute | solution.py:1132
  305.9 21.8 %delta_backward.1 = (bf16[1024,1024]{1,0:T(8,128)(2,1)}, f32[1024,8]{1,0:T(8,128)}, f32[16,1024]{1,0:T(8,128)}, f32[16,1024]{1,0:T(8,128)}) custom-call(s32[1]{0:T(128)} %bitcast.place.refs_9_.refs_7_, bf16[1024,1024]{1,0:T(8,128)(2,1)} %get-tuple-element.92.rows_ref.before_ref, bf16[1024,1024]{1,0:T(8,128)(2,1)} %get-tuple-element.92.rows_ref.before_ref, ...), custom_call_target="tpu_custom_call" | custom-call | flops 3072000000 | bytes 12288000 | tf_op jit(solution)/shard_map/delta_backward/pallas_call | solution.py:588
  335.0 7.4 %settle_grads.1 = (bf16[1024,384]{1,0:T(8,128)(2,1)}, f32[384,1024]{1,0:T(8,128)}, f32[2,128,256]{2,1,0:T(8,128)}, f32[128,512]{1,0:T(8,128)}) custom-call(bf16[1024,1024]{1,0:T(8,128)(2,1)} %get-tuple-element.155.refs_0_, bf16[256,1024]{1,0:T(8,128)(2,1)} %copy-done.9, bf16[256,1024]{1,0:T(8,128)(2,1)} %collective-permute-done.refs_1_.refs_7_.refs_2_, ...), custom_call_target="tpu_custom_call" | custom-call | flops 4096000000 | bytes 5672964 | tf_op jit(solution)/shard_map/settle_grads/pallas_call | solution.py:1080
  347.0 6.1 %collective-permute-done.41 = bf16[128,768]{1,0:T(8,128)(2,1)S(1)} collective-permute-done((bf16[128,768]{1,0:T(8,128)(2,1)S(1)}, bf16[128,768]{1,0:T(8,128)(2,1)S(1)}, u32[]{:S(2)}, u32[]{:S(2)}) %collective-permute-start.41) | collective-permute-done | bytes 196640 | tf_op jit(solution)/shard_map/ppermute | solution.py:1102
  360.0 10.9 %all-to-all-done.3 = bf16[8,16,1792]{2,1,0:T(8,128)(2,1)} async-done(((bf16[8,16,1792]{2,1,0:T(8,128)(2,1)}), bf16[8,16,1792]{2,1,0:T(8,128)(2,1)}, u32[]{:S(2)}, u32[]{:S(2)}) %all-to-all-start.3) | async-done | bytes 458784 | tf_op jit(solution)/shard_map/all_to_all | solution.py:1153
  376.0 10.3 %settle.1 = (bf16[256,1024]{1,0:T(8,128)(2,1)}, bf16[256,1024]{1,0:T(8,128)(2,1)}, bf16[512,1024]{1,0:T(8,128)(2,1)}) custom-call(bf16[1024,1024]{1,0:T(8,128)(2,1)} %get-tuple-element.155.refs_0_, bf16[1024,512]{1,0:T(8,128)(2,1)} %get-tuple-element.162.refs_13_.refs_1_, bf16[1024,384]{1,0:T(8,128)(2,1)} %get-tuple-element.163.refs_2_, ...), custom_call_target="tpu_custom_call" | custom-call | flops 10240000000 | bytes 8814596 | tf_op jit(solution)/shard_map/settle/pallas_call | solution.py:1080
  403.9 6.7 %all-to-all-done.4 = bf16[8,16,1792]{2,1,0:T(8,128)(2,1)} async-done(((bf16[8,16,1792]{2,1,0:T(8,128)(2,1)}), bf16[8,16,1792]{2,1,0:T(8,128)(2,1)}, u32[]{:S(2)}, u32[]{:S(2)}) %all-to-all-start.4) | async-done | bytes 458784 | tf_op jit(solution)/shard_map/all_to_all | solution.py:1160
  417.7 9.0 %collective-permute-done.43 = bf16[128,2048]{1,0:T(8,128)(2,1)S(1)} collective-permute-done((bf16[128,2048]{1,0:T(8,128)(2,1)S(1)}, bf16[128,2048]{1,0:T(8,128)(2,1)S(1)}, u32[]{:S(2)}, u32[]{:S(2)}) %collective-permute-start.43) | collective-permute-done | bytes 524320 | tf_op jit(solution)/shard_map/ppermute | solution.py:1102
  (325 shorter events, 176.3 us)
Async XLA Ops:
  3.3 18.5 %collective-permute-start.3 = (bf16[16,1024]{1,0:T(8,128)(2,1)S(1)}, bf16[16,1024]{1,0:T(8,128)(2,1)S(1)}, u32[]{:S(2)}, u32[]{:S(2)}) collective-permute-start(bf16[16,1024]{1,0:T(8,128)(2,1)S(1)} %slice.310), channel_id=1, source_target_pairs={{3,4},{7,8},{11,12},{15,16},{19,20},{23,24},{27,28}} | collective-permute-start | bytes 98312 | tf_op jit(solution)/shard_map/ppermute | solution.py:1286
  4.0 20.2 %collective-permute-start.4 = (bf16[16,1024]{1,0:T(8,128)(2,1)S(1)}, bf16[16,1024]{1,0:T(8,128)(2,1)S(1)}, u32[]{:S(2)}, u32[]{:S(2)}) collective-permute-start(bf16[16,1024]{1,0:T(8,128)(2,1)S(1)} %slice.310), channel_id=1, source_target_pairs={{3,5},{7,9},{11,13},{15,17},{19,21},{23,25},{27,29}} | collective-permute-start | bytes 98312 | tf_op jit(solution)/shard_map/ppermute | solution.py:1286
  4.7 19.6 %collective-permute-start.5 = (bf16[16,1024]{1,0:T(8,128)(2,1)S(1)}, bf16[16,1024]{1,0:T(8,128)(2,1)S(1)}, u32[]{:S(2)}, u32[]{:S(2)}) collective-permute-start(bf16[16,1024]{1,0:T(8,128)(2,1)S(1)} %slice.310), channel_id=1, source_target_pairs={{3,6},{7,10},{11,14},{15,18},{19,22},{23,26},{27,30}} | collective-permute-start | bytes 98312 | tf_op jit(solution)/shard_map/ppermute | solution.py:1286
  8.3 16.5 %collective-permute-start = (bf16[256,1024]{1,0:T(8,128)(2,1)S(1)}, bf16[256,1024]{1,0:T(8,128)(2,1)}, u32[]{:S(2)}, u32[]{:S(2)}) collective-permute-start(bf16[256,1024]{1,0:T(8,128)(2,1)S(1)} %fusion.4.refs_0_.refs_6_.refs_1_), channel_id=1, source_target_pairs={{0,1},{1,0},{2,3},{3,2},{4,5},{5,4},{6,7},{7,6},{8,9},{9,8},{10,11... | collective-permute-start | bytes 1572872 | tf_op jit(solution)/shard_map/ppermute | solution.py:1102
  40.4 46.0 %collective-permute-start.7 = (bf16[256,1024]{1,0:T(8,128)(2,1)S(1)}, bf16[256,1024]{1,0:T(8,128)(2,1)S(1)}, u32[]{:S(2)}, u32[]{:S(2)}) collective-permute-start(bf16[256,1024]{1,0:T(8,128)(2,1)S(1)} %copy-done.10), channel_id=1, source_target_pairs={{0,1},{1,0},{2,3},{3,2},{4,5},{5,4},{6,7},{7,6},{8,9},{9,8},{10,11... | collective-permute-start | bytes 1572872 | tf_op jit(solution)/shard_map/ppermute | solution.py:1102
  50.6 37.4 %collective-permute-start.9 = (bf16[256,1024]{1,0:T(8,128)(2,1)S(1)}, bf16[256,1024]{1,0:T(8,128)(2,1)S(1)}, u32[]{:S(2)}, u32[]{:S(2)}) collective-permute-start(bf16[256,1024]{1,0:T(8,128)(2,1)S(1)} %collective-permute-done.8.refs_2_.refs_6_), channel_id=1, source_target_pairs={{0,1},{1,0},{2,3},{3,2},{4,5},{5,4},{6,7},{7,6},{8,9},{9,8},{10,11... | collective-permute-start | bytes 1572872 | tf_op jit(solution)/shard_map/ppermute | solution.py:1102
  74.2 21.7 %collective-permute-start.10 = (bf16[2,128,384]{2,1,0:T(8,128)(2,1)}, bf16[2,128,384]{2,1,0:T(8,128)(2,1)S(1)}, u32[]{:S(2)}, u32[]{:S(2)}) collective-permute-start(bf16[2,128,384]{2,1,0:T(8,128)(2,1)} %get-tuple-element.106), channel_id=1, source_target_pairs={{0,4},{4,8},{8,12},{12,16},{16,20},{20,24},{24,28},{1,5},{5,9},{9,... | collective-permute-start | bytes 589832 | tf_op jit(solution)/shard_map/ppermute | solution.py:1132
  78.0 17.8 %collective-permute-start.11 = (bf16[2,128,384]{2,1,0:T(8,128)(2,1)}, bf16[2,128,384]{2,1,0:T(8,128)(2,1)S(1)}, u32[]{:S(2)}, u32[]{:S(2)}) collective-permute-start(bf16[2,128,384]{2,1,0:T(8,128)(2,1)} %get-tuple-element.106), channel_id=1, source_target_pairs={{0,8},{4,12},{8,16},{12,20},{16,24},{20,28},{1,9},{5,13},{9,17},{1... | collective-permute-start | bytes 589832 | tf_op jit(solution)/shard_map/ppermute | solution.py:1132
  163.5 16.6 %collective-permute-start.21 = (bf16[256,1024]{1,0:T(8,128)(2,1)S(1)}, bf16[256,1024]{1,0:T(8,128)(2,1)S(1)}, u32[]{:S(2)}, u32[]{:S(2)}) collective-permute-start(bf16[256,1024]{1,0:T(8,128)(2,1)S(1)} %add_convert_fusion.3), channel_id=1, source_target_pairs={{0,2},{1,3},{2,0},{3,1},{4,6},{5,7},{6,4},{7,5},{8,10},{9,11},{10,... | collective-permute-start | bytes 1572872 | tf_op jit(solution)/shard_map/ppermute | solution.py:1102
  183.0 15.0 %collective-permute-start.23 = (bf16[256,1024]{1,0:T(8,128)(2,1)}, bf16[256,1024]{1,0:T(8,128)(2,1)}, u32[]{:S(2)}, u32[]{:S(2)}) collective-permute-start(bf16[256,1024]{1,0:T(8,128)(2,1)} %get-tuple-element.177.refs_0_), channel_id=1, source_target_pairs={{0,2},{1,3},{2,0},{3,1},{4,6},{5,7},{6,4},{7,5},{8,10},{9,11},{10,... | collective-permute-start | bytes 1572872 | tf_op jit(solution)/shard_map/ppermute | solution.py:1102
  186.5 49.9 %collective-permute-start.20 = (bf16[512,1024]{1,0:T(8,128)(2,1)}, bf16[512,1024]{1,0:T(8,128)(2,1)}, u32[]{:S(2)}, u32[]{:S(2)}) collective-permute-start(bf16[512,1024]{1,0:T(8,128)(2,1)} %get-tuple-element.123), channel_id=1, source_target_pairs={{0,1},{1,0},{2,3},{3,2},{4,5},{5,4},{6,7},{7,6},{8,9},{9,8},{10,11... | collective-permute-start | bytes 3145736 | tf_op jit(solution)/shard_map/ppermute | solution.py:1102
  189.8 26.4 %collective-permute-start.22 = (bf16[256,1024]{1,0:T(8,128)(2,1)}, bf16[256,1024]{1,0:T(8,128)(2,1)}, u32[]{:S(2)}, u32[]{:S(2)}) collective-permute-start(bf16[256,1024]{1,0:T(8,128)(2,1)} %get-tuple-element.177.refs_0_), channel_id=1, source_target_pairs={{0,1},{1,0},{2,3},{3,2},{4,5},{5,4},{6,7},{7,6},{8,9},{9,8},{10,11... | collective-permute-start | bytes 1572872 | tf_op jit(solution)/shard_map/ppermute | solution.py:1102
  203.7 38.1 %all-to-all-start = ((bf16[8,16,3072]{2,1,0:T(8,128)(2,1)}), bf16[8,16,3072]{2,1,0:T(8,128)(2,1)S(1)}, u32[]{:S(2)}, u32[]{:S(2)}) async-start(bf16[8,16,3072]{2,1,0:T(8,128)(2,1)} %bitcast.111), calls=%async_computation | async-start | bytes 1572864 | tf_op jit(solution)/shard_map/all_to_all | solution.py:1153
  241.8 17.3 %all-to-all-start.2 = ((bf16[8,16,1536]{2,1,0:T(8,128)(2,1)}), bf16[8,16,1536]{2,1,0:T(8,128)(2,1)}, u32[]{:S(2)}, u32[]{:S(2)}) async-start(bf16[8,16,1536]{2,1,0:T(8,128)(2,1)} %bitcast.113), calls=%async_computation.2 | async-start | bytes 786432 | tf_op jit(solution)/shard_map/all_to_all | solution.py:1153
  260.1 74.4 %all-to-all-start.1 = ((bf16[8,16,3072]{2,1,0:T(8,128)(2,1)}), bf16[8,16,3072]{2,1,0:T(8,128)(2,1)S(1)}, u32[]{:S(2)}, u32[]{:S(2)}) async-start(bf16[8,16,3072]{2,1,0:T(8,128)(2,1)} %broadcast_in_dim.127), calls=%async_computation.1 | async-start | bytes 1572864 | tf_op jit(solution)/shard_map/all_to_all | solution.py:1160
  266.4 28.3 %collective-permute-start.30 = (bf16[2,128,256]{2,1,0:T(8,128)(2,1)S(1)}, bf16[2,128,256]{2,1,0:T(8,128)(2,1)S(1)}, u32[]{:S(2)}, u32[]{:S(2)}) collective-permute-start(bf16[2,128,256]{2,1,0:T(8,128)(2,1)S(1)} %copy-done.46), channel_id=1, source_target_pairs={{4,0},{8,4},{12,8},{16,12},{20,16},{24,20},{28,24},{5,1},{9,5},{13... | collective-permute-start | bytes 393224 | tf_op jit(solution)/shard_map/ppermute | solution.py:1132
  267.7 27.0 %collective-permute-start.31 = (bf16[2,128,256]{2,1,0:T(8,128)(2,1)S(1)}, bf16[2,128,256]{2,1,0:T(8,128)(2,1)S(1)}, u32[]{:S(2)}, u32[]{:S(2)}) collective-permute-start(bf16[2,128,256]{2,1,0:T(8,128)(2,1)S(1)} %copy-done.46), channel_id=1, source_target_pairs={{8,0},{12,4},{16,8},{20,12},{24,16},{28,20},{9,1},{13,5},{17,9},{2... | collective-permute-start | bytes 393224 | tf_op jit(solution)/shard_map/ppermute | solution.py:1132
  269.0 25.7 %collective-permute-start.32 = (bf16[2,128,256]{2,1,0:T(8,128)(2,1)S(1)}, bf16[2,128,256]{2,1,0:T(8,128)(2,1)S(1)}, u32[]{:S(2)}, u32[]{:S(2)}) collective-permute-start(bf16[2,128,256]{2,1,0:T(8,128)(2,1)S(1)} %copy-done.46), channel_id=1, source_target_pairs={{12,0},{16,4},{20,8},{24,12},{28,16},{13,1},{17,5},{21,9},{25,13},... | collective-permute-start | bytes 393224 | tf_op jit(solution)/shard_map/ppermute | solution.py:1132
  275.6 29.7 %collective-permute-start.33 = (bf16[2,128,256]{2,1,0:T(8,128)(2,1)S(1)}, bf16[2,128,256]{2,1,0:T(8,128)(2,1)S(1)}, u32[]{:S(2)}, u32[]{:S(2)}) collective-permute-start(bf16[2,128,256]{2,1,0:T(8,128)(2,1)S(1)} %copy-done.46), channel_id=1, source_target_pairs={{16,0},{20,4},{24,8},{28,12},{17,1},{21,5},{25,9},{29,13},{18,2},{... | collective-permute-start | bytes 393224 | tf_op jit(solution)/shard_map/ppermute | solution.py:1132
  353.9 17.0 %all-to-all-start.3 = ((bf16[8,16,1792]{2,1,0:T(8,128)(2,1)}), bf16[8,16,1792]{2,1,0:T(8,128)(2,1)}, u32[]{:S(2)}, u32[]{:S(2)}) async-start(bf16[8,16,1792]{2,1,0:T(8,128)(2,1)} %bitcast.112), calls=%async_computation.3 | async-start | bytes 917504 | tf_op jit(solution)/shard_map/all_to_all | solution.py:1153
  358.1 28.3 %collective-permute-start.29 = (bf16[256,1024]{1,0:T(8,128)(2,1)}, bf16[256,1024]{1,0:T(8,128)(2,1)}, u32[]{:S(2)}, u32[]{:S(2)}) collective-permute-start(bf16[256,1024]{1,0:T(8,128)(2,1)} %add_convert_fusion.2), channel_id=1, source_target_pairs={{0,2},{1,3},{2,0},{3,1},{4,6},{5,7},{6,4},{7,5},{8,10},{9,11},{10,... | collective-permute-start | bytes 1572872 | tf_op jit(solution)/shard_map/ppermute | solution.py:1102
  371.7 18.3 %all-to-all-start.5 = ((bf16[8,16,1536]{2,1,0:T(8,128)(2,1)}), bf16[8,16,1536]{2,1,0:T(8,128)(2,1)}, u32[]{:S(2)}, u32[]{:S(2)}) async-start(bf16[8,16,1536]{2,1,0:T(8,128)(2,1)} %broadcast_in_dim.130), calls=%async_computation.5 | async-start | bytes 786432 | tf_op jit(solution)/shard_map/all_to_all | solution.py:1160
  390.8 19.8 %all-to-all-start.4 = ((bf16[8,16,1792]{2,1,0:T(8,128)(2,1)}), bf16[8,16,1792]{2,1,0:T(8,128)(2,1)}, u32[]{:S(2)}, u32[]{:S(2)}) async-start(bf16[8,16,1792]{2,1,0:T(8,128)(2,1)} %broadcast_in_dim.129), calls=%async_computation.4 | async-start | bytes 917504 | tf_op jit(solution)/shard_map/all_to_all | solution.py:1160
  401.2 15.0 %collective-permute-start.40 = (bf16[256,1024]{1,0:T(8,128)(2,1)}, bf16[256,1024]{1,0:T(8,128)(2,1)S(1)}, u32[]{:S(2)}, u32[]{:S(2)}) collective-permute-start(bf16[256,1024]{1,0:T(8,128)(2,1)} %add_convert_fusion), channel_id=1, source_target_pairs={{0,2},{1,3},{2,0},{3,1},{4,6},{5,7},{6,4},{7,5},{8,10},{9,11},{10,... | collective-permute-start | bytes 1572872 | tf_op jit(solution)/shard_map/ppermute | solution.py:1102
  (84 other events, 780.5 us)

commit v2 on v1

--- a/solution.py
+++ b/solution.py
@@ -652,6 +652,21 @@
     ref[...] = jnp.where(first, value, ref[...] + value)
 
 
+def emit_blocks(parts, place, own_ref, far_ref, pair_ref):
+    for k, part in enumerate(parts):
+        rows, size = part.shape[0], part.shape[1] // 4
+        lanes = slice(k * size, (k + 1) * size)
+        for relative, target, row in (
+            (0, own_ref, 0), (2, far_ref, 0), (1, pair_ref, 0), (3, pair_ref, rows)
+        ):
+            start = pl.multiple_of((place ^ relative) * size, 128)
+            target[row : row + rows, lanes] = low(part[:, pl.ds(start, size)])
+
+
+def at_end(fill):
+    pl.when(pl.program_id(0) == pl.num_programs(0) - 1)(fill)
+
+
 def at_start(fill):
     pl.when(pl.program_id(0) == 0)(fill)
 
@@ -812,9 +827,9 @@
 
 def feed_after_kernel(
     rows_ref, grad_ref, hidden_ref, ff_grad_ref, inner_ref, du_ref, du_down_ref, table_ref,
-    sets_ref, wd_ref, down_ffd_ref, up_ref,
-    out_ref, down_grad_ref, res_grad_ref, up_grad_ref, ffd_grad_ref,
-    joined,
+    sets_ref, place_ref, wd_ref, down_ffd_ref, up_ref,
+    out_ref, own_ref, far_ref, pair_ref, flat_ref,
+    joined, down_sum, res_sum, flat_sum,
 ):
     first = pl.program_id(0) == 0
     low_rank = sets_ref.shape[1]
@@ -835,11 +850,24 @@
         nt(hidden, down_ffd_ref[...]), chosen_columns(table_ref[...], sets_ref[...])
     )
     out_ref[...] = low(nn(jnp.concatenate([hidden, u_down], axis=1), joined[...]))
-    accumulate(down_grad_ref, tn(du_ref[...], rows_ref[...]), first)
-    accumulate(res_grad_ref, tn(u_down, grad_ref[...]), first)
-    accumulate(up_grad_ref.at[0], tn(inner[:, :low_rank], ff_grad_ref[:, :padded]), first)
-    accumulate(up_grad_ref.at[1], tn(inner[:, low_rank:], ff_grad_ref[:, padded:]), first)
-    accumulate(ffd_grad_ref, tn(du_down_ref[...], hidden), first)
+    accumulate(down_sum, tn(du_ref[...], rows_ref[...]), first)
+    accumulate(res_sum, tn(u_down, grad_ref[...]), first)
+    for k, grown in enumerate(
+        (
+            tn(inner[:, :low_rank], ff_grad_ref[:, :padded]),
+            tn(inner[:, low_rank:], ff_grad_ref[:, padded:]),
+            tn(du_down_ref[...], hidden),
+        )
+    ):
+        accumulate(flat_sum.at[:, k * padded : (k + 1) * padded], grown, first)
+
+    @at_end
+    def _():
+        flat_ref[...] = low(flat_sum[...])
+        emit_blocks(
+            (down_sum.at[:low_rank], down_sum.at[low_rank:], res_sum),
+            place_ref[0], own_ref, far_ref, pair_ref,
+        )
 
 
 def branch_kernel(
@@ -896,13 +924,19 @@
 
 def branch_after_kernel(
     branch_ref, z_ref, u_out_ref, rows_ref, inner_ref, du_out_ref, du_gate_ref, gate_grad_ref,
-    down_grad_ref, res_grad_ref, out_grad_ref, up_grad_ref,
+    down_grad_ref, res_grad_ref, flat_ref,
+    flat_sum,
 ):
     first = pl.program_id(0) == 0
+    lanes = z_ref.shape[1]
     accumulate(down_grad_ref, tn(du_gate_ref[...], rows_ref[...]), first)
     accumulate(res_grad_ref, tn(u_out_ref[...], branch_ref[...]), first)
-    accumulate(out_grad_ref, tn(du_out_ref[...], z_ref[...]), first)
-    accumulate(up_grad_ref, tn(inner_ref[...], gate_grad_ref[...]), first)
+    accumulate(flat_sum.at[:, :lanes], tn(du_out_ref[...], z_ref[...]), first)
+    accumulate(flat_sum.at[:, lanes:], tn(inner_ref[...], gate_grad_ref[...]), first)
+
+    @at_end
+    def _():
+        flat_ref[...] = low(flat_sum[...])
 
 
 def settled_rows(pre_ref, tail_ref, arrived_ref, place_ref, quarters, window):
@@ -919,9 +953,9 @@
 
 def settle_grads_kernel(
     pre_ref, rows_ref, inner_ref, table_ref, tail_ref, arrived_ref, place_ref, sets_ref,
-    up_qk_ref, up_value_ref,
-    du_ref, down_grad_ref, up_qk_grad_ref, up_v_grad_ref,
-    window,
+    up_qk_ref, up_value_ref, down_late_ref, res_late_ref,
+    du_ref, own_ref, far_ref, pair_ref, flat_ref,
+    window, down_sum, flat_sum,
 ):
     first = pl.program_id(0) == 0
     low_rank = sets_ref.shape[1]
@@ -939,10 +973,24 @@
         axis=1,
     )
     du_ref[...] = du
-    accumulate(down_grad_ref, tn(du, rows_ref[...]), first)
-    accumulate(up_qk_grad_ref.at[0], tn(inner[:, :low_rank], query), first)
-    accumulate(up_qk_grad_ref.at[1], tn(inner[:, low_rank : 2 * low_rank], key), first)
-    accumulate(up_v_grad_ref, tn(inner[:, 2 * low_rank : 3 * low_rank], value), first)
+    accumulate(down_sum, tn(du, rows_ref[...]), first)
+    at = 0
+    for p, part in enumerate((query, key, value)):
+        accumulate(
+            flat_sum.at[:, at : at + part.shape[1]],
+            tn(inner[:, p * low_rank : (p + 1) * low_rank], part),
+            first,
+        )
+        at += part.shape[1]
+
+    @at_end
+    def _():
+        flat_ref[...] = low(flat_sum[...])
+        emit_blocks(
+            [down_sum.at[p * low_rank : (p + 1) * low_rank] for p in range(3)]
+            + [down_late_ref, res_late_ref],
+            place_ref[0], own_ref, far_ref, pair_ref,
+        )
 
 
 def settle_kernel(
@@ -970,6 +1018,56 @@
         nt(jnp.concatenate([pre, gate_grad_ref[...]], axis=1), joined[...])
         + nn(small, down_mix_ref[...])
     )
+
+
+def assemble_kernel(
+    place_ref, own_ref, near_ref, far_ref, corner_ref, last_ref, feed_ref, branch_ref,
+    down_ref, qk_ref, vg_ref, ff_ref, out_ref, ffd_ref, res_ref,
+):
+    place = place_ref[0]
+    size = own_ref.shape[1] // 8
+    targets = [down_ref.at[p] for p in range(4)] + [res_ref.at[0]]
+    targets += [down_ref.at[4], down_ref.at[5], res_ref.at[1]]
+    for relative, piece in enumerate((own_ref, near_ref, far_ref, corner_ref)):
+        start = pl.multiple_of((place ^ relative) * size, 128)
+        for k, target in enumerate(targets):
+            target[:, pl.ds(start, size)] = piece[:, k * size : (k + 1) * size].astype(single)
+    last = last_ref[...].astype(single)
+    qk, values = qk_ref.shape[2], vg_ref.shape[2]
+    qk_ref[0], qk_ref[1] = last[:, :qk], last[:, qk : 2 * qk]
+    vg_ref[0] = last[:, 2 * qk :]
+    branch = branch_ref[...].astype(single)
+    out_ref[...] = branch[:, :values]
+    vg_ref[1] = branch[:, values:]
+    hidden = ff_ref.shape[2]
+    padded = feed_ref.shape[1] // 3
+    feed = feed_ref[...].astype(single)
+    ff_ref[0] = feed[:, :hidden]
+    ff_ref[1] = feed[:, padded : padded + hidden]
+    ffd_ref[...] = feed[:, 2 * padded : 2 * padded + hidden]
+
+
+def assemble(where, shared, last, feed, branch, shapes):
+    rows = last.shape[0]
+    block = min(32, rows)
+
+    def spec(shape):
+        if len(shape) == 2:
+            return pl.BlockSpec((block, shape[1]), lambda i: (i, 0))
+        return pl.BlockSpec((shape[0], block, shape[2]), lambda i: (0, i, 0))
+
+    arrays = [*shared, last, feed, branch]
+    return pl.pallas_call(
+        assemble_kernel,
+        out_shape=tuple(jax.ShapeDtypeStruct(shape, single) for shape in shapes),
+        grid=(rows // block,),
+        in_specs=[pl.BlockSpec(memory_space=pltpu.SMEM)] + [spec(a.shape) for a in arrays],
+        out_specs=[spec(shape) for shape in shapes],
+        compiler_params=pltpu.CompilerParams(
+            dimension_semantics=("arbitrary",), vmem_limit_bytes=VMEM_LIMIT
+        ),
+        name="assemble",
+    )(where, *arrays)
 
 
 WHOLE, SCALAR = "whole", "scalar"
@@ -1132,46 +1230,22 @@
     return lax.ppermute(array, axis, pairs)
 
 
-def head_blocks(parts):
-    place = lax.axis_index("head")
-
-    def block(relative):
-        blocks = []
-        for part in parts:
-            size = part.shape[1] // 4
-            blocks.append(
-                low(lax.dynamic_slice_in_dim(part, (place ^ relative) * size, size, 1))
-            )
-        return jnp.concatenate(blocks, axis=1)
-
-    return block(0), block(2), jnp.concatenate([block(1), block(3)], axis=0)
-
-
-def seq_parts(flat):
+def seq_rows(flat):
     members = lax.axis_size("seq")
-    rows, lanes = flat.shape
-    return lax.all_to_all(flat.reshape(members, rows // members, lanes), "seq", 0, 0)
-
-
-def seq_spread(parts):
-    members, rows, lanes = parts.shape
+    return flat.reshape(members, flat.shape[0] // members, flat.shape[1])
+
+
+def share_sum(parts):
     summed = low(jnp.sum(parts.astype(single), axis=0))
-    spread = jnp.broadcast_to(summed[None], parts.shape)
-    return lax.all_to_all(spread, "seq", 0, 0).reshape(members * rows, lanes)
-
-
-def head_spread(piece, count):
-    place = lax.axis_index("head")
-    far = flip(piece, 2)
-    blocks = jnp.stack([piece, flip(piece, 1), far, flip(far, 1)])
-    ordered = [lax.dynamic_index_in_dim(blocks, place ^ b, 0, False) for b in range(4)]
-    size = piece.shape[1] // count
-    return [
-        jnp.concatenate(
-            [o[:, k * size : (k + 1) * size].astype(single) for o in ordered], axis=1
-        )
-        for k in range(count)
-    ]
+    return jnp.broadcast_to(summed[None], parts.shape)
+
+
+def exchange(parts):
+    return lax.all_to_all(parts, "seq", 0, 0)
+
+
+def all_rows(parts):
+    return parts.reshape(-1, parts.shape[-1])
 
 
 def rms_scale(rows, gain):
@@ -1276,6 +1350,7 @@
     hidden_width = w_down.shape[0]
     padded = -(-hidden_width // 256) * 256
     value_lanes = heads * value_width
+    block_width = width // groups
     widen = lambda a: jnp.pad(a, [(0, 0)] * (a.ndim - 1) + [(0, padded - hidden_width)])
     up_ff_padded, down_ffd_padded = widen(up_ff), widen(down_ffd)
 
@@ -1320,7 +1395,7 @@
         count * 9_000_000,
     )
     out_grad_late, pre = tie(out_grad, pre)
-    grad_all = gather_rows(out_grad_late)
+    grad_near, grad_far = flip(out_grad_late, 1), flip(out_grad_late, 2)
     raw_local, mapped, *saved, sent, sent_state, sent_map = run_forward(
         where, pre, pre_halo, columns, conv, scalars, heads, key_width, value_width, quarter
     )
@@ -1328,7 +1403,8 @@
     hops = min(members - 1, -(-(DOC_MAX - 1) // count))
     got = [shifted_along(sent, "seq", hop) for hop in range(1, hops)]
     got.append(shifted_along(sent_state, "seq", hops))
-    *grad_all, sent_map = tie(*grad_all, sent_map)
+    grad_near, grad_far, sent_map = tie(grad_near, grad_far, sent_map)
+    grad_all = [out_grad, grad_near, grad_far, flip(grad_far, 1)]
     hidden_grad, du_down = blocked_call(
         feed_before_kernel,
         "feed_before",
@@ -1373,11 +1449,14 @@
         [pltpu.VMEM((value_lanes + low_rank, width), bfloat)],
         count * 5_000_000,
     )
-    residual = input_float + far_sum(*near_sum(attention_part))
+    attention_own, attention_far = near_sum(attention_part)
+    attention_far, sent_map = tie(attention_far, sent_map)
+    maps_after = [shifted_along(sent_map, "seq", -hop) for hop in range(1, hops)]
+    residual = input_float + far_sum(attention_own, attention_far)
     normed_mid = low(rms_scale(residual, norm2_gain))
     mid_all = gather_rows(normed_mid)
-    normed_mid_done, sent_map = tie(mid_all[3], sent_map)
-    mid_all = mid_all[:3] + [normed_mid_done]
+    corner_mid, *maps_after = tie(mid_all[3], *maps_after)
+    mid_all = mid_all[:3] + [corner_mid]
 
     mid_part, hidden, ff_grad, u_ff, du_ff = blocked_call(
         feed_kernel,
@@ -1411,7 +1490,7 @@
     mid_own, mid_far = near_sum(mid_part)
     mid_far, hidden = tie(mid_far, hidden)
     mid_grad = far_sum(mid_own, mid_far)
-    out_part, feed_down_grad, feed_res_grad, feed_up_grad, ffd_grad = blocked_call(
+    out_part, feed_own, feed_far, feed_pair, feed_owned = blocked_call(
         feed_after_kernel,
         "feed_after",
         count,
@@ -1425,38 +1504,36 @@
             (du_down, by_rows(low_rank)),
             (table, by_rows(8)),
             (column_sets, WHOLE),
+            (where, SCALAR),
             (w_down, WHOLE),
             (down_ffd_padded, WHOLE),
             (up_res[1], WHOLE),
         ],
         [
             ((count, width), bfloat, "parts"),
-            ((2 * low_rank, width), single, "whole"),
-            ((low_rank, width), single, "whole"),
-            ((2, low_rank, padded), single, "whole"),
-            ((low_rank, padded), single, "whole"),
-        ],
-        [pltpu.VMEM((padded + low_rank, width), bfloat)],
+            ((low_rank, 3 * block_width), bfloat, "whole"),
+            ((low_rank, 3 * block_width), bfloat, "whole"),
+            ((2 * low_rank, 3 * block_width), bfloat, "whole"),
+            ((low_rank, 3 * padded), bfloat, "whole"),
+        ],
+        [
+            pltpu.VMEM((padded + low_rank, width), bfloat),
+            pltpu.VMEM((2 * low_rank, width), single),
+            pltpu.VMEM((low_rank, width), single),
+            pltpu.VMEM((low_rank, 3 * padded), single),
+        ],
         count * 12_000_000,
     )
     residual_grad = out_grad.astype(single) + rms_back(residual, norm2_gain, mid_grad)
+    out_own, out_far = near_sum(out_part)
     branch_low = low(residual_grad)
     branch_all = gather_rows(branch_low)
-    feed_own, feed_far = near_sum(
-        head_blocks([feed_down_grad[:low_rank], feed_down_grad[low_rank:], feed_res_grad])
-    )
     feed_flat = jnp.concatenate(
-        [
-            low(far_sum(feed_own, feed_far)),
-            low(feed_up_grad[0]),
-            low(feed_up_grad[1]),
-            low(ffd_grad),
-        ],
-        axis=1,
-    )
-    corner, feed_flat = tie(branch_all[3], feed_flat)
-    branch_all = branch_all[:3] + [corner]
-    feed_parts = seq_parts(feed_flat)
+        [low(far_sum(*near_sum((feed_own, feed_far, feed_pair)))), feed_owned], axis=1
+    )
+    corner_branch, feed_flat = tie(branch_all[3], feed_flat)
+    branch_all = branch_all[:3] + [corner_branch]
+    feed_parts = exchange(seq_rows(feed_flat))
 
     raw_grad, gate_grad, du_out, du_outgate, state_grad = blocked_call(
         functools.partial(branch_kernel, **sizes),
@@ -1489,10 +1566,9 @@
         ],
         count * 7_000_000,
     )
-    feed_parts, state_grad = tie(feed_parts, state_grad)
-    maps_after = [shifted_along(sent_map, "seq", -hop) for hop in range(1, hops)]
     state_got = [shifted_along(state_grad, "seq", -hop) for hop in range(1, hops + 1)]
-    mixer_down_late, branch_res_grad, out_down_grad, outgate_up_grad = blocked_call(
+    du_out, feed_parts = tie(du_out, feed_parts)
+    mixer_down_late, branch_res_grad, branch_flat = blocked_call(
         branch_after_kernel,
         "branch_after",
         count,
@@ -1509,40 +1585,33 @@
         [
             ((low_rank, width), single, "whole"),
             ((low_rank, width), single, "whole"),
-            ((low_rank, value_lanes), single, "whole"),
-            ((low_rank, value_lanes), single, "whole"),
-        ],
-        [],
-        count * 3_000_000,
-    )
-    branch_flat = jnp.concatenate(
-        [
-            low(far_sum(*near_sum(head_blocks([mixer_down_late, branch_res_grad])))),
-            low(out_down_grad),
-            low(outgate_up_grad),
-        ],
-        axis=1,
-    )
-    out_own, out_far = near_sum(out_part)
-    raw_grad, branch_flat, feed_parts, out_far = tie(raw_grad, branch_flat, feed_parts, out_far)
-    result = residual + far_sum(out_own, out_far)
-    feed_total = seq_spread(feed_parts)
-    branch_parts = seq_parts(branch_flat)
+            ((low_rank, 2 * value_lanes), bfloat, "whole"),
+        ],
+        [pltpu.VMEM((low_rank, 2 * value_lanes), single)],
+        count * 20_000_000,
+    )
+    feed_lanes = feed_parts.shape[-1]
+    both = jnp.concatenate([share_sum(feed_parts), seq_rows(branch_flat)], axis=2)
+    raw_grad, both, out_far, *state_got = tie(raw_grad, both, out_far, *state_got)
+    out_arrived = flip(out_far, 2)
+    both = exchange(both)
 
     pre_grad, mix_grad, tail_grad, edge_grad = run_backward(
         where, pre, pre_halo, columns, conv, scalars, raw_grad, saved, entering, state_got,
         maps_after, heads, key_width, value_width, quarter,
     )
     arrived = shifted_along(edge_grad, "seq", -1)
-    arrived, feed_total, branch_parts = tie(arrived, feed_total, branch_parts)
-    branch_total = seq_spread(branch_parts)
+    arrived, both, out_arrived = tie(arrived, both, out_arrived)
+    result = residual + (out_own + out_arrived.astype(single))
+    feed_total = all_rows(both[:, :, :feed_lanes])
+    branch_parts = both[:, :, feed_lanes:]
     settled = [
         (pre_grad, by_rows(2 * qk + value_lanes)),
         (tail_grad, WHOLE),
         (arrived, WHOLE),
         (where, SCALAR),
     ]
-    du_mix, mixer_down_grad, up_qk_grad, up_v_grad = blocked_call(
+    du_mix, last_own, last_far, last_pair, last_owned = blocked_call(
         settle_grads_kernel,
         "settle_grads",
         count,
@@ -1555,19 +1624,24 @@
             (column_sets, WHOLE),
             (up_qk, WHOLE),
             (up_vg[0], WHOLE),
+            (mixer_down_late, WHOLE),
+            (branch_res_grad, WHOLE),
         ],
         [
             ((count, 3 * low_rank), bfloat, "rows"),
-            ((3 * low_rank, width), single, "whole"),
-            ((2, low_rank, qk), single, "whole"),
-            ((low_rank, value_lanes), single, "whole"),
-        ],
-        [pltpu.VMEM((STEP, 2 * qk + value_lanes), bfloat)],
+            ((low_rank, 5 * block_width), bfloat, "whole"),
+            ((low_rank, 5 * block_width), bfloat, "whole"),
+            ((2 * low_rank, 5 * block_width), bfloat, "whole"),
+            ((low_rank, 2 * qk + value_lanes), bfloat, "whole"),
+        ],
+        [
+            pltpu.VMEM((STEP, 2 * qk + value_lanes), bfloat),
+            pltpu.VMEM((3 * low_rank, width), single),
+            pltpu.VMEM((low_rank, 2 * qk + value_lanes), single),
+        ],
         count * 4_000_000,
     )
-    last_own, last_far = near_sum(
-        head_blocks([mixer_down_grad[p * low_rank : (p + 1) * low_rank] for p in range(3)])
-    )
+    last_own, last_far = near_sum((last_own, last_far, last_pair))
     last_far, gate_grad = tie(last_far, gate_grad)
     (normed_part,) = blocked_call(
         settle_kernel,
@@ -1593,58 +1667,49 @@
         ],
         count * 10_000_000,
     )
-    last_flat = jnp.concatenate(
-        [
-            low(far_sum(last_own, last_far)),
-            low(up_qk_grad[0]),
-            low(up_qk_grad[1]),
-            low(up_v_grad),
-        ],
-        axis=1,
-    )
-    last_parts = seq_parts(last_flat)
+    last_flat = jnp.concatenate([low(far_sum(last_own, last_far)), last_owned], axis=1)
+    last_lanes = last_flat.shape[1]
+    both = exchange(jnp.concatenate([seq_rows(last_flat), share_sum(branch_parts)], axis=2))
+    last_parts, branch_total = both[:, :, :last_lanes], all_rows(both[:, :, last_lanes:])
     normed_grad = far_sum(*near_sum(normed_part))
     input_grad = residual_grad + rms_back(input_float, norm1_gain, normed_grad)
-    last_total = seq_spread(last_parts)
-    block_width = width // groups
-    shared = head_spread(
-        jnp.concatenate(
-            [
-                last_total[:, : 3 * block_width],
-                branch_total[:, : 2 * block_width],
-                feed_total[:, : 3 * block_width],
-            ],
-            axis=1,
-        ),
-        8,
-    )
-
-    def lanes_of(total, start, size):
-        return total[:, start : start + size].astype(single)
-
-    owned_qk = [lanes_of(last_total, 3 * block_width + k * qk, qk) for k in range(2)]
-    owned_value = lanes_of(last_total, 3 * block_width + 2 * qk, value_lanes)
-    owned_out = lanes_of(branch_total, 2 * block_width, value_lanes)
-    owned_outgate = lanes_of(branch_total, 2 * block_width + value_lanes, value_lanes)
-    owned_ff = [lanes_of(feed_total, 3 * block_width + k * padded, hidden_width) for k in range(2)]
-    owned_ffd = lanes_of(feed_total, 3 * block_width + 2 * padded, hidden_width)
+    last_total = all_rows(exchange(share_sum(last_parts)))
+    piece = jnp.concatenate(
+        [last_total[:, : 5 * block_width], feed_total[:, : 3 * block_width]], axis=1
+    )
+    down_grad, qk_grad, vg_grad, ff_grads, out_grads, ffd_grads, res_grad = assemble(
+        where,
+        gather_rows(piece),
+        last_total[:, 5 * block_width :],
+        feed_total[:, 3 * block_width :],
+        branch_total,
+        [
+            (6, low_rank, width),
+            (2, low_rank, qk),
+            (2, low_rank, value_lanes),
+            (2, low_rank, hidden_width),
+            (low_rank, value_lanes),
+            (low_rank, hidden_width),
+            (2, low_rank, width),
+        ],
+    )
 
     def as_down(rows):
-        return rows.reshape(sets, rank, -1).transpose(0, 2, 1)
+        return rows.reshape(rows.shape[:-2] + (sets, rank, -1)).swapaxes(-1, -2)
 
     def as_up(rows):
-        return rows.reshape(sets, rank, -1)
+        return rows.reshape(rows.shape[0], sets, rank, -1)
 
     return (
         low(result),
         input_grad,
-        jnp.stack([as_down(shared[k]) for k in (0, 1, 2, 3, 5, 6)]),
-        jnp.stack([as_up(part) for part in owned_qk]),
-        jnp.stack([as_up(owned_value), as_up(owned_outgate)]),
-        jnp.stack([as_up(part) for part in owned_ff]),
-        as_down(owned_out),
-        as_down(owned_ffd),
-        jnp.stack([as_up(shared[4]), as_up(shared[7])]),
+        as_down(down_grad),
+        as_up(qk_grad),
+        as_up(vg_grad),
+        as_up(ff_grads),
+        as_down(out_grads),
+        as_down(ffd_grads),
+        as_up(res_grad),
     )
 
 

time: 445 us -> 379 us (0.85); the launches traced: 437 us -> 377 us
  waiting for transfers between devices: 143 us -> 114 us
  starting transfers between devices: 89.6 us -> 69.9 us
  local copies, waits for them, and re-layouts: 30.7 us -> 22 us
  other arithmetic: 40.3 us -> 32.9 us
  Pallas kernels: 131 us -> 137 us
    all_to_all x6 -> x4, starting transfers between devices: 36.8 us -> 20.2 us  [exchange(): return lax.all_to_all(parts, 'seq', 0, 0)]
    ppermute x12, waiting for transfers between devices: 37.7 us -> 26.4 us  [shifted_along(): return lax.ppermute(array, axis, pairs)]
    ppermute x29 -> x27, waiting for transfers between devices: 76.5 us -> 67.6 us  [flip(): return lax.ppermute(array, 'head', [(i, i ^ bit) for i in range(groups)])]
    all_to_all x6 -> x4, waiting for transfers between devices: 28.7 us -> 20.2 us  [exchange(): return lax.all_to_all(parts, 'seq', 0, 0)]
    another operation x9 -> x0, other arithmetic: 6.91 us -> none  [the longest x1 2.08 us: on_device(): jnp.stack([as_down(shared[k]) for k in (0, 1, 2, 3, 5, 6)])]
    pallas_call x0 -> x1, Pallas kernels: none -> 5.06 us  [assemble(): pl.pallas_call(assemble_kernel, out_shape=tuple((jax.ShapeDtypeStruct(sha...]
    convert_element_type x9 -> x0, local copies, waits for them, and re-layouts: 4.52 us -> none  [low(): return array.astype(bfloat)]
    ppermute x29 -> x27, starting transfers between devices: 26 us -> 23.2 us  [flip(): return lax.ppermute(array, 'head', [(i, i ^ bit) for i in range(groups)])]
  transfers between devices with their start and end apart: 51 -> 47, of which waited for: 22 -> 19; matrix products, arithmetic and copies ran while one was open for 12% -> 11% of each run, Pallas kernels for 20% -> 23%
where the time goes in v2:
time: 379 us; the launch traced here: 377 us
  Pallas kernels  137 us (36%)
  waiting for transfers between devices  114 us (30%)
  starting transfers between devices  69.9 us (18%)
  other arithmetic  32.9 us (9%)
  local copies, waits for them, and re-layouts  22 us (6%)
    pallas_call x9, Pallas kernels, blocked_call(): pl.pallas_call(wrapped, out_shape=tuple(shapes), grid=(steps,), in_specs=...  89.3 us
    ppermute x27, waiting for transfers between devices, flip(): return lax.ppermute(array, 'head', [(i, i ^ bit) for i in range(groups)])  67.6 us
    ppermute x12, waiting for transfers between devices, shifted_along(): return lax.ppermute(array, axis, pairs)  26.4 us
    ppermute x12, starting transfers between devices, shifted_along(): return lax.ppermute(array, axis, pairs)  23.8 us
    ppermute x27, starting transfers between devices, flip(): return lax.ppermute(array, 'head', [(i, i ^ bit) for i in range(groups)])  23.2 us
    pallas_call x1, Pallas kernels, run_backward(): pl.pallas_call(body, out_shape=shapes, grid_spec=pltpu.PrefetchScalarGrid...  21.8 us
    pallas_call x1, Pallas kernels, run_forward(): pl.pallas_call(body, out_shape=shapes, grid_spec=pltpu.PrefetchScalarGrid...  20.6 us
    all_to_all x4, starting transfers between devices, exchange(): return lax.all_to_all(parts, 'seq', 0, 0)  20.2 us
  transfers between devices with their start and end apart: 47, of which 19 were waited for; matrix products, arithmetic and copies ran while one was open for 11% of the time, Pallas kernels for 23%

profile of v2, /device:TPU:0, one launch (start us, length us, event | category | flops | bytes accessed | tf_op | source)
XLA Modules:
  0.0 377.4 jit_solution(17897823200885519303)
XLA Ops:
  25.5 11.8 %project.1 = (bf16[1024,1024]{1,0:T(8,128)(2,1)}, f32[1024,512]{1,0:T(8,128)}, bf16[1024,512]{1,0:T(8,128)(2,1)}, f32[1024,8]{1,0:T(8,128)}, bf16[16,1024]{1,0:T(8,128)(2,1)}) custom-call(bf16[256,1024]{1,0:T(8,128)(2,1)} %copy-done.8, bf16[256,1024]{1,0:T(8,128)(2,1)} %collective-permute-done.refs_1_.refs_7_.refs_2_, ...), custom_call_target="tpu_custom_call" | custom-call | flops 9216000000 | bytes 7016960 | tf_op jit(solution)/shard_map/project/pallas_call | solution.py:1178
  42.9 20.6 %delta_forward.1 = (f32[1024,512]{1,0:T(8,128)}, bf16[1024,256]{1,0:T(8,128)(2,1)}, bf16[1024,768]{1,0:T(8,128)(2,1)}, bf16[8,2,128,384]{3,2,1,0:T(8,128)(2,1)},...) custom-call(s32[1]{0:T(128)} %bitcast.place.refs_15_.refs_9_.refs_7_, ...), custom_call_target="tpu_custom_call" | custom-call | flops 2048000000 | bytes 10240000 | tf_op jit(solution)/shard_map/delta_forward/pallas_call | solution.py:515
  72.9 5.1 %collective-permute-start.12 = (bf16[2,128,384]{2,1,0:T(8,128)(2,1)}, bf16[2,128,384]{2,1,0:T(8,128)(2,1)S(1)}, u32[]{:S(2)}, u32[]{:S(2)}) collective-permute-start(bf16[2,128,384]{2,1,0:T(8,128)(2,1)} %get-tuple-element.116), channel_id=1, source_target_pairs={{0,12},{4,16},{8,20},{12,24},{16,28},{1,13},{5,17},{9,21},{13,25},... | collective-permute-start | bytes 589832 | tf_op jit(solution)/shard_map/ppermute | solution.py:1230
  80.3 6.9 %feed_before.1 = (f32[1024,768]{1,0:T(8,128)}, bf16[1024,128]{1,0:T(8,128)(2,1)}) custom-call(bf16[256,1024]{1,0:T(8,128)(2,1)} %refs_4_.1, bf16[256,1024]{1,0:T(8,128)(2,1)} %copy-done.36, bf16[256,1024]{1,0:T(8,128)(2,1)} %collective-permute-done.8.refs_2_.refs_6_, bf16[256,1024]{1,0:T(8,128)(2,1)} %copy-done.37, ...), custom_call_target="tpu_custom_call" | custom-call | flops 6144000000 | bytes 4018176 | tf_op jit(solution)/shard_map/feed_before/pallas_call | solution.py:1178
  88.1 8.6 %attend.1 = (bf16[256,1024]{1,0:T(8,128)(2,1)}, bf16[256,1024]{1,0:T(8,128)(2,1)}, bf16[512,1024]{1,0:T(8,128)(2,1)}, bf16[1024,512]{1,0:T(8,128)(2,1)}, bf16[10...) custom-call(f32[1024,512]{1,0:T(8,128)} %get-tuple-element.113.refs_0_.refs_4_, ...), custom_call_target="tpu_custom_call" | custom-call | flops 5120000000 | bytes 6926336 | tf_op jit(solution)/shard_map/attend/pallas_call | solution.py:1178
  101.1 13.8 %collective-permute-done.15 = bf16[256,1024]{1,0:T(8,128)(2,1)S(1)} collective-permute-done((bf16[256,1024]{1,0:T(8,128)(2,1)S(1)}, bf16[256,1024]{1,0:T(8,128)(2,1)S(1)}, u32[]{:S(2)}, u32[]{:S(2)}) %collective-permute-start.15) | collective-permute-done | bytes 524320 | tf_op jit(solution)/shard_map/ppermute | solution.py:1200
  116.6 13.2 %collective-permute-done.17.refs_2_ = bf16[256,1024]{1,0:T(8,128)(2,1)} collective-permute-done((bf16[256,1024]{1,0:T(8,128)(2,1)}, bf16[256,1024]{1,0:T(8,128)(2,1)}, u32[]{:S(2)}, u32[]{:S(2)}) %collective-permute-start.17) | collective-permute-done | bytes 524320 | tf_op jit(solution)/shard_map/ppermute | solution.py:1200
  138.9 8.5 %collective-permute-done.21.rest_6_ = bf16[2,128,128]{2,1,0:T(8,128)(2,1)} collective-permute-done((bf16[2,128,128]{2,1,0:T(8,128)(2,1)}, bf16[2,128,128]{2,1,0:T(8,128)(2,1)}, u32[]{:S(2)}, u32[]{:S(2)}) %collective-permute-start.21) | collective-permute-done | bytes 65568 | tf_op jit(solution)/shard_map/ppermute | solution.py:1230
  147.4 17.4 %feed.1 = (bf16[256,1024]{1,0:T(8,128)(2,1)}, bf16[256,1024]{1,0:T(8,128)(2,1)}, bf16[512,1024]{1,0:T(8,128)(2,1)}, bf16[1024,768]{1,0:T(8,128)(2,1)}, bf16[1024...) custom-call(bf16[256,1024]{1,0:T(8,128)(2,1)} %multiply_convert_fusion.refs_0_, ...), custom_call_target="tpu_custom_call" | custom-call | flops 15360000000 | bytes 9441280 | tf_op jit(solution)/shard_map/feed/pallas_call | solution.py:1178
  169.6 11.2 %feed_after.1 = (bf16[256,1024]{1,0:T(8,128)(2,1)}, bf16[256,1024]{1,0:T(8,128)(2,1)}, bf16[512,1024]{1,0:T(8,128)(2,1)}, bf16[128,768]{1,0:T(8,128)(2,1)}, bf16...) custom-call(bf16[256,1024]{1,0:T(8,128)(2,1)} %multiply_convert_fusion.refs_0_, ...), custom_call_target="tpu_custom_call" | custom-call | flops 12288000000 | bytes 12161028 | tf_op jit(solution)/shard_map/feed_after/pallas_call | solution.py:1178
  186.1 12.7 %collective-permute-done.26.refs_2_ = bf16[256,1024]{1,0:T(8,128)(2,1)S(1)} collective-permute-done((bf16[256,1024]{1,0:T(8,128)(2,1)S(1)}, bf16[256,1024]{1,0:T(8,128)(2,1)S(1)}, u32[]{:S(2)}, u32[]{:S(2)}) %collective-permute-start.26) | collective-permute-done | bytes 524320 | tf_op jit(solution)/shard_map/ppermute | solution.py:1200
  203.1 5.7 %all-to-all-start = ((bf16[8,16,3072]{2,1,0:T(8,128)(2,1)}), bf16[8,16,3072]{2,1,0:T(8,128)(2,1)S(1)}, u32[]{:S(2)}, u32[]{:S(2)}) async-start(bf16[8,16,3072]{2,1,0:T(8,128)(2,1)} %bitcast.55), calls=%async_computation | async-start | bytes 1572864 | tf_op jit(solution)/shard_map/all_to_all | solution.py:1244
  213.5 8.9 %branch.1 = (bf16[1024,512]{1,0:T(8,128)(2,1)}, bf16[1024,512]{1,0:T(8,128)(2,1)}, bf16[1024,128]{1,0:T(8,128)(2,1)}, bf16[1024,128]{1,0:T(8,128)(2,1)}, bf16[2,128,256]{2,1,0:T(8,128)(2,1)}) custom-call(bf16[256,1024]{1,0:T(8,128)(2,1)} %copy-done.13, bf16[256,1024]{1,0:T(8,128)(2,1)} %collective-permute-done.25.refs_1_, bf16[256,1024]{1,0:T(8,128)(2,1)} %copy-done.38, ...), custom_call_target="tpu_custom_call" | custom-call | flops 7168000000 | bytes 8564736 | tf_op jit(solution)/shard_map/branch/pallas_call | solution.py:1178
  227.9 6.2 %branch_after.1 = (f32[128,1024]{1,0:T(8,128)}, f32[128,1024]{1,0:T(8,128)}, bf16[128,1024]{1,0:T(8,128)(2,1)}) custom-call(bf16[256,1024]{1,0:T(8,128)(2,1)} %copy-done.13, bf16[256,1024]{1,0:T(8,128)(2,1)} %collective-permute-done.25.refs_1_, bf16[256,1024]{1,0:T(8,128)(2,1)} %copy-done.38, bf16[256,1024]{1,0:T(8,128)(2,1)} %copy-done.39, ...), custom_call_target="tpu_custom_call" | custom-call | flops 20480000000 | bytes 8126464 | tf_op jit(solution)/shard_map/branch_after/pallas_call | solution.py:1178
  236.7 10.2 %collective-permute-done.33.rest_3_ = bf16[2,128,256]{2,1,0:T(8,128)(2,1)} collective-permute-done((bf16[2,128,256]{2,1,0:T(8,128)(2,1)}, bf16[2,128,256]{2,1,0:T(8,128)(2,1)}, u32[]{:S(2)}, u32[]{:S(2)}) %collective-permute-start.33) | collective-permute-done | bytes 131104 | tf_op jit(solution)/shard_map/ppermute | solution.py:1230
  251.8 21.8 %delta_backward.1 = (bf16[1024,1024]{1,0:T(8,128)(2,1)}, f32[1024,8]{1,0:T(8,128)}, f32[16,1024]{1,0:T(8,128)}, f32[16,1024]{1,0:T(8,128)}) custom-call(s32[1]{0:T(128)} %bitcast.place.refs_15_.refs_9_.refs_7_.place_ref, bf16[1024,1024]{1,0:T(8,128)(2,1)} %get-tuple-element.104.rows_ref.before_ref, ...), custom_call_target="tpu_custom_call" | custom-call | flops 3072000000 | bytes 12288000 | tf_op jit(solution)/shard_map/delta_backward/pallas_call | solution.py:588
  275.0 5.1 %collective-permute-done.34.refs_8_.refs_6_ = f32[16,1024]{1,0:T(8,128)S(1)} collective-permute-done((f32[16,1024]{1,0:T(8,128)}, f32[16,1024]{1,0:T(8,128)S(1)}, u32[]{:S(2)}, u32[]{:S(2)}) %collective-permute-start.34) | collective-permute-done | bytes 65568 | tf_op jit(solution)/shard_map/ppermute | solution.py:1230
  280.7 8.0 %settle_grads.1 = (bf16[1024,384]{1,0:T(8,128)(2,1)}, bf16[128,1280]{1,0:T(8,128)(2,1)}, bf16[128,1280]{1,0:T(8,128)(2,1)}, bf16[256,1280]{1,0:T(8,128)(2,1)}, bf16[128,1024]{1,0:T(8,128)(2,1)}) custom-call(bf16[1024,1024]{1,0:T(8,128)(2,1)} %get-tuple-element.173.refs_0_, bf16[256,1024]{1,0:T(8,128)(2,1)} %copy-done.8, ...), custom_call_target="tpu_custom_call" | custom-call | flops 4096000000 | bytes 6721540 | tf_op jit(solution)/shard_map/settle_grads/pallas_call | solution.py:1178
  294.6 7.3 %collective-permute-done.39 = bf16[128,1280]{1,0:T(8,128)(2,1)S(1)} collective-permute-done((bf16[128,1280]{1,0:T(8,128)(2,1)S(1)}, bf16[128,1280]{1,0:T(8,128)(2,1)S(1)}, u32[]{:S(2)}, u32[]{:S(2)}) %collective-permute-start.39) | collective-permute-done | bytes 327712 | tf_op jit(solution)/shard_map/ppermute | solution.py:1200
  304.1 5.8 %all-to-all-start.2 = ((bf16[8,16,3328]{2,1,0:T(8,128)(2,1)}), bf16[8,16,3328]{2,1,0:T(8,128)(2,1)S(1)}, u32[]{:S(2)}, u32[]{:S(2)}) async-start(bf16[8,16,3328]{2,1,0:T(8,128)(2,1)} %pad_maximum_fusion.1), calls=%async_computation.2 | async-start | bytes 1703936 | tf_op jit(solution)/shard_map/all_to_all | solution.py:1244
  309.9 10.3 %settle.1 = (bf16[256,1024]{1,0:T(8,128)(2,1)}, bf16[256,1024]{1,0:T(8,128)(2,1)}, bf16[512,1024]{1,0:T(8,128)(2,1)}) custom-call(bf16[1024,1024]{1,0:T(8,128)(2,1)} %get-tuple-element.173.refs_0_, bf16[1024,512]{1,0:T(8,128)(2,1)} %get-tuple-element.180.refs_13_.refs_1_, bf16[1024,384]{1,0:T(8,128)(2,1)} %get-tuple-element.181.refs_2_, ...), custom_call_target="tpu_custom_call" | custom-call | flops 10240000000 | bytes 8814596 | tf_op jit(solution)/shard_map/settle/pallas_call | solution.py:1178
  320.3 10.9 %all-to-all-done.2 = bf16[8,16,3328]{2,1,0:T(8,128)(2,1)S(1)} async-done(((bf16[8,16,3328]{2,1,0:T(8,128)(2,1)}), bf16[8,16,3328]{2,1,0:T(8,128)(2,1)S(1)}, u32[]{:S(2)}, u32[]{:S(2)}) %all-to-all-start.2) | async-done | bytes 852000 | tf_op jit(solution)/shard_map/all_to_all | solution.py:1244
  342.8 9.1 %all-to-all-done.3 = bf16[8,16,2304]{2,1,0:T(8,128)(2,1)} async-done(((bf16[8,16,2304]{2,1,0:T(8,128)(2,1)}), bf16[8,16,2304]{2,1,0:T(8,128)(2,1)}, u32[]{:S(2)}, u32[]{:S(2)}) %all-to-all-start.3) | async-done | bytes 589856 | tf_op jit(solution)/shard_map/all_to_all | solution.py:1244
  359.6 6.4 %collective-permute-done.41.far_ref = bf16[128,2048]{1,0:T(8,128)(2,1)S(1)} collective-permute-done((bf16[128,2048]{1,0:T(8,128)(2,1)S(1)}, bf16[128,2048]{1,0:T(8,128)(2,1)S(1)}, u32[]{:S(2)}, u32[]{:S(2)}) %collective-permute-start.41) | collective-permute-done | bytes 524320 | tf_op jit(solution)/shard_map/ppermute | solution.py:1200
  (246 shorter events, 130.1 us)
Async XLA Ops:
  3.3 18.5 %collective-permute-start.3 = (bf16[16,1024]{1,0:T(8,128)(2,1)S(1)}, bf16[16,1024]{1,0:T(8,128)(2,1)S(1)}, u32[]{:S(2)}, u32[]{:S(2)}) collective-permute-start(bf16[16,1024]{1,0:T(8,128)(2,1)S(1)} %slice.122), channel_id=1, source_target_pairs={{3,4},{7,8},{11,12},{15,16},{19,20},{23,24},{27,28}} | collective-permute-start | bytes 98312 | tf_op jit(solution)/shard_map/ppermute | solution.py:1361
  3.9 20.2 %collective-permute-start.4 = (bf16[16,1024]{1,0:T(8,128)(2,1)S(1)}, bf16[16,1024]{1,0:T(8,128)(2,1)S(1)}, u32[]{:S(2)}, u32[]{:S(2)}) collective-permute-start(bf16[16,1024]{1,0:T(8,128)(2,1)S(1)} %slice.122), channel_id=1, source_target_pairs={{3,5},{7,9},{11,13},{15,17},{19,21},{23,25},{27,29}} | collective-permute-start | bytes 98312 | tf_op jit(solution)/shard_map/ppermute | solution.py:1361
  4.6 19.6 %collective-permute-start.5 = (bf16[16,1024]{1,0:T(8,128)(2,1)S(1)}, bf16[16,1024]{1,0:T(8,128)(2,1)S(1)}, u32[]{:S(2)}, u32[]{:S(2)}) collective-permute-start(bf16[16,1024]{1,0:T(8,128)(2,1)S(1)} %slice.122), channel_id=1, source_target_pairs={{3,6},{7,10},{11,14},{15,18},{19,22},{23,26},{27,30}} | collective-permute-start | bytes 98312 | tf_op jit(solution)/shard_map/ppermute | solution.py:1361
  8.3 16.5 %collective-permute-start = (bf16[256,1024]{1,0:T(8,128)(2,1)S(1)}, bf16[256,1024]{1,0:T(8,128)(2,1)}, u32[]{:S(2)}, u32[]{:S(2)}) collective-permute-start(bf16[256,1024]{1,0:T(8,128)(2,1)S(1)} %fusion.4.refs_0_.refs_6_.refs_1_), channel_id=1, source_target_pairs={{0,1},{1,0},{2,3},{3,2},{4,5},{5,4},{6,7},{7,6},{8,9},{9,8},{10,11... | collective-permute-start | bytes 1572872 | tf_op jit(solution)/shard_map/ppermute | solution.py:1200
  37.3 26.3 %collective-permute-start.7 = (bf16[256,1024]{1,0:T(8,128)(2,1)S(1)}, bf16[256,1024]{1,0:T(8,128)(2,1)S(1)}, u32[]{:S(2)}, u32[]{:S(2)}) collective-permute-start(bf16[256,1024]{1,0:T(8,128)(2,1)S(1)} %copy-done.10), channel_id=1, source_target_pairs={{0,1},{1,0},{2,3},{3,2},{4,5},{5,4},{6,7},{7,6},{8,9},{9,8},{10,11... | collective-permute-start | bytes 1572872 | tf_op jit(solution)/shard_map/ppermute | solution.py:1200
  37.4 26.2 %collective-permute-start.8 = (bf16[256,1024]{1,0:T(8,128)(2,1)S(1)}, bf16[256,1024]{1,0:T(8,128)(2,1)}, u32[]{:S(2)}, u32[]{:S(2)}) collective-permute-start(bf16[256,1024]{1,0:T(8,128)(2,1)S(1)} %copy-done.10), channel_id=1, source_target_pairs={{0,2},{1,3},{2,0},{3,1},{4,6},{5,7},{6,4},{7,5},{8,10},{9,11},{10,... | collective-permute-start | bytes 1572872 | tf_op jit(solution)/shard_map/ppermute | solution.py:1200
  64.4 15.2 %collective-permute-start.9 = (bf16[256,1024]{1,0:T(8,128)(2,1)}, bf16[256,1024]{1,0:T(8,128)(2,1)S(1)}, u32[]{:S(2)}, u32[]{:S(2)}) collective-permute-start(bf16[256,1024]{1,0:T(8,128)(2,1)} %collective-permute-done.8.refs_2_.refs_6_), channel_id=1, source_target_pairs={{0,1},{1,0},{2,3},{3,2},{4,5},{5,4},{6,7},{7,6},{8,9},{9,8},{10,11... | collective-permute-start | bytes 1572872 | tf_op jit(solution)/shard_map/ppermute | solution.py:1200
  66.0 21.2 %collective-permute-start.10 = (bf16[2,128,384]{2,1,0:T(8,128)(2,1)}, bf16[2,128,384]{2,1,0:T(8,128)(2,1)S(1)}, u32[]{:S(2)}, u32[]{:S(2)}) collective-permute-start(bf16[2,128,384]{2,1,0:T(8,128)(2,1)} %get-tuple-element.116), channel_id=1, source_target_pairs={{0,4},{4,8},{8,12},{12,16},{16,20},{20,24},{24,28},{1,5},{5,9},{9,... | collective-permute-start | bytes 589832 | tf_op jit(solution)/shard_map/ppermute | solution.py:1230
  69.5 17.8 %collective-permute-start.11 = (bf16[2,128,384]{2,1,0:T(8,128)(2,1)}, bf16[2,128,384]{2,1,0:T(8,128)(2,1)S(1)}, u32[]{:S(2)}, u32[]{:S(2)}) collective-permute-start(bf16[2,128,384]{2,1,0:T(8,128)(2,1)} %get-tuple-element.116), channel_id=1, source_target_pairs={{0,8},{4,12},{8,16},{12,20},{16,24},{20,28},{1,9},{5,13},{9,17},{1... | collective-permute-start | bytes 589832 | tf_op jit(solution)/shard_map/ppermute | solution.py:1230
  72.9 14.3 %collective-permute-start.12 = (bf16[2,128,384]{2,1,0:T(8,128)(2,1)}, bf16[2,128,384]{2,1,0:T(8,128)(2,1)S(1)}, u32[]{:S(2)}, u32[]{:S(2)}) collective-permute-start(bf16[2,128,384]{2,1,0:T(8,128)(2,1)} %get-tuple-element.116), channel_id=1, source_target_pairs={{0,12},{4,16},{8,20},{12,24},{16,28},{1,13},{5,17},{9,21},{13,25},... | collective-permute-start | bytes 589832 | tf_op jit(solution)/shard_map/ppermute | solution.py:1230
  129.8 17.6 %collective-permute-start.18 = (bf16[256,1024]{1,0:T(8,128)(2,1)}, bf16[256,1024]{1,0:T(8,128)(2,1)}, u32[]{:S(2)}, u32[]{:S(2)}) collective-permute-start(bf16[256,1024]{1,0:T(8,128)(2,1)} %collective-permute-done.17.refs_2_), channel_id=1, source_target_pairs={{0,1},{1,0},{2,3},{3,2},{4,5},{5,4},{6,7},{7,6},{8,9},{9,8},{10,11... | collective-permute-start | bytes 1572872 | tf_op jit(solution)/shard_map/ppermute | solution.py:1200
  129.8 17.6 %collective-permute-start.16 = (bf16[256,1024]{1,0:T(8,128)(2,1)}, bf16[256,1024]{1,0:T(8,128)(2,1)}, u32[]{:S(2)}, u32[]{:S(2)}) collective-permute-start(bf16[256,1024]{1,0:T(8,128)(2,1)} %multiply_convert_fusion.refs_0_), channel_id=1, source_target_pairs={{0,1},{1,0},{2,3},{3,2},{4,5},{5,4},{6,7},{7,6},{8,9},{9,8},{10,11... | collective-permute-start | bytes 1572872 | tf_op jit(solution)/shard_map/ppermute | solution.py:1200
  132.9 14.5 %collective-permute-start.21 = (bf16[2,128,128]{2,1,0:T(8,128)(2,1)}, bf16[2,128,128]{2,1,0:T(8,128)(2,1)}, u32[]{:S(2)}, u32[]{:S(2)}) collective-permute-start(bf16[2,128,128]{2,1,0:T(8,128)(2,1)} %get-tuple-element.123), channel_id=1, source_target_pairs={{12,0},{16,4},{20,8},{24,12},{28,16},{13,1},{17,5},{21,9},{25,13},... | collective-permute-start | bytes 196616 | tf_op jit(solution)/shard_map/ppermute | solution.py:1230
  183.8 14.9 %collective-permute-start.26 = (bf16[256,1024]{1,0:T(8,128)(2,1)S(1)}, bf16[256,1024]{1,0:T(8,128)(2,1)S(1)}, u32[]{:S(2)}, u32[]{:S(2)}) collective-permute-start(bf16[256,1024]{1,0:T(8,128)(2,1)S(1)} %get-tuple-element.201.refs_0_), channel_id=1, source_target_pairs={{0,2},{1,3},{2,0},{3,1},{4,6},{5,7},{6,4},{7,5},{8,10},{9,11},{10,... | collective-permute-start | bytes 1572872 | tf_op jit(solution)/shard_map/ppermute | solution.py:1200
  184.6 16.7 %collective-permute-start.29 = (bf16[128,768]{1,0:T(8,128)(2,1)S(1)}, bf16[128,768]{1,0:T(8,128)(2,1)S(1)}, u32[]{:S(2)}, u32[]{:S(2)}) collective-permute-start(bf16[128,768]{1,0:T(8,128)(2,1)S(1)} %add_convert_fusion.8), channel_id=1, source_target_pairs={{0,2},{1,3},{2,0},{3,1},{4,6},{5,7},{6,4},{7,5},{8,10},{9,11},{10,... | collective-permute-start | bytes 589832 | tf_op jit(solution)/shard_map/ppermute | solution.py:1200
  186.0 25.3 %collective-permute-start.23 = (bf16[512,1024]{1,0:T(8,128)(2,1)}, bf16[512,1024]{1,0:T(8,128)(2,1)}, u32[]{:S(2)}, u32[]{:S(2)}) collective-permute-start(bf16[512,1024]{1,0:T(8,128)(2,1)} %get-tuple-element.135), channel_id=1, source_target_pairs={{0,1},{1,0},{2,3},{3,2},{4,5},{5,4},{6,7},{7,6},{8,9},{9,8},{10,11... | collective-permute-start | bytes 3145736 | tf_op jit(solution)/shard_map/ppermute | solution.py:1200
  203.1 24.6 %all-to-all-start = ((bf16[8,16,3072]{2,1,0:T(8,128)(2,1)}), bf16[8,16,3072]{2,1,0:T(8,128)(2,1)S(1)}, u32[]{:S(2)}, u32[]{:S(2)}) async-start(bf16[8,16,3072]{2,1,0:T(8,128)(2,1)} %bitcast.55), calls=%async_computation | async-start | bytes 1572864 | tf_op jit(solution)/shard_map/all_to_all | solution.py:1244
  226.3 20.6 %collective-permute-start.33 = (bf16[2,128,256]{2,1,0:T(8,128)(2,1)}, bf16[2,128,256]{2,1,0:T(8,128)(2,1)}, u32[]{:S(2)}, u32[]{:S(2)}) collective-permute-start(bf16[2,128,256]{2,1,0:T(8,128)(2,1)} %get-tuple-element.156), channel_id=1, source_target_pairs={{16,0},{20,4},{24,8},{28,12},{17,1},{21,5},{25,9},{29,13},{18,2},{... | collective-permute-start | bytes 393224 | tf_op jit(solution)/shard_map/ppermute | solution.py:1230
  246.9 33.1 %all-to-all-start.1 = ((bf16[8,16,4096]{2,1,0:T(8,128)(2,1)}), bf16[8,16,4096]{2,1,0:T(8,128)(2,1)}, u32[]{:S(2)}, u32[]{:S(2)}) async-start(bf16[8,16,4096]{2,1,0:T(8,128)(2,1)} %pad_maximum_fusion), calls=%async_computation.1 | async-start | bytes 2097152 | tf_op jit(solution)/shard_map/all_to_all | solution.py:1244
  251.2 28.9 %collective-permute-start.35 = (bf16[256,1024]{1,0:T(8,128)(2,1)S(1)}, bf16[256,1024]{1,0:T(8,128)(2,1)}, u32[]{:S(2)}, u32[]{:S(2)}) collective-permute-start(bf16[256,1024]{1,0:T(8,128)(2,1)S(1)} %copy-done.12), channel_id=1, source_target_pairs={{0,2},{1,3},{2,0},{3,1},{4,6},{5,7},{6,4},{7,5},{8,10},{9,11},{10,... | collective-permute-start | bytes 1572872 | tf_op jit(solution)/shard_map/ppermute | solution.py:1200
  304.1 27.0 %all-to-all-start.2 = ((bf16[8,16,3328]{2,1,0:T(8,128)(2,1)}), bf16[8,16,3328]{2,1,0:T(8,128)(2,1)S(1)}, u32[]{:S(2)}, u32[]{:S(2)}) async-start(bf16[8,16,3328]{2,1,0:T(8,128)(2,1)} %pad_maximum_fusion.1), calls=%async_computation.2 | async-start | bytes 1703936 | tf_op jit(solution)/shard_map/all_to_all | solution.py:1244
  320.2 19.1 %collective-permute-start.37 = (bf16[512,1024]{1,0:T(8,128)(2,1)}, bf16[512,1024]{1,0:T(8,128)(2,1)}, u32[]{:S(2)}, u32[]{:S(2)}) collective-permute-start(bf16[512,1024]{1,0:T(8,128)(2,1)} %get-tuple-element.184), channel_id=1, source_target_pairs={{0,1},{1,0},{2,3},{3,2},{4,5},{5,4},{6,7},{7,6},{8,9},{9,8},{10,11... | collective-permute-start | bytes 3145736 | tf_op jit(solution)/shard_map/ppermute | solution.py:1200
  332.1 19.9 %all-to-all-start.3 = ((bf16[8,16,2304]{2,1,0:T(8,128)(2,1)}), bf16[8,16,2304]{2,1,0:T(8,128)(2,1)}, u32[]{:S(2)}, u32[]{:S(2)}) async-start(bf16[8,16,2304]{2,1,0:T(8,128)(2,1)} %broadcast_in_dim.130), calls=%async_computation.3 | async-start | bytes 1179648 | tf_op jit(solution)/shard_map/all_to_all | solution.py:1244
  341.4 16.5 %collective-permute-start.38 = (bf16[256,1024]{1,0:T(8,128)(2,1)}, bf16[256,1024]{1,0:T(8,128)(2,1)}, u32[]{:S(2)}, u32[]{:S(2)}) collective-permute-start(bf16[256,1024]{1,0:T(8,128)(2,1)} %add_convert_fusion), channel_id=1, source_target_pairs={{0,2},{1,3},{2,0},{3,1},{4,6},{5,7},{6,4},{7,5},{8,10},{9,11},{10,... | collective-permute-start | bytes 1572872 | tf_op jit(solution)/shard_map/ppermute | solution.py:1200
  (68 other events, 632.1 us)

commit v3 on v2

--- a/solution.py
+++ b/solution.py
@@ -145,7 +145,6 @@
     end_ref,
     sent_ref,
     sent_state_ref,
-    sent_map_ref,
     window,
     state,
     *,
@@ -239,7 +238,6 @@
         end_ref[...] = final
         sent_ref[...] = low(final)
         sent_state_ref[...] = low(final[:, :, :value_width])
-        sent_map_ref[...] = low(final[:, :, value_width:])
 
 
 def backward_kernel(
@@ -262,7 +260,7 @@
     key_width,
     value_width,
 ):
-    got_refs, after_refs, rest = rest[:hops], rest[hops : 2 * hops - 1], rest[2 * hops - 1 :]
+    got_refs, rest = rest[:hops], rest[hops:]
     out_ref, mix_ref, tail_ref, edge_ref, window, shifted, shifted_start, cotangent, ahead = rest
     step = pl.program_id(0)
     steps = pl.num_programs(0)
@@ -278,11 +276,9 @@
         shifted[STEP : STEP + 8, :] = jnp.zeros((8, lanes), single)
         shifted_start[STEP : STEP + 8, :] = jnp.zeros((8, 1), jnp.int32)
         for h in range(heads):
-            passed = got_refs[hops - 1][h].astype(single)
-            for hop in range(hops - 1, 0, -1):
-                passed = got_refs[hop - 1][h].astype(single) + tn(
-                    after_refs[hop - 1][h], low(passed)
-                )
+            passed = got_refs[0][h].astype(single)
+            for hop in range(1, hops):
+                passed = passed + got_refs[hop][h].astype(single)
             cotangent[h] = passed
             ahead[h] = end_ref[h, :, :value_width] + nn(
                 low(end_ref[h, :, value_width:]), low(entering_ref[h])
@@ -510,7 +506,6 @@
         jax.ShapeDtypeStruct((heads, key_width, wide), single),
         jax.ShapeDtypeStruct((heads, key_width, wide), bfloat),
         jax.ShapeDtypeStruct((heads, key_width, value_width), bfloat),
-        jax.ShapeDtypeStruct((heads, key_width, key_width), bfloat),
     )
     return pl.pallas_call(
         body,
@@ -534,7 +529,6 @@
                 pl.BlockSpec((heads, key_width, wide), lambda i, place: (0, 0, 0)),
                 pl.BlockSpec((heads, key_width, wide), lambda i, place: (0, 0, 0)),
                 pl.BlockSpec((heads, key_width, value_width), lambda i, place: (0, 0, 0)),
-                pl.BlockSpec((heads, key_width, key_width), lambda i, place: (0, 0, 0)),
             ],
             scratch_shapes=[
                 pltpu.VMEM((STEP + HALO, lanes), single),
@@ -552,7 +546,7 @@
 
 
 def run_backward(
-    place, rows, halo, columns, weights, scalars, grad, saved, entering, got, after, heads,
+    place, rows, halo, columns, weights, scalars, grad, saved, entering, got, heads,
     key_width, value_width, quarter,
 ):
     written, states, inverses, end = saved
@@ -607,7 +601,7 @@
                 pl.BlockSpec(end.shape, whole),
                 pl.BlockSpec(entering.shape, whole),
             ]
-            + [pl.BlockSpec(part.shape, whole) for part in (*got, *after)],
+            + [pl.BlockSpec(part.shape, whole) for part in got],
             out_specs=[
                 pl.BlockSpec((STEP, lanes), at),
                 pl.BlockSpec((STEP, columns.shape[1]), at),
@@ -631,7 +625,7 @@
         name="delta_backward",
     )(
         place, rows, rows, halo, columns, weights, scalars, grad, written, states, inverses, end,
-        entering, *got, *after,
+        entering, *got,
     )
 
 
@@ -649,7 +643,10 @@
 
 
 def accumulate(ref, value, first):
-    ref[...] = jnp.where(first, value, ref[...] + value)
+    if first is True:
+        ref[...] = value
+    else:
+        ref[...] = jnp.where(first, value, ref[...] + value)
 
 
 def emit_blocks(parts, place, own_ref, far_ref, pair_ref):
@@ -872,11 +869,12 @@
 
 def branch_kernel(
     branch_ref, raw_ref, map_ref, gate_ref, table_ref, entering_ref, gain_ref, sets_ref, wo_ref,
-    down_out_t_ref, up_ref, up_gate_ref,
-    raw_grad_ref, gate_grad_ref, du_out_ref, du_gate_ref, state_grad_ref,
-    joined, total,
-    *, heads, key_width, value_width,
+    down_out_t_ref, up_ref, up_gate_ref, *rest,
+    heads, key_width, value_width, hops,
 ):
+    got_refs, rest = rest[: hops - 1], rest[hops - 1 :]
+    raw_grad_ref, gate_grad_ref, du_out_ref, du_gate_ref, *rest = rest
+    sent_refs, (joined, total) = rest[:hops], rest[hops:]
     first = pl.program_id(0) == 0
     width = wo_ref.shape[1]
 
@@ -917,9 +915,14 @@
     gate_grad_ref[...] = gate_grad
     du_gate_ref[...] = masked(nt(gate_grad, up_gate_ref[...]), chosen)
 
-    @pl.when(pl.program_id(0) == pl.num_programs(0) - 1)
-    def _():
-        state_grad_ref[...] = low(total[...])
+    @at_end
+    def _():
+        for h in range(heads):
+            passed = low(total[h])
+            sent_refs[0][h] = passed
+            for hop in range(1, hops):
+                passed = low(tn(got_refs[hop - 1][h][:, value_width:], passed))
+                sent_refs[hop][h] = passed
 
 
 def branch_after_kernel(
@@ -927,26 +930,25 @@
     down_grad_ref, res_grad_ref, flat_ref,
     flat_sum,
 ):
-    first = pl.program_id(0) == 0
     lanes = z_ref.shape[1]
-    accumulate(down_grad_ref, tn(du_gate_ref[...], rows_ref[...]), first)
-    accumulate(res_grad_ref, tn(u_out_ref[...], branch_ref[...]), first)
-    accumulate(flat_sum.at[:, :lanes], tn(du_out_ref[...], z_ref[...]), first)
-    accumulate(flat_sum.at[:, lanes:], tn(inner_ref[...], gate_grad_ref[...]), first)
+    accumulate(down_grad_ref, tn(du_gate_ref[...], rows_ref[...]), True)
+    accumulate(res_grad_ref, tn(u_out_ref[...], branch_ref[...]), True)
+    accumulate(flat_sum.at[:, :lanes], tn(du_out_ref[...], z_ref[...]), True)
+    accumulate(flat_sum.at[:, lanes:], tn(inner_ref[...], gate_grad_ref[...]), True)
 
     @at_end
     def _():
         flat_ref[...] = low(flat_sum[...])
 
 
-def settled_rows(pre_ref, tail_ref, arrived_ref, place_ref, quarters, window):
-    per_quarter = pl.num_programs(0) // quarters
-    last = ((quarters - 1) ^ place_ref[0]) * per_quarter + per_quarter - 1
+def settled_rows(pre_ref, tail_ref, arrived_ref, place_ref, quarter, window):
+    block = window.shape[0]
+    start = ((3 ^ place_ref[0]) + 1) * quarter - HALO - pl.program_id(0) * block
     window[...] = pre_ref[...]
 
-    @pl.when(pl.program_id(0) == last)
-    def _():
-        window[window.shape[0] - HALO :, :] = low(tail_ref[...] + arrived_ref[...])
+    @pl.when((start >= 0) & (start < block))
+    def _():
+        window[pl.ds(pl.multiple_of(start, HALO), HALO), :] = low(tail_ref[...] + arrived_ref[...])
 
     return window[...]
 
@@ -956,12 +958,12 @@
     up_qk_ref, up_value_ref, down_late_ref, res_late_ref,
     du_ref, own_ref, far_ref, pair_ref, flat_ref,
     window, down_sum, flat_sum,
+    *, quarter,
 ):
-    first = pl.program_id(0) == 0
     low_rank = sets_ref.shape[1]
     q_width = up_qk_ref.shape[2]
     chosen = chosen_columns(table_ref[...], sets_ref[...])
-    pre = settled_rows(pre_ref, tail_ref, arrived_ref, place_ref, 4, window)
+    pre = settled_rows(pre_ref, tail_ref, arrived_ref, place_ref, quarter, window)
     query, key, value = pre[:, :q_width], pre[:, q_width : 2 * q_width], pre[:, 2 * q_width :]
     inner = inner_ref[...]
     du = jnp.concatenate(
@@ -973,13 +975,13 @@
         axis=1,
     )
     du_ref[...] = du
-    accumulate(down_sum, tn(du, rows_ref[...]), first)
+    accumulate(down_sum, tn(du, rows_ref[...]), True)
     at = 0
     for p, part in enumerate((query, key, value)):
         accumulate(
             flat_sum.at[:, at : at + part.shape[1]],
             tn(inner[:, p * low_rank : (p + 1) * low_rank], part),
-            first,
+            True,
         )
         at += part.shape[1]
 
@@ -998,6 +1000,7 @@
     down_mix_ref, wq_ref, wk_ref, wv_ref, wg_ref,
     part_ref,
     window, joined,
+    *, quarter,
 ):
     q_width, v_width = wq_ref.shape[1], wv_ref.shape[1]
 
@@ -1008,7 +1011,7 @@
         joined[:, 2 * q_width : 2 * q_width + v_width] = wv_ref[...]
         joined[:, 2 * q_width + v_width :] = wg_ref[...]
 
-    pre = settled_rows(pre_ref, tail_ref, arrived_ref, place_ref, 4, window)
+    pre = settled_rows(pre_ref, tail_ref, arrived_ref, place_ref, quarter, window)
     mix = low(mix_ref[...])
     spare = down_mix_ref.shape[0] - du_ref.shape[1] - du_gate_ref.shape[1] - mix.shape[1]
     small = jnp.concatenate(
@@ -1021,33 +1024,38 @@
 
 
 def assemble_kernel(
-    place_ref, own_ref, near_ref, far_ref, corner_ref, last_ref, feed_ref, branch_ref,
-    down_ref, qk_ref, vg_ref, ff_ref, out_ref, ffd_ref, res_ref,
+    place_ref, *refs, padded,
 ):
+    pieces_last, pieces_feed = refs[:4], refs[4:8]
+    last_ref, feed_ref, branch_ref = refs[8:11]
+    down_ref, qk_ref, vg_ref, ff_ref, out_ref, ffd_ref, res_ref = refs[11:]
     place = place_ref[0]
-    size = own_ref.shape[1] // 8
-    targets = [down_ref.at[p] for p in range(4)] + [res_ref.at[0]]
-    targets += [down_ref.at[4], down_ref.at[5], res_ref.at[1]]
-    for relative, piece in enumerate((own_ref, near_ref, far_ref, corner_ref)):
+    size = pieces_last[0].shape[1] // 5
+    first = [down_ref.at[p] for p in range(4)] + [res_ref.at[0]]
+    second = [down_ref.at[4], down_ref.at[5], res_ref.at[1]]
+    for relative in range(4):
         start = pl.multiple_of((place ^ relative) * size, 128)
-        for k, target in enumerate(targets):
-            target[:, pl.ds(start, size)] = piece[:, k * size : (k + 1) * size].astype(single)
-    last = last_ref[...].astype(single)
-    qk, values = qk_ref.shape[2], vg_ref.shape[2]
-    qk_ref[0], qk_ref[1] = last[:, :qk], last[:, qk : 2 * qk]
-    vg_ref[0] = last[:, 2 * qk :]
-    branch = branch_ref[...].astype(single)
-    out_ref[...] = branch[:, :values]
-    vg_ref[1] = branch[:, values:]
-    hidden = ff_ref.shape[2]
-    padded = feed_ref.shape[1] // 3
-    feed = feed_ref[...].astype(single)
-    ff_ref[0] = feed[:, :hidden]
-    ff_ref[1] = feed[:, padded : padded + hidden]
-    ffd_ref[...] = feed[:, 2 * padded : 2 * padded + hidden]
-
-
-def assemble(where, shared, last, feed, branch, shapes):
+        for targets, piece in ((first, pieces_last[relative]), (second, pieces_feed[relative])):
+            for k, target in enumerate(targets):
+                target[:, pl.ds(start, size)] = piece[:, k * size : (k + 1) * size].astype(single)
+    qk, values, hidden = qk_ref.shape[2], vg_ref.shape[2], ff_ref.shape[2]
+
+    def lanes(ref, start, width):
+        return ref[:, start : start + width].astype(single)
+
+    own = 5 * size
+    qk_ref[0], qk_ref[1] = lanes(last_ref, own, qk), lanes(last_ref, own + qk, qk)
+    vg_ref[0] = lanes(last_ref, own + 2 * qk, values)
+    at = last_ref.shape[1]
+    out_ref[...] = lanes(branch_ref, at, values)
+    vg_ref[1] = lanes(branch_ref, at + values, values)
+    own = 3 * size
+    ff_ref[0] = lanes(feed_ref, own, hidden)
+    ff_ref[1] = lanes(feed_ref, own + padded, hidden)
+    ffd_ref[...] = lanes(feed_ref, own + 2 * padded, hidden)
+
+
+def assemble(where, shared, last, feed, branch, padded, shapes):
     rows = last.shape[0]
     block = min(32, rows)
 
@@ -1058,7 +1066,7 @@
 
     arrays = [*shared, last, feed, branch]
     return pl.pallas_call(
-        assemble_kernel,
+        functools.partial(assemble_kernel, padded=padded),
         out_shape=tuple(jax.ShapeDtypeStruct(shape, single) for shape in shapes),
         grid=(rows // block,),
         in_specs=[pl.BlockSpec(memory_space=pltpu.SMEM)] + [spec(a.shape) for a in arrays],
@@ -1111,6 +1119,9 @@
                     )
                 )
             extra.append(pltpu.VMEM((block, kind[1]), members[0].dtype))
+            if steps == 1:
+                for b in range(4):
+                    in_specs[b - 4] = pl.BlockSpec(members[b].shape, lambda i: (0, 0))
     out_specs, shapes, groups_out = [], [], []
     for shape, dtype, kind in outputs:
         if kind == "parts":
@@ -1151,7 +1162,11 @@
             else:
                 held = spare[used]
                 used += 1
-                for b in range(size):
+                if steps == 1:
+                    for b in range(size):
+                        piece = refs[at + b]
+                        held[b * piece.shape[0] : (b + 1) * piece.shape[0], :] = piece[...]
+                for b in range(size if steps > 1 else 0):
 
                     @pl.when(quarter == b)
                     def _(held=held, source=refs[at + b]):
@@ -1396,14 +1411,14 @@
     )
     out_grad_late, pre = tie(out_grad, pre)
     grad_near, grad_far = flip(out_grad_late, 1), flip(out_grad_late, 2)
-    raw_local, mapped, *saved, sent, sent_state, sent_map = run_forward(
+    raw_local, mapped, *saved, sent, sent_state = run_forward(
         where, pre, pre_halo, columns, conv, scalars, heads, key_width, value_width, quarter
     )
 
     hops = min(members - 1, -(-(DOC_MAX - 1) // count))
     got = [shifted_along(sent, "seq", hop) for hop in range(1, hops)]
     got.append(shifted_along(sent_state, "seq", hops))
-    grad_near, grad_far, sent_map = tie(grad_near, grad_far, sent_map)
+    grad_near, grad_far, sent_state = tie(grad_near, grad_far, sent_state)
     grad_all = [out_grad, grad_near, grad_far, flip(grad_far, 1)]
     hidden_grad, du_down = blocked_call(
         feed_before_kernel,
@@ -1450,13 +1465,9 @@
         count * 5_000_000,
     )
     attention_own, attention_far = near_sum(attention_part)
-    attention_far, sent_map = tie(attention_far, sent_map)
-    maps_after = [shifted_along(sent_map, "seq", -hop) for hop in range(1, hops)]
     residual = input_float + far_sum(attention_own, attention_far)
     normed_mid = low(rms_scale(residual, norm2_gain))
     mid_all = gather_rows(normed_mid)
-    corner_mid, *maps_after = tie(mid_all[3], *maps_after)
-    mid_all = mid_all[:3] + [corner_mid]
 
     mid_part, hidden, ff_grad, u_ff, du_ff = blocked_call(
         feed_kernel,
@@ -1525,7 +1536,6 @@
         count * 12_000_000,
     )
     residual_grad = out_grad.astype(single) + rms_back(residual, norm2_gain, mid_grad)
-    out_own, out_far = near_sum(out_part)
     branch_low = low(residual_grad)
     branch_all = gather_rows(branch_low)
     feed_flat = jnp.concatenate(
@@ -1535,8 +1545,8 @@
     branch_all = branch_all[:3] + [corner_branch]
     feed_parts = exchange(seq_rows(feed_flat))
 
-    raw_grad, gate_grad, du_out, du_outgate, state_grad = blocked_call(
-        functools.partial(branch_kernel, **sizes),
+    raw_grad, gate_grad, du_out, du_outgate, *state_grads = blocked_call(
+        functools.partial(branch_kernel, hops=hops, **sizes),
         "branch",
         count,
         [
@@ -1552,22 +1562,26 @@
             (down_out.T, WHOLE),
             (up_res[0], WHOLE),
             (up_vg[1], WHOLE),
-        ],
+        ]
+        + [(part, WHOLE) for part in got[:-1]],
         [
             ((count, value_lanes), bfloat, "rows"),
             ((count, value_lanes), bfloat, "rows"),
             ((count, low_rank), bfloat, "rows"),
             ((count, low_rank), bfloat, "rows"),
-            ((heads, key_width, value_width), bfloat, "whole"),
-        ],
+        ]
+        + [((heads, key_width, value_width), bfloat, "whole")] * hops,
         [
             pltpu.VMEM((value_lanes, width + low_rank), bfloat),
             pltpu.VMEM((heads, key_width, value_width), single),
         ],
         count * 7_000_000,
     )
-    state_got = [shifted_along(state_grad, "seq", -hop) for hop in range(1, hops + 1)]
-    du_out, feed_parts = tie(du_out, feed_parts)
+    state_got = [
+        shifted_along(part, "seq", -hop) for hop, part in enumerate(state_grads, start=1)
+    ]
+    du_out, feed_parts, out_pair = tie(du_out, feed_parts, out_part[2])
+    out_own, out_far = near_sum((out_part[0], out_part[1], out_pair))
     mixer_down_late, branch_res_grad, branch_flat = blocked_call(
         branch_after_kernel,
         "branch_after",
@@ -1589,6 +1603,7 @@
         ],
         [pltpu.VMEM((low_rank, 2 * value_lanes), single)],
         count * 20_000_000,
+        block=count,
     )
     feed_lanes = feed_parts.shape[-1]
     both = jnp.concatenate([share_sum(feed_parts), seq_rows(branch_flat)], axis=2)
@@ -1598,12 +1613,11 @@
 
     pre_grad, mix_grad, tail_grad, edge_grad = run_backward(
         where, pre, pre_halo, columns, conv, scalars, raw_grad, saved, entering, state_got,
-        maps_after, heads, key_width, value_width, quarter,
+        heads, key_width, value_width, quarter,
     )
     arrived = shifted_along(edge_grad, "seq", -1)
     arrived, both, out_arrived = tie(arrived, both, out_arrived)
     result = residual + (out_own + out_arrived.astype(single))
-    feed_total = all_rows(both[:, :, :feed_lanes])
     branch_parts = both[:, :, feed_lanes:]
     settled = [
         (pre_grad, by_rows(2 * qk + value_lanes)),
@@ -1612,7 +1626,7 @@
         (where, SCALAR),
     ]
     du_mix, last_own, last_far, last_pair, last_owned = blocked_call(
-        settle_grads_kernel,
+        functools.partial(settle_grads_kernel, quarter=quarter),
         "settle_grads",
         count,
         [
@@ -1635,16 +1649,17 @@
             ((low_rank, 2 * qk + value_lanes), bfloat, "whole"),
         ],
         [
-            pltpu.VMEM((STEP, 2 * qk + value_lanes), bfloat),
+            pltpu.VMEM((count, 2 * qk + value_lanes), bfloat),
             pltpu.VMEM((3 * low_rank, width), single),
             pltpu.VMEM((low_rank, 2 * qk + value_lanes), single),
         ],
         count * 4_000_000,
+        block=count,
     )
     last_own, last_far = near_sum((last_own, last_far, last_pair))
     last_far, gate_grad = tie(last_far, gate_grad)
     (normed_part,) = blocked_call(
-        settle_kernel,
+        functools.partial(settle_kernel, quarter=quarter),
         "settle",
         count,
         [
@@ -1668,21 +1683,24 @@
         count * 10_000_000,
     )
     last_flat = jnp.concatenate([low(far_sum(last_own, last_far)), last_owned], axis=1)
+    feed_rows = all_rows(both)
+    feed_pieces = gather_rows(feed_rows[:, : 3 * block_width])
     last_lanes = last_flat.shape[1]
     both = exchange(jnp.concatenate([seq_rows(last_flat), share_sum(branch_parts)], axis=2))
-    last_parts, branch_total = both[:, :, :last_lanes], all_rows(both[:, :, last_lanes:])
+    branch_rows = all_rows(both)
+    last_parts = both[:, :, :last_lanes]
     normed_grad = far_sum(*near_sum(normed_part))
     input_grad = residual_grad + rms_back(input_float, norm1_gain, normed_grad)
-    last_total = all_rows(exchange(share_sum(last_parts)))
-    piece = jnp.concatenate(
-        [last_total[:, : 5 * block_width], feed_total[:, : 3 * block_width]], axis=1
-    )
+    last_parts, *feed_pieces = tie(last_parts, *feed_pieces)
+    last_rows = all_rows(exchange(share_sum(last_parts)))
+    last_pieces = gather_rows(last_rows[:, : 5 * block_width])
     down_grad, qk_grad, vg_grad, ff_grads, out_grads, ffd_grads, res_grad = assemble(
         where,
-        gather_rows(piece),
-        last_total[:, 5 * block_width :],
-        feed_total[:, 3 * block_width :],
-        branch_total,
+        [*last_pieces, *feed_pieces],
+        last_rows,
+        feed_rows,
+        branch_rows,
+        padded,
         [
             (6, low_rank, width),
             (2, low_rank, qk),

time: 379 us -> 361 us (0.953)
  waiting for transfers between devices: 114 us -> 102 us
  local copies, waits for them, and re-layouts: 22 us -> 13.9 us
  starting transfers between devices: 69.9 us -> 75.1 us
    ppermute x12 -> x9, waiting for transfers between devices: 26.4 us -> 13.7 us  [shifted_along(): return lax.ppermute(array, axis, pairs)]
    all_to_all x4, starting transfers between devices: 20.2 us -> 27.6 us  [exchange(): return lax.all_to_all(parts, 'seq', 0, 0)]
    ppermute x27 -> x30, waiting for transfers between devices: 67.6 us -> 74 us  [flip(): return lax.ppermute(array, 'head', [(i, i ^ bit) for i in range(groups)])]
    slice x6 -> x3, local copies, waits for them, and re-layouts: 6.29 us -> 0.77 us  [the longest x1 0.71 us: on_device(): feed_pieces = gather_rows(feed_rows[:, :3 * block_width])]
    all_to_all x4, waiting for transfers between devices: 20.2 us -> 14.7 us  [exchange(): return lax.all_to_all(parts, 'seq', 0, 0)]
    ppermute x12 -> x9, starting transfers between devices: 23.8 us -> 19.9 us  [shifted_along(): return lax.ppermute(array, axis, pairs)]
    ppermute x27 -> x30, starting transfers between devices: 23.2 us -> 24.9 us  [flip(): return lax.ppermute(array, 'head', [(i, i ^ bit) for i in range(groups)])]
  transfers between devices with their start and end apart: 47 -> 47, of which waited for: 19 -> 18; matrix products, arithmetic and copies ran while one was open for 11% -> 9% of each run, Pallas kernels for 23% -> 24%
where the time goes in v3:
time: 361 us; the launch traced here: 359 us
  Pallas kernels  135 us (37%)
  waiting for transfers between devices  102 us (28%)
  starting transfers between devices  75.1 us (21%)
  other arithmetic  30.8 us (9%)
  local copies, waits for them, and re-layouts  13.9 us (4%)
    pallas_call x9, Pallas kernels, blocked_call(): pl.pallas_call(wrapped, out_shape=tuple(shapes), grid=(steps,), in_specs=...  88 us
    ppermute x30, waiting for transfers between devices, flip(): return lax.ppermute(array, 'head', [(i, i ^ bit) for i in range(groups)])  74 us
    all_to_all x4, starting transfers between devices, exchange(): return lax.all_to_all(parts, 'seq', 0, 0)  27.6 us
    ppermute x30, starting transfers between devices, flip(): return lax.ppermute(array, 'head', [(i, i ^ bit) for i in range(groups)])  24.9 us
    pallas_call x1, Pallas kernels, run_backward(): pl.pallas_call(body, out_shape=shapes, grid_spec=pltpu.PrefetchScalarGrid...  21.2 us
    pallas_call x1, Pallas kernels, run_forward(): pl.pallas_call(body, out_shape=shapes, grid_spec=pltpu.PrefetchScalarGrid...  20.6 us
    ppermute x9, starting transfers between devices, shifted_along(): return lax.ppermute(array, axis, pairs)  19.9 us
    all_to_all x4, waiting for transfers between devices, exchange(): return lax.all_to_all(parts, 'seq', 0, 0)  14.7 us
  transfers between devices with their start and end apart: 47, of which 18 were waited for; matrix products, arithmetic and copies ran while one was open for 9% of the time, Pallas kernels for 24%

profile of v3, /device:TPU:0, one launch (start us, length us, event | category | flops | bytes accessed | tf_op | source)
XLA Modules:
  0.0 359.2 jit_solution(12271463172958339592)
XLA Ops:
  25.5 11.8 %project.1 = (bf16[1024,1024]{1,0:T(8,128)(2,1)}, f32[1024,512]{1,0:T(8,128)}, bf16[1024,512]{1,0:T(8,128)(2,1)}, f32[1024,8]{1,0:T(8,128)}, bf16[16,1024]{1,0:T(8,128)(2,1)}) custom-call(bf16[256,1024]{1,0:T(8,128)(2,1)} %copy-done.14, bf16[256,1024]{1,0:T(8,128)(2,1)} %collective-permute-done.refs_1_.refs_7_.refs_2_, ...), custom_call_target="tpu_custom_call" | custom-call | flops 9216000000 | bytes 7016960 | tf_op jit(solution)/shard_map/project/pallas_call | solution.py:1193
  43.0 20.6 %delta_forward.1 = (f32[1024,512]{1,0:T(8,128)}, bf16[1024,256]{1,0:T(8,128)(2,1)}, bf16[1024,768]{1,0:T(8,128)(2,1)}, bf16[8,2,128,384]{3,2,1,0:T(8,128)(2,1)},...) custom-call(s32[1]{0:T(128)} %bitcast.place.refs_15_.refs_9_.refs_7_, ...), custom_call_target="tpu_custom_call" | custom-call | flops 2048000000 | bytes 10240000 | tf_op jit(solution)/shard_map/delta_forward/pallas_call | solution.py:510
  72.3 5.0 %collective-permute-start.12 = (bf16[2,128,384]{2,1,0:T(8,128)(2,1)}, bf16[2,128,384]{2,1,0:T(8,128)(2,1)S(1)}, u32[]{:S(2)}, u32[]{:S(2)}) collective-permute-start(bf16[2,128,384]{2,1,0:T(8,128)(2,1)} %get-tuple-element.117), channel_id=1, source_target_pairs={{0,12},{4,16},{8,20},{12,24},{16,28},{1,13},{5,17},{9,21},{13,25},... | collective-permute-start | bytes 589832 | tf_op jit(solution)/shard_map/ppermute | solution.py:1245
  78.9 6.9 %feed_before.1 = (f32[1024,768]{1,0:T(8,128)}, bf16[1024,128]{1,0:T(8,128)(2,1)}) custom-call(bf16[256,1024]{1,0:T(8,128)(2,1)} %refs_4_.1, bf16[256,1024]{1,0:T(8,128)(2,1)} %copy-done.43, bf16[256,1024]{1,0:T(8,128)(2,1)} %collective-permute-done.8.refs_2_.refs_6_, bf16[256,1024]{1,0:T(8,128)(2,1)} %collective-permute-done.9.refs_3_.refs_7_, ...), custom_call_target="tpu_custom_call" | custom-call | flops 6144000000 | bytes 4018176 | tf_op jit(solution)/shard_map/feed_before/pallas_call | solution.py:1193
  86.7 8.6 %attend.1 = (bf16[256,1024]{1,0:T(8,128)(2,1)}, bf16[256,1024]{1,0:T(8,128)(2,1)}, bf16[512,1024]{1,0:T(8,128)(2,1)}, bf16[1024,512]{1,0:T(8,128)(2,1)}, bf16[10...) custom-call(f32[1024,512]{1,0:T(8,128)} %get-tuple-element.114.refs_0_.refs_4_, ...), custom_call_target="tpu_custom_call" | custom-call | flops 5120000000 | bytes 6926336 | tf_op jit(solution)/shard_map/attend/pallas_call | solution.py:1193
  99.6 13.9 %collective-permute-done.15 = bf16[256,1024]{1,0:T(8,128)(2,1)S(1)} collective-permute-done((bf16[256,1024]{1,0:T(8,128)(2,1)S(1)}, bf16[256,1024]{1,0:T(8,128)(2,1)S(1)}, u32[]{:S(2)}, u32[]{:S(2)}) %collective-permute-start.15) | collective-permute-done | bytes 524320 | tf_op jit(solution)/shard_map/ppermute | solution.py:1215
  115.2 13.2 %collective-permute-done.17.refs_2_ = bf16[256,1024]{1,0:T(8,128)(2,1)} collective-permute-done((bf16[256,1024]{1,0:T(8,128)(2,1)}, bf16[256,1024]{1,0:T(8,128)(2,1)}, u32[]{:S(2)}, u32[]{:S(2)}) %collective-permute-start.17) | collective-permute-done | bytes 524320 | tf_op jit(solution)/shard_map/ppermute | solution.py:1215
  130.9 17.4 %feed.1 = (bf16[256,1024]{1,0:T(8,128)(2,1)}, bf16[256,1024]{1,0:T(8,128)(2,1)}, bf16[512,1024]{1,0:T(8,128)(2,1)}, bf16[1024,768]{1,0:T(8,128)(2,1)}, bf16[1024...) custom-call(bf16[256,1024]{1,0:T(8,128)(2,1)} %multiply_convert_fusion.refs_0_, ...), custom_call_target="tpu_custom_call" | custom-call | flops 15360000000 | bytes 9441280 | tf_op jit(solution)/shard_map/feed/pallas_call | solution.py:1193
  153.1 11.2 %feed_after.1 = (bf16[256,1024]{1,0:T(8,128)(2,1)}, bf16[256,1024]{1,0:T(8,128)(2,1)}, bf16[512,1024]{1,0:T(8,128)(2,1)}, bf16[128,768]{1,0:T(8,128)(2,1)}, bf16...) custom-call(bf16[256,1024]{1,0:T(8,128)(2,1)} %multiply_convert_fusion.refs_0_, ...), custom_call_target="tpu_custom_call" | custom-call | flops 12288000000 | bytes 12161028 | tf_op jit(solution)/shard_map/feed_after/pallas_call | solution.py:1193
  170.8 12.7 %collective-permute-done.22.refs_2_ = bf16[256,1024]{1,0:T(8,128)(2,1)S(1)} collective-permute-done((bf16[256,1024]{1,0:T(8,128)(2,1)S(1)}, bf16[256,1024]{1,0:T(8,128)(2,1)S(1)}, u32[]{:S(2)}, u32[]{:S(2)}) %collective-permute-start.22) | collective-permute-done | bytes 524320 | tf_op jit(solution)/shard_map/ppermute | solution.py:1215
  188.1 13.5 %all-to-all-start = ((bf16[8,16,3072]{2,1,0:T(8,128)(2,1)}), bf16[8,16,3072]{2,1,0:T(8,128)(2,1)S(1)}, u32[]{:S(2)}, u32[]{:S(2)}) async-start(bf16[8,16,3072]{2,1,0:T(8,128)(2,1)} %bitcast.28), calls=%async_computation | async-start | bytes 1572864 | tf_op jit(solution)/shard_map/all_to_all | solution.py:1259
  203.7 9.9 %branch.1 = (bf16[1024,512]{1,0:T(8,128)(2,1)}, bf16[1024,512]{1,0:T(8,128)(2,1)}, bf16[1024,128]{1,0:T(8,128)(2,1)}, bf16[1024,128]{1,0:T(8,128)(2,1)}, bf16[2,...) custom-call(bf16[256,1024]{1,0:T(8,128)(2,1)} %copy-done.19, ...), custom_call_target="tpu_custom_call" | custom-call | flops 7168000000 | bytes 9154560 | tf_op jit(solution)/shard_map/branch/pallas_call | solution.py:1193
  220.8 4.8 %branch_after.1 = (f32[128,1024]{1,0:T(8,128)}, f32[128,1024]{1,0:T(8,128)}, bf16[128,1024]{1,0:T(8,128)(2,1)}) custom-call(bf16[256,1024]{1,0:T(8,128)(2,1)} %copy-done.19, bf16[256,1024]{1,0:T(8,128)(2,1)} %collective-permute-done.21.refs_1_, bf16[256,1024]{1,0:T(8,128)(2,1)} %copy-done.44, bf16[256,1024]{1,0:T(8,128)(2,1)} %copy-done.45, ...), custom_call_target="tpu_custom_call" | custom-call | flops 20480000000 | bytes 8126464 | tf_op jit(solution)/shard_map/branch_after/pallas_call | solution.py:1193
  229.1 8.6 %collective-permute-done.30.rest_3_ = bf16[2,128,256]{2,1,0:T(8,128)(2,1)} collective-permute-done((bf16[2,128,256]{2,1,0:T(8,128)(2,1)}, bf16[2,128,256]{2,1,0:T(8,128)(2,1)}, u32[]{:S(2)}, u32[]{:S(2)}) %collective-permute-start.30) | collective-permute-done | bytes 131104 | tf_op jit(solution)/shard_map/ppermute | solution.py:1245
  241.9 21.2 %delta_backward.1 = (bf16[1024,1024]{1,0:T(8,128)(2,1)}, f32[1024,8]{1,0:T(8,128)}, f32[16,1024]{1,0:T(8,128)}, f32[16,1024]{1,0:T(8,128)}) custom-call(s32[1]{0:T(128)} %bitcast.place.refs_15_.refs_9_.refs_7_.place_ref, bf16[1024,1024]{1,0:T(8,128)(2,1)} %get-tuple-element.105.rows_ref.before_ref, ...), custom_call_target="tpu_custom_call" | custom-call | flops 3072000000 | bytes 12288000 | tf_op jit(solution)/shard_map/delta_backward/pallas_call | solution.py:582
  264.3 5.1 %collective-permute-done.31.refs_8_.refs_6_ = f32[16,1024]{1,0:T(8,128)S(1)} collective-permute-done((f32[16,1024]{1,0:T(8,128)}, f32[16,1024]{1,0:T(8,128)S(1)}, u32[]{:S(2)}, u32[]{:S(2)}) %collective-permute-start.31) | collective-permute-done | bytes 65568 | tf_op jit(solution)/shard_map/ppermute | solution.py:1245
  270.0 7.1 %settle_grads.1 = (bf16[1024,384]{1,0:T(8,128)(2,1)}, bf16[128,1280]{1,0:T(8,128)(2,1)}, bf16[128,1280]{1,0:T(8,128)(2,1)}, bf16[256,1280]{1,0:T(8,128)(2,1)}, bf16[128,1024]{1,0:T(8,128)(2,1)}) custom-call(bf16[1024,1024]{1,0:T(8,128)(2,1)} %get-tuple-element.170.refs_0_, bf16[256,1024]{1,0:T(8,128)(2,1)} %copy-done.14, ...), custom_call_target="tpu_custom_call" | custom-call | flops 4096000000 | bytes 6721540 | tf_op jit(solution)/shard_map/settle_grads/pallas_call | solution.py:1193
  282.2 8.3 %collective-permute-done.36 = bf16[128,1280]{1,0:T(8,128)(2,1)S(1)} collective-permute-done((bf16[128,1280]{1,0:T(8,128)(2,1)S(1)}, bf16[128,1280]{1,0:T(8,128)(2,1)S(1)}, u32[]{:S(2)}, u32[]{:S(2)}) %collective-permute-start.36) | collective-permute-done | bytes 327712 | tf_op jit(solution)/shard_map/ppermute | solution.py:1215
  292.6 5.9 %all-to-all-start.2 = ((bf16[8,16,3328]{2,1,0:T(8,128)(2,1)}), bf16[8,16,3328]{2,1,0:T(8,128)(2,1)S(1)}, u32[]{:S(2)}, u32[]{:S(2)}) async-start(bf16[8,16,3328]{2,1,0:T(8,128)(2,1)} %pad_maximum_fusion.1), calls=%async_computation.2 | async-start | bytes 1703936 | tf_op jit(solution)/shard_map/all_to_all | solution.py:1259
  298.4 10.3 %settle.1 = (bf16[256,1024]{1,0:T(8,128)(2,1)}, bf16[256,1024]{1,0:T(8,128)(2,1)}, bf16[512,1024]{1,0:T(8,128)(2,1)}) custom-call(bf16[1024,1024]{1,0:T(8,128)(2,1)} %get-tuple-element.170.refs_0_, bf16[1024,512]{1,0:T(8,128)(2,1)} %get-tuple-element.177.refs_13_.refs_1_, bf16[1024,384]{1,0:T(8,128)(2,1)} %get-tuple-element.178.refs_2_, ...), custom_call_target="tpu_custom_call" | custom-call | flops 10240000000 | bytes 8814596 | tf_op jit(solution)/shard_map/settle/pallas_call | solution.py:1193
  311.1 5.8 %collective-permute-done.38.refs_6_ = bf16[128,768]{1,0:T(8,128)(2,1)S(1)} collective-permute-done((bf16[128,768]{1,0:T(8,128)(2,1)}, bf16[128,768]{1,0:T(8,128)(2,1)S(1)}, u32[]{:S(2)}, u32[]{:S(2)}) %collective-permute-start.38) | collective-permute-done | bytes 196640 | tf_op jit(solution)/shard_map/ppermute | solution.py:1215
  331.6 10.1 %all-to-all-done.3 = bf16[8,16,2304]{2,1,0:T(8,128)(2,1)S(1)} async-done(((bf16[8,16,2304]{2,1,0:T(8,128)(2,1)}), bf16[8,16,2304]{2,1,0:T(8,128)(2,1)S(1)}, u32[]{:S(2)}, u32[]{:S(2)}) %all-to-all-start.3) | async-done | bytes 589856 | tf_op jit(solution)/shard_map/all_to_all | solution.py:1259
  344.8 5.3 %collective-permute-done.41.refs_2_ = bf16[128,1280]{1,0:T(8,128)(2,1)S(1)} collective-permute-done((bf16[128,1280]{1,0:T(8,128)(2,1)S(1)}, bf16[128,1280]{1,0:T(8,128)(2,1)S(1)}, u32[]{:S(2)}, u32[]{:S(2)}) %collective-permute-start.41) | collective-permute-done | bytes 327712 | tf_op jit(solution)/shard_map/ppermute | solution.py:1215
  353.5 5.4 %assemble.1 = (f32[6,128,1024]{2,1,0:T(8,128)}, f32[2,128,256]{2,1,0:T(8,128)}, f32[2,128,512]{2,1,0:T(8,128)}, f32[2,128,704]{2,1,0:T(8,128)}, f32[128,512]{1,0...) custom-call(s32[1]{0:T(128)} %bitcast.place.refs_15_.refs_9_.refs_7_.place_ref, bf16[128,1280]{1,0:T(8,128)(2,1)} %copy-done.9, ...), custom_call_target="tpu_custom_call" | custom-call | tf_op jit(solution)/shard_map/assemble/pallas_call | solution.py:1068
  (254 shorter events, 114.9 us)
Async XLA Ops:
  3.3 18.5 %collective-permute-start.3 = (bf16[16,1024]{1,0:T(8,128)(2,1)S(1)}, bf16[16,1024]{1,0:T(8,128)(2,1)S(1)}, u32[]{:S(2)}, u32[]{:S(2)}) collective-permute-start(bf16[16,1024]{1,0:T(8,128)(2,1)S(1)} %slice.106), channel_id=1, source_target_pairs={{3,4},{7,8},{11,12},{15,16},{19,20},{23,24},{27,28}} | collective-permute-start | bytes 98312 | tf_op jit(solution)/shard_map/ppermute | solution.py:1376
  3.9 20.2 %collective-permute-start.4 = (bf16[16,1024]{1,0:T(8,128)(2,1)S(1)}, bf16[16,1024]{1,0:T(8,128)(2,1)S(1)}, u32[]{:S(2)}, u32[]{:S(2)}) collective-permute-start(bf16[16,1024]{1,0:T(8,128)(2,1)S(1)} %slice.106), channel_id=1, source_target_pairs={{3,5},{7,9},{11,13},{15,17},{19,21},{23,25},{27,29}} | collective-permute-start | bytes 98312 | tf_op jit(solution)/shard_map/ppermute | solution.py:1376
  4.6 19.6 %collective-permute-start.5 = (bf16[16,1024]{1,0:T(8,128)(2,1)S(1)}, bf16[16,1024]{1,0:T(8,128)(2,1)S(1)}, u32[]{:S(2)}, u32[]{:S(2)}) collective-permute-start(bf16[16,1024]{1,0:T(8,128)(2,1)S(1)} %slice.106), channel_id=1, source_target_pairs={{3,6},{7,10},{11,14},{15,18},{19,22},{23,26},{27,30}} | collective-permute-start | bytes 98312 | tf_op jit(solution)/shard_map/ppermute | solution.py:1376
  8.3 16.5 %collective-permute-start = (bf16[256,1024]{1,0:T(8,128)(2,1)S(1)}, bf16[256,1024]{1,0:T(8,128)(2,1)}, u32[]{:S(2)}, u32[]{:S(2)}) collective-permute-start(bf16[256,1024]{1,0:T(8,128)(2,1)S(1)} %fusion.4.refs_0_.refs_6_.refs_1_), channel_id=1, source_target_pairs={{0,1},{1,0},{2,3},{3,2},{4,5},{5,4},{6,7},{7,6},{8,9},{9,8},{10,11... | collective-permute-start | bytes 1572872 | tf_op jit(solution)/shard_map/ppermute | solution.py:1215
  37.3 26.3 %collective-permute-start.7 = (bf16[256,1024]{1,0:T(8,128)(2,1)S(1)}, bf16[256,1024]{1,0:T(8,128)(2,1)S(1)}, u32[]{:S(2)}, u32[]{:S(2)}) collective-permute-start(bf16[256,1024]{1,0:T(8,128)(2,1)S(1)} %copy-done.16), channel_id=1, source_target_pairs={{0,1},{1,0},{2,3},{3,2},{4,5},{5,4},{6,7},{7,6},{8,9},{9,8},{10,11... | collective-permute-start | bytes 1572872 | tf_op jit(solution)/shard_map/ppermute | solution.py:1215
  37.4 26.3 %collective-permute-start.8 = (bf16[256,1024]{1,0:T(8,128)(2,1)S(1)}, bf16[256,1024]{1,0:T(8,128)(2,1)}, u32[]{:S(2)}, u32[]{:S(2)}) collective-permute-start(bf16[256,1024]{1,0:T(8,128)(2,1)S(1)} %copy-done.16), channel_id=1, source_target_pairs={{0,2},{1,3},{2,0},{3,1},{4,6},{5,7},{6,4},{7,5},{8,10},{9,11},{10,... | collective-permute-start | bytes 1572872 | tf_op jit(solution)/shard_map/ppermute | solution.py:1215
  63.6 15.2 %collective-permute-start.9 = (bf16[256,1024]{1,0:T(8,128)(2,1)}, bf16[256,1024]{1,0:T(8,128)(2,1)}, u32[]{:S(2)}, u32[]{:S(2)}) collective-permute-start(bf16[256,1024]{1,0:T(8,128)(2,1)} %collective-permute-done.8.refs_2_.refs_6_), channel_id=1, source_target_pairs={{0,1},{1,0},{2,3},{3,2},{4,5},{5,4},{6,7},{7,6},{8,9},{9,8},{10,11... | collective-permute-start | bytes 1572872 | tf_op jit(solution)/shard_map/ppermute | solution.py:1215
  65.4 20.4 %collective-permute-start.10 = (bf16[2,128,384]{2,1,0:T(8,128)(2,1)}, bf16[2,128,384]{2,1,0:T(8,128)(2,1)S(1)}, u32[]{:S(2)}, u32[]{:S(2)}) collective-permute-start(bf16[2,128,384]{2,1,0:T(8,128)(2,1)} %get-tuple-element.117), channel_id=1, source_target_pairs={{0,4},{4,8},{8,12},{12,16},{16,20},{20,24},{24,28},{1,5},{5,9},{9,... | collective-permute-start | bytes 589832 | tf_op jit(solution)/shard_map/ppermute | solution.py:1245
  68.8 17.0 %collective-permute-start.11 = (bf16[2,128,384]{2,1,0:T(8,128)(2,1)}, bf16[2,128,384]{2,1,0:T(8,128)(2,1)S(1)}, u32[]{:S(2)}, u32[]{:S(2)}) collective-permute-start(bf16[2,128,384]{2,1,0:T(8,128)(2,1)} %get-tuple-element.117), channel_id=1, source_target_pairs={{0,8},{4,12},{8,16},{12,20},{16,24},{20,28},{1,9},{5,13},{9,17},{1... | collective-permute-start | bytes 589832 | tf_op jit(solution)/shard_map/ppermute | solution.py:1245
  99.5 14.0 %collective-permute-start.15 = (bf16[256,1024]{1,0:T(8,128)(2,1)S(1)}, bf16[256,1024]{1,0:T(8,128)(2,1)S(1)}, u32[]{:S(2)}, u32[]{:S(2)}) collective-permute-start(bf16[256,1024]{1,0:T(8,128)(2,1)S(1)} %add_convert_fusion.4), channel_id=1, source_target_pairs={{0,2},{1,3},{2,0},{3,1},{4,6},{5,7},{6,4},{7,5},{8,10},{9,11},{10,... | collective-permute-start | bytes 1572872 | tf_op jit(solution)/shard_map/ppermute | solution.py:1215
  115.2 15.7 %collective-permute-start.16 = (bf16[256,1024]{1,0:T(8,128)(2,1)}, bf16[256,1024]{1,0:T(8,128)(2,1)}, u32[]{:S(2)}, u32[]{:S(2)}) collective-permute-start(bf16[256,1024]{1,0:T(8,128)(2,1)} %multiply_convert_fusion.refs_0_), channel_id=1, source_target_pairs={{0,1},{1,0},{2,3},{3,2},{4,5},{5,4},{6,7},{7,6},{8,9},{9,8},{10,11... | collective-permute-start | bytes 1572872 | tf_op jit(solution)/shard_map/ppermute | solution.py:1215
  152.5 14.3 %collective-permute-start.20 = (bf16[256,1024]{1,0:T(8,128)(2,1)S(1)}, bf16[256,1024]{1,0:T(8,128)(2,1)S(1)}, u32[]{:S(2)}, u32[]{:S(2)}) collective-permute-start(bf16[256,1024]{1,0:T(8,128)(2,1)S(1)} %add_convert_fusion.3), channel_id=1, source_target_pairs={{0,2},{1,3},{2,0},{3,1},{4,6},{5,7},{6,4},{7,5},{8,10},{9,11},{10,... | collective-permute-start | bytes 1572872 | tf_op jit(solution)/shard_map/ppermute | solution.py:1215
  168.6 14.8 %collective-permute-start.22 = (bf16[256,1024]{1,0:T(8,128)(2,1)S(1)}, bf16[256,1024]{1,0:T(8,128)(2,1)S(1)}, u32[]{:S(2)}, u32[]{:S(2)}) collective-permute-start(bf16[256,1024]{1,0:T(8,128)(2,1)S(1)} %get-tuple-element.203.refs_0_), channel_id=1, source_target_pairs={{0,2},{1,3},{2,0},{3,1},{4,6},{5,7},{6,4},{7,5},{8,10},{9,11},{10,... | collective-permute-start | bytes 1572872 | tf_op jit(solution)/shard_map/ppermute | solution.py:1215
  169.2 17.0 %collective-permute-start.25 = (bf16[128,768]{1,0:T(8,128)(2,1)S(1)}, bf16[128,768]{1,0:T(8,128)(2,1)S(1)}, u32[]{:S(2)}, u32[]{:S(2)}) collective-permute-start(bf16[128,768]{1,0:T(8,128)(2,1)S(1)} %add_convert_fusion.8), channel_id=1, source_target_pairs={{0,2},{1,3},{2,0},{3,1},{4,6},{5,7},{6,4},{7,5},{8,10},{9,11},{10,... | collective-permute-start | bytes 589832 | tf_op jit(solution)/shard_map/ppermute | solution.py:1215
  188.1 32.6 %all-to-all-start = ((bf16[8,16,3072]{2,1,0:T(8,128)(2,1)}), bf16[8,16,3072]{2,1,0:T(8,128)(2,1)S(1)}, u32[]{:S(2)}, u32[]{:S(2)}) async-start(bf16[8,16,3072]{2,1,0:T(8,128)(2,1)} %bitcast.28), calls=%async_computation | async-start | bytes 1572864 | tf_op jit(solution)/shard_map/all_to_all | solution.py:1259
  213.6 15.5 %collective-permute-start.27 = (bf16[2,128,256]{2,1,0:T(8,128)(2,1)}, bf16[2,128,256]{2,1,0:T(8,128)(2,1)}, u32[]{:S(2)}, u32[]{:S(2)}) collective-permute-start(bf16[2,128,256]{2,1,0:T(8,128)(2,1)} %get-tuple-element.153), channel_id=1, source_target_pairs={{4,0},{8,4},{12,8},{16,12},{20,16},{24,20},{28,24},{5,1},{9,5},{13... | collective-permute-start | bytes 393224 | tf_op jit(solution)/shard_map/ppermute | solution.py:1245
  214.9 14.2 %collective-permute-start.28 = (bf16[2,128,256]{2,1,0:T(8,128)(2,1)}, bf16[2,128,256]{2,1,0:T(8,128)(2,1)}, u32[]{:S(2)}, u32[]{:S(2)}) collective-permute-start(bf16[2,128,256]{2,1,0:T(8,128)(2,1)} %get-tuple-element.154), channel_id=1, source_target_pairs={{8,0},{12,4},{16,8},{20,12},{24,16},{28,20},{9,1},{13,5},{17,9},{2... | collective-permute-start | bytes 393224 | tf_op jit(solution)/shard_map/ppermute | solution.py:1245
  217.5 20.2 %collective-permute-start.30 = (bf16[2,128,256]{2,1,0:T(8,128)(2,1)}, bf16[2,128,256]{2,1,0:T(8,128)(2,1)}, u32[]{:S(2)}, u32[]{:S(2)}) collective-permute-start(bf16[2,128,256]{2,1,0:T(8,128)(2,1)} %get-tuple-element.156), channel_id=1, source_target_pairs={{16,0},{20,4},{24,8},{28,12},{17,1},{21,5},{25,9},{29,13},{18,2},{... | collective-permute-start | bytes 393224 | tf_op jit(solution)/shard_map/ppermute | solution.py:1245
  237.7 31.7 %all-to-all-start.1 = ((bf16[8,16,4096]{2,1,0:T(8,128)(2,1)}), bf16[8,16,4096]{2,1,0:T(8,128)(2,1)S(1)}, u32[]{:S(2)}, u32[]{:S(2)}) async-start(bf16[8,16,4096]{2,1,0:T(8,128)(2,1)} %pad_maximum_fusion), calls=%async_computation.1 | async-start | bytes 2097152 | tf_op jit(solution)/shard_map/all_to_all | solution.py:1259
  241.2 28.2 %collective-permute-start.32 = (bf16[256,1024]{1,0:T(8,128)(2,1)}, bf16[256,1024]{1,0:T(8,128)(2,1)}, u32[]{:S(2)}, u32[]{:S(2)}) collective-permute-start(bf16[256,1024]{1,0:T(8,128)(2,1)} %add_convert_fusion.2), channel_id=1, source_target_pairs={{0,2},{1,3},{2,0},{3,1},{4,6},{5,7},{6,4},{7,5},{8,10},{9,11},{10,... | collective-permute-start | bytes 1572872 | tf_op jit(solution)/shard_map/ppermute | solution.py:1215
  292.6 27.1 %all-to-all-start.2 = ((bf16[8,16,3328]{2,1,0:T(8,128)(2,1)}), bf16[8,16,3328]{2,1,0:T(8,128)(2,1)S(1)}, u32[]{:S(2)}, u32[]{:S(2)}) async-start(bf16[8,16,3328]{2,1,0:T(8,128)(2,1)} %pad_maximum_fusion.1), calls=%async_computation.2 | async-start | bytes 1703936 | tf_op jit(solution)/shard_map/all_to_all | solution.py:1259
  308.7 16.8 %collective-permute-start.34 = (bf16[512,1024]{1,0:T(8,128)(2,1)}, bf16[512,1024]{1,0:T(8,128)(2,1)}, u32[]{:S(2)}, u32[]{:S(2)}) collective-permute-start(bf16[512,1024]{1,0:T(8,128)(2,1)} %get-tuple-element.181), channel_id=1, source_target_pairs={{0,1},{1,0},{2,3},{3,2},{4,5},{5,4},{6,7},{7,6},{8,9},{9,8},{10,11... | collective-permute-start | bytes 3145736 | tf_op jit(solution)/shard_map/ppermute | solution.py:1215
  320.8 20.9 %all-to-all-start.3 = ((bf16[8,16,2304]{2,1,0:T(8,128)(2,1)}), bf16[8,16,2304]{2,1,0:T(8,128)(2,1)S(1)}, u32[]{:S(2)}, u32[]{:S(2)}) async-start(bf16[8,16,2304]{2,1,0:T(8,128)(2,1)} %broadcast_in_dim.130), calls=%async_computation.3 | async-start | bytes 1179648 | tf_op jit(solution)/shard_map/all_to_all | solution.py:1259
  327.8 15.4 %collective-permute-start.35 = (bf16[256,1024]{1,0:T(8,128)(2,1)}, bf16[256,1024]{1,0:T(8,128)(2,1)S(1)}, u32[]{:S(2)}, u32[]{:S(2)}) collective-permute-start(bf16[256,1024]{1,0:T(8,128)(2,1)} %add_convert_fusion), channel_id=1, source_target_pairs={{0,2},{1,3},{2,0},{3,1},{4,6},{5,7},{6,4},{7,5},{8,10},{9,11},{10,... | collective-permute-start | bytes 1572872 | tf_op jit(solution)/shard_map/ppermute | solution.py:1215
  (74 other events, 737.6 us)
